TPU v7x, 32 devices: a whole 2x2x4 slice. The times are simulated.
32 devices in a mesh: grp: 4 (over y, core), fsdp: 8 (over z, x).
Axes of the slice: x: 2, y: 2, z: 4, core: 2. Of those that a mesh axis runs over, the one named last changes fastest.
Arguments:
- traj_hidden: bfloat16 [32768, 4096], P(('grp', 'fsdp')), may hold values from -6 to 6
- traj_tokens: int32 [32768], P(('grp', 'fsdp')), may hold values from 0 to 511
- traj_action: int32 [32768], P(('grp', 'fsdp')), may hold values from 0 to 511
- traj_return: float32 [32768], P(('grp', 'fsdp')), may hold values from -6 to 6
- traj_episode: int32 [32, 1024], P(('grp', 'fsdp')), may hold values from 0 to 7, never falling along the last dimension, each value on 1 to 512 neighbouring positions
- roll_hidden: bfloat16 [2048, 4096], P(('grp', 'fsdp')), may hold values from -6 to 6
- roll_tokens: int32 [2048], P(('grp', 'fsdp')), may hold values from 0 to 511
- roll_action: int32 [2048], P(('grp', 'fsdp')), may hold values from 0 to 511
- station_table: bfloat16 [512, 4096], replicated, may hold values from -3 to 3
- norm_gain: float32 [4096], replicated, may hold values from 0.7 to 3.9
- head_weight: bfloat16 [4096, 512], P('fsdp'), may hold values from -6 to 6
Outputs:
- new_head: bfloat16 [4096, 512], P('fsdp')
- action_logp: float32 [2048], P(('grp', 'fsdp'))
- episode_logp: float32 [32], P(('grp', 'fsdp'))
Inputs may be any that keep to these rules, and one draw needn't show every extreme that they name: `traj_episode`: within each block of 1024 tokens the episode numbers never fall and every number 0 to 7 occurs.
All inputs are finite; a program needn't handle non-finite values.
Results may differ from a plain program's by a relative error of at most 0.0034.
Values may be sent and summed in bfloat16 or wider, within the bound.
No kernel may reach another device: no remote copies, remote signals or barrier semaphores. Data moves between devices by JAX's collectives and lax.ppermute only.
A program may use at most 64 MiB of HBM per device.

v0:
```python
import jax
import jax.numpy as jnp
from jax import lax
from jax.sharding import PartitionSpec as P

ACTIONS = 512
STATIONS = 512
EPI_BLK = 8
STEPS = 64


step_length = 8.0


def station_rows(hidden, tokens, table, gain):
    lookup = (tokens[:, None] == jnp.arange(STATIONS, dtype=jnp.int32)[None, :]).astype(
        jnp.bfloat16
    )
    embedded = jnp.dot(lookup, table, preferred_element_type=jnp.float32)
    mixed = hidden.astype(jnp.float32) + embedded
    power = jnp.mean(mixed * mixed, axis=-1, keepdims=True)
    return (mixed * lax.rsqrt(power + 1e-05) * gain).astype(jnp.bfloat16)


def picked_logp(logits, actions):
    top = jnp.max(logits, axis=-1, keepdims=True)
    total = jnp.log(jnp.sum(jnp.exp(logits - top), axis=-1)) + top[:, 0]
    chosen = (actions[:, None] == jnp.arange(ACTIONS, dtype=jnp.int32)[None, :]).astype(jnp.float32)
    return jnp.sum(logits * chosen, axis=-1) - total


def episode_advantage(returns, episode):
    member = (episode[:, None] == jnp.arange(EPI_BLK, dtype=jnp.int32)[None, :]).astype(jnp.float32)
    sums = jnp.dot(member.T, returns, precision=lax.Precision.HIGHEST)
    counts = jnp.sum(member, axis=0)
    baseline = jnp.dot(member, sums / counts, precision=lax.Precision.HIGHEST)
    return returns - baseline


def outer_rows(left, right):
    return lax.dot_general(
        left, right, (((0,), (0,)), ((), ())), preferred_element_type=jnp.float32
    )


def local(
    traj_hidden,
    traj_tokens,
    traj_action,
    traj_return,
    traj_episode,
    roll_hidden,
    roll_tokens,
    roll_action,
    station_table,
    norm_gain,
    head_weight,
):
    shard_rows = head_weight.shape[0]
    features = station_rows(traj_hidden, traj_tokens, station_table, norm_gain)
    rollout = station_rows(roll_hidden, roll_tokens, station_table, norm_gain)
    advantage = episode_advantage(traj_return, traj_episode[0])
    full_old = lax.all_gather(head_weight, "fsdp", axis=0, tiled=True)
    logits = jnp.dot(features, full_old, preferred_element_type=jnp.float32)
    top = jnp.max(logits, axis=-1, keepdims=True)
    expo = jnp.exp(logits - top)
    probs = expo / jnp.sum(expo, axis=-1, keepdims=True)
    chosen = (traj_action[:, None] == jnp.arange(ACTIONS, dtype=jnp.int32)[None, :]).astype(
        jnp.float32
    )
    scores = (advantage[:, None] * (probs - chosen)).astype(jnp.bfloat16)
    gathered, all_scores = (features, scores)
    local_grad = outer_rows(gathered, all_scores)
    grad = lax.psum(local_grad, ("grp", "fsdp"))
    gnorm = jnp.sqrt(jnp.sum(grad * grad) + 1e-06)
    new_full = (full_old.astype(jnp.float32) - step_length * grad / gnorm).astype(jnp.bfloat16)
    position = lax.axis_index("fsdp")
    new_head = lax.dynamic_slice_in_dim(new_full, position * shard_rows, shard_rows, 0)
    roll_logits = jnp.dot(rollout, new_full, preferred_element_type=jnp.float32)
    action_logp = picked_logp(roll_logits, roll_action)
    episode_logp = jnp.sum(action_logp.reshape(-1, STEPS), axis=1)
    return (new_head, action_logp, episode_logp)


def solution(mesh):
    placed = (
        P(("grp", "fsdp"), None),
        P(("grp", "fsdp")),
        P(("grp", "fsdp")),
        P(("grp", "fsdp")),
        P(("grp", "fsdp"), None),
        P(("grp", "fsdp"), None),
        P(("grp", "fsdp")),
        P(("grp", "fsdp")),
        P(),
        P(),
        P("fsdp", None),
    )
    return jax.shard_map(
        local,
        mesh=mesh,
        in_specs=placed,
        out_specs=(P("fsdp", None), P(("grp", "fsdp")), P(("grp", "fsdp"))),
        check_vma=False,
    )
```

profile of v0, /device:TPU:0, one launch (start us, length us, event | category | flops | bytes accessed | tf_op | source)
XLA Modules:
  0.0 302.0 jit_solution(3129072394212469227)
XLA Ops:
  7.2 0.0 all-gather.2.cloned.1.call-start
  7.2 0.7 all-gather.2.cloned.1.call-update
  7.9 0.0 all-reduce.2.cloned.1.call-start
  7.9 0.8 convert_reduce_fusion
  8.8 0.8 fusion.3
  9.6 0.9 fusion.14
  10.4 0.7 sub.30
  11.1 0.0 copy-start.2
  11.1 8.8 %multiply_reduce_fusion = (f32[1024]{0:T(1024)S(1)}, f32[1024,4096]{1,0:T(8,128)S(1)}) fusion(bf16[1024,4096]{1,0:T(8,128)(2,1)} %param.11, bf16[512,4096]{1,0:T(8,128)(2,1)} %param.19, s32[1024]{0:T(1024)} %param.12), kind=kOutput, calls=%fused_computation.1 | convolution fusion | flops 4312267776 | bytes 29368320 | tf_op jit(solution)/shard_map/dot_general | solution.py:19
  19.9 0.0 copy-done.2
  20.0 9.0 %multiply_convert_fusion = bf16[1024,4096]{1,0:T(8,128)(2,1)} fusion(f32[1024,4096]{1,0:T(8,128)S(1)} %get-tuple-element.8, bf16[1024,4096]{1,0:T(8,128)(2,1)} %param.11, f32[4096]{0:T(1024)S(1)} %copy-done.2, f32[1024]{0:T(1024)S(1)} %add_rsqrt_fusion), kind=kLoop, calls=%fused_computation | loop fusion | flops 20971520 | bytes 33574912 | tf_op jit(solution)/shard_map/convert_element_type | solution.py:22
  29.0 0.0 copy-start.5
  29.0 56.7 %all-gather.2.cloned.1.call-done = bf16[4096,512]{1,0:T(8,128)(2,1)} async-done(((bf16[512,512]{1,0:T(8,128)(2,1)}), bf16[4096,512]{1,0:T(8,128)(2,1)}) %all-gather.2.cloned.1.call-update) | async-done | bytes 4194320 | tf_op jit(solution)/shard_map/all_gather | solution.py:63
  85.6 0.0 copy-start
  85.7 8.4 %fusion.18 = (f32[1024]{0:T(1024)S(1)}, f32[1024,512]{0,1:T(8,128)S(1)}) fusion(bf16[1024,4096]{1,0:T(8,128)(2,1)} %multiply_convert_fusion, bf16[4096,512]{1,0:T(8,128)(2,1)} %all-gather.2.cloned.1.call-done), kind=kOutput, calls=%fused_computation.42 | convolution fusion | flops 4295490560 | bytes 14684160 | tf_op jit(solution)/shard_map/dot_general | solution.py:64
  94.1 0.3 fusion.1
  94.4 0.0 copy-done.5
  94.4 0.0 copy-done
  94.4 7.6 %fusion.4 = f32[4096,512]{1,0:T(8,128)} fusion(bf16[1024,4096]{1,0:T(8,128)(2,1)S(1)} %copy-done, f32[1024,512]{0,1:T(8,128)S(1)} %get-tuple-element.10, s32[1024]{0:T(1024)S(1)} %copy-done.5, f32[1024]{0:T(1024)S(1)} %fusion.1, f32[1024]{0:T(1024)S(1)} %get-tuple-element.9, f32[1024]{0:T(1024)S(1)} %sub.30), kind=kOutput, calls=%fused_computation.15 | convolution fusion | flops 4298637312 | bytes 18890752 | tf_op jit(solution)/shard_map/dot_general | solution.py:41
  102.0 0.0 all-reduce.2.cloned.1.call-update
  102.0 1.0 copy-done.1
  103.1 0.0 copy-done.3
  103.1 3.2 %multiply_reduce_fusion.2 = (f32[64]{0:T(128)S(1)}, f32[64,4096]{1,0:T(8,128)S(1)}) fusion(bf16[512,4096]{1,0:T(8,128)(2,1)} %param.19, s32[64]{0:T(128)S(1)} %copy-done.3, bf16[64,4096]{1,0:T(8,128)(2,1)S(1)} %copy-done.1), kind=kOutput, calls=%fused_computation.17 | convolution fusion | flops 269516736 | bytes 5767680 | tf_op jit(solution)/shard_map/dot_general | solution.py:19
  106.3 173.5 %all-reduce.2.cloned.1.call-done = f32[4096,512]{1,0:T(8,128)} async-done(((f32[4096,512]{1,0:T(8,128)}), f32[4096,512]{1,0:T(8,128)}) %all-reduce.2.cloned.1.call-update) | async-done | bytes 8388624 | tf_op jit(solution)/shard_map/psum | solution.py:74
  279.7 6.1 %multiply_reduce_fusion.1 = f32[]{:T(128)} fusion(f32[4096,512]{1,0:T(8,128)} %all-reduce.2.cloned.1.call-done), kind=kLoop, calls=%fused_computation.4 | loop fusion | flops 4194303 | bytes 8388612 | tf_op jit(solution)/shard_map/reduce_sum | solution.py:75
  286.6 5.4 %subtract_convert_fusion = bf16[4096,512]{1,0:T(8,128)(2,1)S(1)} fusion(f32[4096,512]{1,0:T(8,128)} %all-reduce.2.cloned.1.call-done, bf16[4096,512]{1,0:T(8,128)(2,1)} %all-gather.2.cloned.1.call-done, f32[]{:T(128)S(6)} %sqrt.3), kind=kLoop, calls=%fused_computation.3 | loop fusion | flops 10485760 | bytes 16777220 | tf_op jit(solution)/shard_map/convert_element_type | solution.py:76
  292.0 0.0 copy-start.4
  292.0 0.8 constant_dynamic-slice_fusion
  292.9 1.0 fusion.19
  293.9 0.0 copy-done.4
  293.9 0.2 exponential_reduce_fusion
  294.1 1.1 fusion.17
  (4 shorter events, 0.0 us)
Async XLA Ops:
  7.2 78.5 %all-gather.2.cloned.1.call-start = ((), (), s32[]{:S(2)}) async-start(), calls=%async_computation | async-start | bytes 4718592 | tf_op jit(solution)/shard_map/all_gather | solution.py:63
  7.9 271.8 %all-reduce.2.cloned.1.call-start = ((), (), s32[]{:S(2)}) async-start(), calls=%async_computation.1 | async-start | bytes 16777216 | tf_op jit(solution)/shard_map/psum | solution.py:74
  11.1 8.8 %copy-start.2 = (f32[4096]{0:T(1024)S(1)}, f32[4096]{0:T(1024)}, u32[]{:S(2)}) copy-start(f32[4096]{0:T(1024)} %param.20) | copy-start | bytes 49156
  29.0 65.4 %copy-start.5 = (s32[1024]{0:T(1024)S(1)}, s32[1024]{0:T(1024)}, u32[]{:S(2)}) copy-start(s32[1024]{0:T(1024)} %param.13) | copy-start | bytes 12292
  85.6 8.8 %copy-start = (bf16[1024,4096]{1,0:T(8,128)(2,1)S(1)}, bf16[1024,4096]{1,0:T(8,128)(2,1)}, u32[]{:S(2)}) copy-start(bf16[1024,4096]{1,0:T(8,128)(2,1)} %multiply_convert_fusion) | copy-start | bytes 25165828
  102.0 1.0 copy-start.1
  102.0 1.0 copy-start.3
  292.0 1.8 copy-start.4
Sparse Core Ops, SparseCore 0:
  10.1 75.5 all-gather.1
  102.2 177.5 all-reduce.1
where the time goes:
time: 302 us
  waiting for transfers between devices  231 us (76%)
  matrix products  30.7 us (10%)
  other arithmetic  23.8 us (8%)
  between operations  14.8 us (5%)
    psum x1, waiting for transfers between devices, local(): grad = lax.psum(local_grad, ('grp', 'fsdp'))  173 us
    all_gather x1, waiting for transfers between devices, local(): full_old = lax.all_gather(head_weight, 'fsdp', axis=0, tiled=True)  56.7 us
    dot_general x2, matrix products, station_rows(): embedded = jnp.dot(lookup, table, preferred_element_type=jnp.float32)  12 us
    convert_element_type x1, other arithmetic, station_rows(): return (mixed * lax.rsqrt(power + 1e-05) * gain).astype(jnp.bfloat16)  9.02 us
    dot_general x1, matrix products, local(): logits = jnp.dot(features, full_old, preferred_element_type=jnp.float32)  8.4 us
    dot_general x1, matrix products, outer_rows(): lax.dot_general(left, right, (((0,), (0,)), ((), ())), preferred_element_...  7.6 us
    reduce_sum x1, other arithmetic, local(): gnorm = jnp.sqrt(jnp.sum(grad * grad) + 1e-06)  6.14 us
  transfers between devices with their start and end apart: 2, of which 2 were waited for; matrix products, arithmetic and copies ran while one was open for 8% of the time, Pallas kernels for 0%

commit v1 on v0

v1 whole, which is shorter than its diff:
```python
import functools

import jax
import jax.numpy as jnp
from jax import lax
from jax.experimental import pallas as pl
from jax.experimental.pallas import tpu as pltpu
from jax.sharding import PartitionSpec as P


EPI_BLK = 8
STEPS = 64
AXES = ("grp", "fsdp")
F32, BF16, I32 = jnp.float32, jnp.bfloat16, jnp.int32

step_length = 8.0


def column(row):
    blocks = [jnp.broadcast_to(row[:, at : at + 128], (128, 128)) for at in range(0, row.shape[1], 128)]
    return jnp.concatenate([jnp.transpose(b) for b in blocks], axis=0)


def features_kernel(
    chunks, tab_ref, hidden_ref, roll_ref, token_ref, table_ref, gain_ref, return_ref, episode_ref, action_ref,
    feats_ref, turned_ref, roll_out_ref, roll_rel_ref, advantage_ref, chosen_ref,
    lookup_ref, mixed_ref, power_ref,
):
    step = pl.program_id(0)
    rows, wide = hidden_ref.shape
    few = roll_ref.shape[0]
    half = wide // 2

    @pl.when(step == 0)
    def _():
        down = column(token_ref[...])[: rows + few]
        lane = lax.broadcasted_iota(I32, down.shape, 1)
        for at in range(0, table_ref.shape[0], 128):
            lookup_ref[:, at : at + 128] = jnp.where(down == lane + at, 1.0, 0.0).astype(BF16)
        power_ref[...] = jnp.zeros_like(power_ref)
        returns, episode = return_ref[...], episode_ref[...]
        baseline = jnp.zeros_like(returns)
        for e in range(EPI_BLK):
            member = episode == e
            total = jnp.sum(jnp.where(member, returns, 0.0), axis=-1, keepdims=True)
            count = jnp.sum(jnp.where(member, 1.0, 0.0), axis=-1, keepdims=True)
            baseline = jnp.where(member, total / jnp.maximum(count, 1.0), baseline)
        advantage_ref[...] = column(returns - baseline)
        chosen_ref[...] = column(action_ref[...])

    @pl.when(step < chunks)
    def _():
        embedded = jnp.dot(lookup_ref[...], table_ref[...], preferred_element_type=F32)
        for lo, n, ref in ((0, rows, hidden_ref), (rows, few, roll_ref)):
            mixed = ref[...].astype(F32) + embedded[lo : lo + n]
            mixed_ref[step, lo : lo + n] = mixed
            square = mixed * mixed
            power = square[:, :128]
            for at in range(128, wide, 128):
                power = power + square[:, at : at + 128]
            power_ref[lo : lo + n] += power

    @pl.when(step == chunks - 1)
    def _():
        mean = jnp.sum(power_ref[...], axis=-1, keepdims=True) / (chunks * wide)
        power_ref[...] = jnp.broadcast_to(lax.rsqrt(mean + 1e-05), power_ref.shape)

    @pl.when(step >= chunks)
    def _():
        scale = jnp.concatenate([power_ref[...]] * (wide // 128), axis=1)
        value = (mixed_ref[step - chunks] * scale * gain_ref[...]).astype(BF16)
        feats_ref[0], feats_ref[1] = value[:rows, :half], value[:rows, half:]
        roll_out_ref[0], roll_out_ref[1] = value[rows:, :half], value[rows:, half:]
        roll_rel_ref[0] = value[rows:]
        turned_ref[...] = jnp.transpose(value[:rows]).reshape(turned_ref.shape)


def features_call(shard, tab, hidden, roll, tokens, table, gain, returns, episode, action):
    rows, width = hidden.shape
    half, few, chunks = shard // 2, roll.shape[0], width // shard
    quarter = half // 2
    full = lambda shape: pl.BlockSpec(shape, lambda i, t: (0,) * len(shape))
    before = lambda i: jnp.minimum(i, chunks - 1)
    after = lambda i: jnp.maximum(i - chunks, 0)
    return pl.pallas_call(
        functools.partial(features_kernel, chunks),
        grid_spec=pltpu.PrefetchScalarGridSpec(
            num_scalar_prefetch=1,
            grid=(2 * chunks,),
            in_specs=[
                pl.BlockSpec((rows, shard), lambda i, t: (0, before(i))),
                pl.BlockSpec((few, shard), lambda i, t: (0, before(i))),
                full(tokens.shape),
                pl.BlockSpec((table.shape[0], shard), lambda i, t: (0, before(i))),
                pl.BlockSpec((1, shard), lambda i, t: (0, after(i))),
                full((1, rows)),
                full((1, rows)),
                full((1, rows)),
            ],
            out_specs=[
                pl.BlockSpec((2, rows, half), lambda i, t: (after(i), 0, 0)),
                pl.BlockSpec((4, quarter, rows), lambda i, t: (after(i), 0, 0)),
                pl.BlockSpec((2, few, half), lambda i, t: (after(i), 0, 0)),
                pl.BlockSpec((1, few, shard), lambda i, t: (t[0] ^ after(i), 0, 0)),
                full((rows, 128)),
                full((rows, 128)),
            ],
            scratch_shapes=[
                pltpu.VMEM((rows + few, table.shape[0]), BF16),
                pltpu.VMEM((chunks, rows + few, shard), F32),
                pltpu.VMEM((rows + few, 128), F32),
            ],
        ),
        out_shape=[
            jax.ShapeDtypeStruct((2 * chunks, rows, half), BF16),
            jax.ShapeDtypeStruct((4 * chunks, quarter, rows), BF16),
            jax.ShapeDtypeStruct((2 * chunks, few, half), BF16),
            jax.ShapeDtypeStruct((chunks, few, shard), BF16),
            jax.ShapeDtypeStruct((rows, 128), F32),
            jax.ShapeDtypeStruct((rows, 128), I32),
        ],
        cost_estimate=pl.CostEstimate(
            flops=4 * rows * width * table.shape[0], transcendentals=0, bytes_accessed=8 * rows * width
        ),
        name="features",
    )(tab, hidden, roll, tokens, table, gain, returns, episode, action)


def logits_kernel(pieces, has_acc, last, tab_ref, *refs):
    count = sum(pieces)
    feats, refs = refs[:count], refs[count:]
    heads, refs = refs[: len(pieces)], refs[len(pieces) :]
    left = jnp.concatenate([ref[0] for ref in feats], axis=1)
    right = jnp.concatenate([ref[p] for ref, n in zip(heads, pieces) for p in range(n)], axis=0)
    logits = jnp.dot(left, right, preferred_element_type=F32)
    if has_acc:
        logits = logits + refs[0][...]
        refs = refs[1:]
    if not last:
        refs[0][...] = logits
        return
    advantage_ref, chosen_ref, out_ref = refs
    actions = logits.shape[1]
    top = jnp.max(logits, axis=1, keepdims=True)
    expo = jnp.exp(logits - top)
    probs = expo / jnp.sum(expo, axis=1, keepdims=True)
    advantage, action = advantage_ref[...], chosen_ref[...]
    lane = lax.broadcasted_iota(I32, action.shape, 1)
    for at in range(0, actions, 128):
        chosen = jnp.where(action == lane + at, 1.0, 0.0)
        out_ref[:, at : at + 128] = (advantage * (probs[:, at : at + 128] - chosen)).astype(BF16)


def logits_call(feats, tab, at, heads, acc=None, last=None):
    _, rows, half = feats.shape
    actions = heads[0].shape[2]
    pieces = tuple(h.shape[0] for h in heads)
    count = sum(pieces)
    tall = 512
    block = pl.BlockSpec((tall, actions), lambda i, t: (i, 0))
    thin = pl.BlockSpec((tall, 128), lambda i, t: (i, 0))
    in_specs = [
        pl.BlockSpec((1, tall, half), functools.partial(lambda k, i, t: (t[k], i, 0), at + k)) for k in range(count)
    ]
    in_specs += [pl.BlockSpec(h.shape, lambda i, t: (0, 0, 0)) for h in heads]
    args = [feats] * count + list(heads)
    if acc is not None:
        in_specs.append(block)
        args.append(acc)
    if last is not None:
        in_specs += [thin, thin]
        args += list(last)
    return pl.pallas_call(
        functools.partial(logits_kernel, pieces, acc is not None, last is not None),
        grid_spec=pltpu.PrefetchScalarGridSpec(
            num_scalar_prefetch=1, grid=(rows // tall,), in_specs=in_specs, out_specs=block
        ),
        out_shape=jax.ShapeDtypeStruct((rows, actions), F32 if last is None else BF16),
        cost_estimate=pl.CostEstimate(
            flops=2 * rows * count * half * actions, transcendentals=0, bytes_accessed=2 * rows * count * half
        ),
        name="logits",
    )(tab, *args)


def grad_kernel(count, tab_ref, scores_ref, *refs):
    feats, out_ref = refs[:count], refs[count]
    left = jnp.concatenate([ref[0] for ref in feats], axis=0)
    out = jnp.dot(left, scores_ref[...], preferred_element_type=F32)
    out_ref[...] = out.astype(out_ref.dtype).reshape(out_ref.shape)


def grad_call(scores, turned, tab, at, count, dtype):
    _, quarter, rows = turned.shape
    actions = scores.shape[1]
    each = min(count, 4)
    return pl.pallas_call(
        functools.partial(grad_kernel, each),
        grid_spec=pltpu.PrefetchScalarGridSpec(
            num_scalar_prefetch=1,
            grid=(count // each,),
            in_specs=[pl.BlockSpec((rows, actions), lambda i, t: (0, 0))]
            + [
                pl.BlockSpec((1, quarter, rows), functools.partial(lambda k, i, t: (t[at + i * each + k], 0, 0), k))
                for k in range(each)
            ],
            out_specs=pl.BlockSpec((each, quarter, actions), lambda i, t: (i, 0, 0)),
        ),
        out_shape=jax.ShapeDtypeStruct((count, quarter, actions), dtype),
        cost_estimate=pl.CostEstimate(
            flops=2 * rows * count * quarter * actions, transcendentals=0, bytes_accessed=2 * rows * count * quarter
        ),
        name="grad",
    )(tab, scores, *[turned] * each)


def old_logits_kernel(pieces, tab_ref, roll_ref, *refs):
    heads, out_ref = refs[:-1], refs[-1]
    blocks = [ref[p] for ref, n in zip(heads, pieces) for p in range(n)]
    left = jnp.concatenate([roll_ref[tab_ref[k]] for k in range(len(blocks))], axis=1)
    out_ref[...] = jnp.dot(left, jnp.concatenate(blocks, axis=0), preferred_element_type=F32)


def old_logits_call(roll, tab, heads):
    pieces = tuple(h.shape[0] for h in heads)
    full = lambda shape: pl.BlockSpec(shape, lambda i, t: (0,) * len(shape))
    out = (roll.shape[1], heads[0].shape[2])
    return pl.pallas_call(
        functools.partial(old_logits_kernel, pieces),
        grid_spec=pltpu.PrefetchScalarGridSpec(
            num_scalar_prefetch=1,
            grid=(1,),
            in_specs=[full(roll.shape)] + [full(h.shape) for h in heads],
            out_specs=full(out),
        ),
        out_shape=jax.ShapeDtypeStruct(out, F32),
        name="old_logits",
    )(tab, roll, *heads)


def share_kernel(count, tab_ref, own_ref, other_ref, *refs):
    rolls, grad_ref, outs = refs[:count], refs[count], refs[count + 1 :]
    quarter, actions = own_ref.shape[1:]
    for k in range(2):
        grad_ref[tab_ref[k]] = own_ref[k]
        grad_ref[tab_ref[2 + k]] = other_ref[k]
    grad = grad_ref[...].reshape(4 * quarter, actions)
    wide = grad.astype(F32)
    square = jnp.sum(wide * wide, keepdims=True)
    first = square.astype(BF16).astype(F32)
    second = (square - first).astype(BF16).astype(F32)
    third = square - first - second
    rows = rolls[0].shape[1]
    left = jnp.concatenate([ref[0] for ref in rolls], axis=0)
    part = jnp.dot(left, grad, preferred_element_type=F32)
    line = lax.broadcasted_iota(I32, (16, actions), 0)
    foot = jnp.where(line == 0, first, jnp.where(line == 1, second, third)).astype(BF16)
    for m in range(count):
        outs[m][:rows] = part[m * rows : (m + 1) * rows].astype(BF16)
        outs[m][rows:] = foot


def share_call(tab, own, other, rolls):
    quarter, actions = own.shape[1:]
    rows = rolls[0].shape[1]
    full = lambda shape: pl.BlockSpec(shape, lambda i, t: (0,) * len(shape))
    shape = (rows + 16, actions)
    return pl.pallas_call(
        functools.partial(share_kernel, len(rolls)),
        grid_spec=pltpu.PrefetchScalarGridSpec(
            num_scalar_prefetch=1,
            grid=(1,),
            in_specs=[full(own.shape)] * 2 + [full(rolls[0].shape)] * len(rolls),
            out_specs=[full((4, quarter, actions))] + [full(shape)] * len(rolls),
        ),
        out_shape=[jax.ShapeDtypeStruct((4, quarter, actions), BF16)]
        + [jax.ShapeDtypeStruct(shape, BF16)] * len(rolls),
        name="share",
    )(tab, own, other, *rolls)


def finish_kernel(count, old_ref, chosen_ref, head_ref, grad_ref, *refs):
    parts, (head_out, logp_out, episode_out) = refs[:count], refs[count:]
    rows, actions = old_ref.shape
    update = jnp.zeros((rows, actions), F32)
    square = jnp.zeros((1, actions), F32)
    for ref in parts:
        update += ref[:rows].astype(F32)
        foot = ref[rows:].astype(F32)
        square += foot[0:1] + foot[1:2] + foot[2:3]
    gnorm = jnp.sqrt(square + 1e-06)
    logits = old_ref[...] - step_length * update / gnorm
    top = jnp.max(logits, axis=-1, keepdims=True)
    total = jnp.log(jnp.sum(jnp.exp(logits - top), axis=-1, keepdims=True)) + top
    logp = jnp.sum(logits * chosen_ref[...], axis=-1, keepdims=True) - total
    here = lax.broadcasted_iota(I32, (rows, rows), 0) == lax.broadcasted_iota(I32, (rows, rows), 1)
    logp_out[...] = jnp.sum(jnp.where(here, logp, 0.0), axis=0, keepdims=True)
    episodes = rows // STEPS
    mine = lax.broadcasted_iota(I32, (rows, episodes), 0) // STEPS == lax.broadcasted_iota(I32, (rows, episodes), 1)
    episode_out[...] = jnp.sum(jnp.where(mine, logp, 0.0), axis=0, keepdims=True)
    head_out[...] = (head_ref[...].astype(F32) - step_length * grad_ref[...].astype(F32) / gnorm).astype(BF16)


def finish_call(old, chosen, head, grad, parts):
    rows = old.shape[0]
    return pl.pallas_call(
        functools.partial(finish_kernel, len(parts)),
        out_shape=[
            jax.ShapeDtypeStruct(head.shape, BF16),
            jax.ShapeDtypeStruct((1, rows), F32),
            jax.ShapeDtypeStruct((1, rows // STEPS), F32),
        ],
        name="finish",
    )(old, chosen, head, grad, *parts)


X, NEAR, FAR, CORE, Y = 1, 2, 4, 8, 16
GATHER = ((FAR, NEAR, X), (FAR, X, NEAR))
REDUCE = ((FAR, NEAR, Y, X), (FAR, X, NEAR, Y))


def span(basis):
    return [
        functools.reduce(lambda a, b: a ^ b, [m for k, m in enumerate(basis) if address >> k & 1], 0)
        for address in range(1 << len(basis))
    ]


def swap(value, mask):
    masks = mask if isinstance(mask, tuple) else (mask, mask)
    shards, devices = lax.axis_size("fsdp"), lax.axis_size(AXES)
    return lax.ppermute(value, AXES, [(i, i ^ masks[i // shards & 1]) for i in range(devices)])


def local_cube(
    traj_hidden, traj_tokens, traj_action, traj_return, traj_episode,
    roll_hidden, roll_tokens, roll_action, station_table, norm_gain, head_weight,
):
    shard, actions = head_weight.shape
    half, few = shard // 2, roll_hidden.shape[0]
    place = lax.axis_index("fsdp")
    group = lax.axis_index("grp")
    core, level = group % 2, group // 2

    def addresses(masks, flip):
        spans = [jnp.array(span(m), I32) for m in masks]
        mine = jnp.where(core == flip, spans[0], spans[1])
        return place ^ (mine & 7), level ^ (mine >> 4)

    halves = [2 * addresses(GATHER, flip)[0] + (core if flip == 0 else 1 - core) for flip in (0, 1)]
    order = jnp.concatenate([halves[0][:4], halves[1][:4], halves[0][4:], halves[1][4:]]).astype(I32)
    quarters = []
    for flip in (0, 1):
        at, up = addresses(REDUCE, flip)
        quarters.append(4 * at + 2 * (core if flip == 0 else 1 - core) + up)
    blocks = jnp.concatenate([quarters[1][8:], quarters[0][8:], quarters[1][:8], quarters[0][:8]]).astype(I32)
    lines = jnp.stack([2 * core + level, 2 * core + 1 - level, 2 - 2 * core + level, 3 - 2 * core - level])
    lines = lines.astype(I32)

    held = lax.dynamic_slice_in_dim(head_weight, core * half, half, 0)[None]
    came = swap(held, tuple(g[0] for g in GATHER))
    held = jnp.concatenate([held, came], axis=0)
    came = swap(held, tuple(g[1] for g in GATHER))
    held = jnp.concatenate([held, came], axis=0)
    came = swap(held, tuple(g[2] for g in GATHER))
    other_held = swap(held, CORE)
    other_came = swap(came, CORE)

    tokens = jnp.concatenate([traj_tokens, jnp.pad(roll_tokens, (0, 128 - few))]).reshape(1, -1)
    features, turned, roll_blocks, roll_parts, advantage, chosen = features_call(
        shard, place[None].astype(I32), traj_hidden, roll_hidden, tokens, station_table,
        norm_gain.reshape(1, -1), traj_return.reshape(1, -1), traj_episode, traj_action.reshape(1, -1),
    )
    logits = logits_call(features, order, 0, [held, other_held])
    logits = logits_call(features, order, 8, [came], acc=logits)
    scores = logits_call(features, order, 12, [other_came], acc=logits, last=(advantage, chosen))

    terms = []
    for part in range(2):
        out = grad_call(scores, turned, blocks, 16 * part, 8, BF16)
        crossed = swap(out, CORE)
        keep = grad_call(scores, turned, blocks, 16 * part + 8, 8, F32)
        terms.append([keep, crossed])
    (high, low), n = terms[::-1][1], 8
    send = (high + low.astype(F32)).astype(BF16)
    came_back = swap(send, tuple(r[3] for r in REDUCE))
    parts = terms[1] + [came_back]
    for k in (2, 1, 0):
        n = 1 << k
        send = sum(t[n : 2 * n].astype(F32) for t in parts).astype(BF16)
        parts = [t[:n] for t in parts] + [swap(send, tuple(r[k] for r in REDUCE))]
    own = sum(t.astype(F32) for t in parts).astype(BF16)
    own = jnp.concatenate([own, swap(own, Y)], axis=0)
    other = swap(own, CORE)

    rolls = [roll_parts[0:1]]
    for m in range(1, 8):
        rolls.append(swap(roll_parts[m : m + 1], m))
    grad, *shares = share_call(lines, own, other, rolls)
    for m in range(1, 8):
        shares[m] = swap(shares[m], m)
    old = old_logits_call(roll_blocks, order, [held, other_held, came, other_came])
    picked = (roll_action[:, None] == jnp.arange(actions, dtype=I32)[None, :]).astype(F32)
    new_head, action_logp, episode_logp = finish_call(old, picked, head_weight, grad.reshape(shard, actions), shares)
    return new_head, action_logp.reshape(-1), episode_logp.reshape(-1)


def station_rows(hidden, tokens, table, gain):
    stations = table.shape[0]
    lookup = (tokens[:, None] == jnp.arange(stations, dtype=I32)[None, :]).astype(BF16)
    embedded = jnp.dot(lookup, table, preferred_element_type=F32)
    mixed = hidden.astype(F32) + embedded
    power = jnp.mean(mixed * mixed, axis=-1, keepdims=True)
    return (mixed * lax.rsqrt(power + 1e-05) * gain).astype(BF16)


def picked_logp(logits, actions):
    top = jnp.max(logits, axis=-1, keepdims=True)
    total = jnp.log(jnp.sum(jnp.exp(logits - top), axis=-1)) + top[:, 0]
    chosen = (actions[:, None] == jnp.arange(logits.shape[1], dtype=I32)[None, :]).astype(F32)
    return jnp.sum(logits * chosen, axis=-1) - total


def episode_advantage(returns, episode):
    member = (episode[:, None] == jnp.arange(EPI_BLK, dtype=I32)[None, :]).astype(F32)
    sums = jnp.dot(member.T, returns, precision=lax.Precision.HIGHEST)
    counts = jnp.sum(member, axis=0)
    baseline = jnp.dot(member, sums / counts, precision=lax.Precision.HIGHEST)
    return returns - baseline


def local_plain(
    traj_hidden, traj_tokens, traj_action, traj_return, traj_episode,
    roll_hidden, roll_tokens, roll_action, station_table, norm_gain, head_weight,
):
    shard, actions = head_weight.shape
    features = station_rows(traj_hidden, traj_tokens, station_table, norm_gain)
    rollout = station_rows(roll_hidden, roll_tokens, station_table, norm_gain)
    advantage = episode_advantage(traj_return, traj_episode[0])
    full_old = lax.all_gather(head_weight, "fsdp", axis=0, tiled=True)
    logits = jnp.dot(features, full_old, preferred_element_type=F32)
    top = jnp.max(logits, axis=-1, keepdims=True)
    expo = jnp.exp(logits - top)
    probs = expo / jnp.sum(expo, axis=-1, keepdims=True)
    chosen = (traj_action[:, None] == jnp.arange(actions, dtype=I32)[None, :]).astype(F32)
    scores = (advantage[:, None] * (probs - chosen)).astype(BF16)
    local_grad = lax.dot_general(features, scores, (((0,), (0,)), ((), ())), preferred_element_type=F32)
    grad = lax.psum(local_grad, AXES)
    gnorm = jnp.sqrt(jnp.sum(grad * grad) + 1e-06)
    new_full = (full_old.astype(F32) - step_length * grad / gnorm).astype(BF16)
    new_head = lax.dynamic_slice_in_dim(new_full, lax.axis_index("fsdp") * shard, shard, 0)
    roll_logits = jnp.dot(rollout, new_full, preferred_element_type=F32)
    action_logp = picked_logp(roll_logits, roll_action)
    return new_head, action_logp, jnp.sum(action_logp.reshape(-1, STEPS), axis=1)


def fits(args, groups, shards):
    hidden, episode, roll, table, head = args[0], args[4], args[5], args[8], args[10]
    if (groups, shards) != (4, 8) or episode.shape[0] != 1:
        return False
    aligned = head.shape[0] % 512 == 0 and head.shape[1] % 128 == 0 and table.shape[0] % 128 == 0
    whole = hidden.shape[1] == shards * head.shape[0] and hidden.shape[0] % 512 == 0
    return aligned and whole and roll.shape[0] <= 128 and roll.shape[0] % STEPS == 0


def solution(mesh):
    groups, shards = mesh.shape["grp"], mesh.shape["fsdp"]

    def local(*args):
        if not fits(args, groups, shards):
            return local_plain(*args)
        return local_cube(*args)

    both = P(AXES)
    wide = P(AXES, None)
    return jax.shard_map(
        local,
        mesh=mesh,
        in_specs=(wide, both, both, both, wide, wide, both, both, P(), P(), P("fsdp", None)),
        out_specs=(P("fsdp", None), both, both),
        check_vma=False,
    )
```

time: 302 us -> 187 us (0.62)
  waiting for transfers between devices: 231 us -> 70.1 us
  Pallas kernels: 0 us -> 66.6 us
  starting transfers between devices: 0.08 us -> 37.2 us
  matrix products: 30.7 us -> 0 us
  other arithmetic: 23.8 us -> 6.42 us
  between operations: 14.8 us -> 1.07 us
  local copies, waits for them, and re-layouts: 1.87 us -> 4.9 us
    psum x1 -> x0, waiting for transfers between devices: 173 us -> none  [local(): grad = lax.psum(local_grad, ('grp', 'fsdp'))]
    ppermute x0 -> x27, waiting for transfers between devices: none -> 70.1 us  [swap(): lax.ppermute(value, AXES, [(i, i ^ masks[i // shards & 1]) for i in range...]
    pallas_call x0 -> x11, Pallas kernels: none -> 66.6 us  [the longest x1 19.3 us: features_call(): pl.pallas_call(functools.partial(features_kernel, chunks), grid_spec=pltp...]
    all_gather x1 -> x0, waiting for transfers between devices: 56.7 us -> none  [local(): full_old = lax.all_gather(head_weight, 'fsdp', axis=0, tiled=True)]
    ppermute x0 -> x27, starting transfers between devices: none -> 37.2 us  [swap(): lax.ppermute(value, AXES, [(i, i ^ masks[i // shards & 1]) for i in range...]
    dot_general x7 -> x0, matrix products: 30.7 us -> none  [the longest x2 12 us: station_rows(): embedded = jnp.dot(lookup, table, preferred_element_type=jnp.float32)]
    convert_element_type x2 -> x6, other arithmetic: 14.5 us -> 4.43 us  [the longest x1 1.94 us: local_cube(): send = (high + low.astype(F32)).astype(BF16)]
    reduce_sum x5 -> x0, other arithmetic: 8.62 us -> none  [the longest x1 6.14 us: local(): gnorm = jnp.sqrt(jnp.sum(grad * grad) + 1e-06)]
  transfers between devices with their start and end apart: 2 -> 27, of which waited for: 2 -> 12; matrix products, arithmetic and copies ran while one was open for 8% -> 3% of each run, Pallas kernels for 0% -> 27%
where the time goes in v1:
time: 187 us; the launch traced here: 186 us
  waiting for transfers between devices  70.1 us (37%)
  Pallas kernels  66.6 us (36%)
  starting transfers between devices  37.2 us (20%)
  other arithmetic  6.42 us (3%)
  local copies, waits for them, and re-layouts  4.9 us (3%)
    ppermute x27, waiting for transfers between devices, swap(): lax.ppermute(value, AXES, [(i, i ^ masks[i // shards & 1]) for i in range...  70.1 us
    ppermute x27, starting transfers between devices, swap(): lax.ppermute(value, AXES, [(i, i ^ masks[i // shards & 1]) for i in range...  37.2 us
    pallas_call x1, Pallas kernels, features_call(): pl.pallas_call(functools.partial(features_kernel, chunks), grid_spec=pltp...  19.3 us
    pallas_call x4, Pallas kernels, grad_call(): pl.pallas_call(functools.partial(grad_kernel, each), grid_spec=pltpu.Pref...  18.9 us
    pallas_call x3, Pallas kernels, logits_call(): pl.pallas_call(functools.partial(logits_kernel, pieces, acc is not None,...  17.9 us
    pallas_call x1, Pallas kernels, old_logits_call(): pl.pallas_call(functools.partial(old_logits_kernel, pieces), grid_spec=pl...  4.48 us
  transfers between devices with their start and end apart: 27, of which 12 were waited for; matrix products, arithmetic and copies ran while one was open for 3% of the time, Pallas kernels for 27%

profile of v1, /device:TPU:0, one launch (start us, length us, event | category | flops | bytes accessed | tf_op | source)
XLA Modules:
  0.0 186.3 jit_solution(8544043077409443424)
XLA Ops:
  1.7 4.1 %collective-permute-start = (bf16[1,256,512]{2,1,0:T(8,128)(2,1)S(1)}, bf16[1,256,512]{2,1,0:T(8,128)(2,1)S(1)}, u32[]{:S(2)}, u32[]{:S(2)}) collective-permute-start(bf16[1,256,512]{2,1,0:T(8,128)(2,1)S(1)} %dynamic-slice_bitcast_fusion), channel_id=1, source_target_pairs={{0,4},{1,5},{2,6},{3,7},{4,0},{5,1},{6,2},{7,3},{8,12},{9,13},{10,... | collective-permute-start | bytes 786440 | tf_op jit(solution)/shard_map/ppermute | solution.py:332
  5.8 11.9 %collective-permute-done = bf16[1,256,512]{2,1,0:T(8,128)(2,1)S(1)} collective-permute-done((bf16[1,256,512]{2,1,0:T(8,128)(2,1)S(1)}, bf16[1,256,512]{2,1,0:T(8,128)(2,1)S(1)}, u32[]{:S(2)}, u32[]{:S(2)}) %collective-permute-start) | collective-permute-done | bytes 262176 | tf_op jit(solution)/shard_map/ppermute | solution.py:332
  18.6 8.5 %collective-permute-done.1 = bf16[2,256,512]{2,1,0:T(8,128)(2,1)S(1)} collective-permute-done((bf16[2,256,512]{2,1,0:T(8,128)(2,1)S(1)}, bf16[2,256,512]{2,1,0:T(8,128)(2,1)S(1)}, u32[]{:S(2)}, u32[]{:S(2)}) %collective-permute-start.1) | collective-permute-done | bytes 524320 | tf_op jit(solution)/shard_map/ppermute | solution.py:332
  30.8 11.2 %collective-permute-done.3.refs_2_.refs_4_ = bf16[4,256,512]{2,1,0:T(8,128)(2,1)S(1)} collective-permute-done((bf16[4,256,512]{2,1,0:T(8,128)(2,1)S(1)}, bf16[4,256,512]{2,1,0:T(8,128)(2,1)S(1)}, u32[]{:S(2)}, u32[]{:S(2)}) %collective-permute-start.3) | collective-permute-done | bytes 1048608 | tf_op jit(solution)/shard_map/ppermute | solution.py:332
  42.0 19.3 %features.1 = (bf16[16,1024,256]{2,1,0:T(8,128)(2,1)}, bf16[32,128,1024]{2,1,0:T(8,128)(2,1)}, bf16[16,64,256]{2,1,0:T(8,128)(2,1)}, bf16[8,64,512]{2,1,0:T(8,12...) custom-call(s32[1]{0:T(128)} %bitcast.tab_ref, bf16[1024,4096]{1,0:T(8,128)(2,1)} %hidden_ref.1, ...), custom_call_target="tpu_custom_call" | custom-call | flops 8589934592 | bytes 33554432 | tf_op jit(solution)/shard_map/features/pallas_call | solution.py:85
  62.5 6.7 %logits.3.refs_5_ = f32[1024,512]{1,0:T(8,128)} custom-call(s32[16]{0:T(128)} %pad_add_fusion.1.tab_ref, bf16[16,1024,256]{2,1,0:T(8,128)(2,1)} %get-tuple-element.22.refs_0_.refs_1_.refs_2_.refs_3_.refs_4_.refs_5_.refs_6_.refs_7_, bf16[16,1024,256]{2,1,0:T(8,128)(2,1)} %get-tuple-element.22.refs_0_.refs_1_.refs_2_.refs_3_.refs_4_.refs_5_.refs_6_.refs_7_, ...), custom_call_target="tpu_custom_call" | custom-call | flops 2147483648 | bytes 4194304 | tf_op jit(solution)/shard_map/logits/pallas_call | solution.py:173
  69.2 5.2 %logits.4.refs_5_ = f32[1024,512]{1,0:T(8,128)} custom-call(s32[16]{0:T(128)} %pad_add_fusion.1.tab_ref, bf16[16,1024,256]{2,1,0:T(8,128)(2,1)} %get-tuple-element.22.refs_0_.refs_1_.refs_2_.refs_3_.refs_4_.refs_5_.refs_6_.refs_7_, bf16[16,1024,256]{2,1,0:T(8,128)(2,1)} %get-tuple-element.22.refs_0_.refs_1_.refs_2_.refs_3_.refs_4_.refs_5_.refs_6_.refs_7_, ...), custom_call_target="tpu_custom_call" | custom-call | flops 1073741824 | bytes 2097152 | tf_op jit(solution)/shard_map/logits/pallas_call | solution.py:173
  74.4 6.0 %logits.5.scores_ref = bf16[1024,512]{1,0:T(8,128)(2,1)} custom-call(s32[16]{0:T(128)} %pad_add_fusion.1.tab_ref, bf16[16,1024,256]{2,1,0:T(8,128)(2,1)} %get-tuple-element.22.refs_0_.refs_1_.refs_2_.refs_3_.refs_4_.refs_5_.refs_6_.refs_7_, bf16[16,1024,256]{2,1,0:T(8,128)(2,1)} %get-tuple-element.22.refs_0_.refs_1_.refs_2_.refs_3_.refs_4_.refs_5_.refs_6_.refs_7_, ...), custom_call_target="tpu_custom_call" | custom-call | flops 1073741824 | bytes 2097152 | tf_op jit(solution)/shard_map/logits/pallas_call | solution.py:173
  80.3 4.6 %grad.7 = bf16[8,128,512]{2,1,0:T(8,128)(2,1)} custom-call(s32[32]{0:T(128)} %pad_add_fusion.3.tab_ref, bf16[1024,512]{1,0:T(8,128)(2,1)} %logits.5.scores_ref, bf16[32,128,1024]{2,1,0:T(8,128)(2,1)} %get-tuple-element.25.refs_0_.refs_1_.refs_2_.refs_3_, bf16[32,128,1024]{2,1,0:T(8,128)(2,1)} %get-tuple-element.25.refs_0_.refs_1_.refs_2_.refs_3_, ...), custom_call_target="tpu_custom_call" | custom-call | flops 1073741824 | bytes 2097152 | tf_op jit(solution)/shard_map/grad/pallas_call | solution.py:197
  85.1 4.6 %grad.5 = bf16[8,128,512]{2,1,0:T(8,128)(2,1)} custom-call(s32[32]{0:T(128)} %pad_add_fusion.3.tab_ref, bf16[1024,512]{1,0:T(8,128)(2,1)} %logits.5.scores_ref, bf16[32,128,1024]{2,1,0:T(8,128)(2,1)} %get-tuple-element.25.refs_0_.refs_1_.refs_2_.refs_3_, bf16[32,128,1024]{2,1,0:T(8,128)(2,1)} %get-tuple-element.25.refs_0_.refs_1_.refs_2_.refs_3_, ...), custom_call_target="tpu_custom_call" | custom-call | flops 1073741824 | bytes 2097152 | tf_op jit(solution)/shard_map/grad/pallas_call | solution.py:197
  90.1 4.8 %grad.6 = f32[8,128,512]{2,1,0:T(8,128)} custom-call(s32[32]{0:T(128)} %pad_add_fusion.3.tab_ref, bf16[1024,512]{1,0:T(8,128)(2,1)} %logits.5.scores_ref, bf16[32,128,1024]{2,1,0:T(8,128)(2,1)} %get-tuple-element.25.refs_0_.refs_1_.refs_2_.refs_3_, bf16[32,128,1024]{2,1,0:T(8,128)(2,1)} %get-tuple-element.25.refs_0_.refs_1_.refs_2_.refs_3_, ...), custom_call_target="tpu_custom_call" | custom-call | flops 1073741824 | bytes 2097152 | tf_op jit(solution)/shard_map/grad/pallas_call | solution.py:197
  94.9 1.9 %add_convert_fusion = bf16[8,128,512]{2,1,0:T(8,128)(2,1)S(1)} fusion(f32[8,128,512]{2,1,0:T(8,128)} %grad.6, bf16[8,128,512]{2,1,0:T(8,128)(2,1)S(1)} %collective-permute-done.6), kind=kLoop, calls=%fused_computation | loop fusion | flops 1572864 | bytes 4194304 | tf_op jit(solution)/shard_map/convert_element_type | solution.py:385
  98.5 4.8 %grad.4 = f32[8,128,512]{2,1,0:T(8,128)} custom-call(s32[32]{0:T(128)} %pad_add_fusion.3.tab_ref, bf16[1024,512]{1,0:T(8,128)(2,1)} %logits.5.scores_ref, bf16[32,128,1024]{2,1,0:T(8,128)(2,1)} %get-tuple-element.25.refs_0_.refs_1_.refs_2_.refs_3_, bf16[32,128,1024]{2,1,0:T(8,128)(2,1)} %get-tuple-element.25.refs_0_.refs_1_.refs_2_.refs_3_, ...), custom_call_target="tpu_custom_call" | custom-call | flops 1073741824 | bytes 2097152 | tf_op jit(solution)/shard_map/grad/pallas_call | solution.py:197
  103.3 8.4 %collective-permute-done.7 = bf16[8,128,512]{2,1,0:T(8,128)(2,1)S(1)} collective-permute-done((bf16[8,128,512]{2,1,0:T(8,128)(2,1)S(1)}, bf16[8,128,512]{2,1,0:T(8,128)(2,1)S(1)}, u32[]{:S(2)}, u32[]{:S(2)}) %collective-permute-start.7) | collective-permute-done | bytes 1048608 | tf_op jit(solution)/shard_map/ppermute | solution.py:332
  114.8 7.6 %collective-permute-done.8 = bf16[4,128,512]{2,1,0:T(8,128)(2,1)S(1)} collective-permute-done((bf16[4,128,512]{2,1,0:T(8,128)(2,1)S(1)}, bf16[4,128,512]{2,1,0:T(8,128)(2,1)S(1)}, u32[]{:S(2)}, u32[]{:S(2)}) %collective-permute-start.8) | collective-permute-done | bytes 524320 | tf_op jit(solution)/shard_map/ppermute | solution.py:332
  123.4 5.6 %collective-permute-done.9 = bf16[2,128,512]{2,1,0:T(8,128)(2,1)S(1)} collective-permute-done((bf16[2,128,512]{2,1,0:T(8,128)(2,1)S(1)}, bf16[2,128,512]{2,1,0:T(8,128)(2,1)S(1)}, u32[]{:S(2)}, u32[]{:S(2)}) %collective-permute-start.9) | collective-permute-done | bytes 262176 | tf_op jit(solution)/shard_map/ppermute | solution.py:332
  129.1 2.2 %collective-permute-start.10 = (bf16[1,128,512]{2,1,0:T(8,128)(2,1)S(1)}, bf16[1,128,512]{2,1,0:T(8,128)(2,1)S(1)}, u32[]{:S(2)}, u32[]{:S(2)}) collective-permute-start(bf16[1,128,512]{2,1,0:T(8,128)(2,1)S(1)} %fusion.8), channel_id=1, source_target_pairs={{0,4},{1,5},{2,6},{3,7},{4,0},{5,1},{6,2},{7,3},{8,12},{9,13},{10,... | collective-permute-start | bytes 393224 | tf_op jit(solution)/shard_map/ppermute | solution.py:332
  131.3 5.2 %collective-permute-done.10 = bf16[1,128,512]{2,1,0:T(8,128)(2,1)S(1)} collective-permute-done((bf16[1,128,512]{2,1,0:T(8,128)(2,1)S(1)}, bf16[1,128,512]{2,1,0:T(8,128)(2,1)S(1)}, u32[]{:S(2)}, u32[]{:S(2)}) %collective-permute-start.10) | collective-permute-done | bytes 131104 | tf_op jit(solution)/shard_map/ppermute | solution.py:332
  138.2 3.4 %collective-permute-done.11 = bf16[1,128,512]{2,1,0:T(8,128)(2,1)S(1)} collective-permute-done((bf16[1,128,512]{2,1,0:T(8,128)(2,1)S(1)}, bf16[1,128,512]{2,1,0:T(8,128)(2,1)S(1)}, u32[]{:S(2)}, u32[]{:S(2)}) %collective-permute-start.11) | collective-permute-done | bytes 131104 | tf_op jit(solution)/shard_map/ppermute | solution.py:332
  142.4 3.9 %collective-permute-start.19 = (bf16[1,64,512]{2,1,0:T(8,128)(2,1)S(1)}, bf16[1,64,512]{2,1,0:T(8,128)(2,1)S(1)}, u32[]{:S(2)}, u32[]{:S(2)}) collective-permute-start(bf16[1,64,512]{2,1,0:T(8,128)(2,1)S(1)} %get-tuple-element.39), channel_id=1, source_target_pairs={{0,7},{1,6},{2,5},{3,4},{4,3},{5,2},{6,1},{7,0},{8,15},{9,14},{10,... | collective-permute-start | bytes 196616 | tf_op jit(solution)/shard_map/ppermute | solution.py:332
  147.2 2.8 %collective-permute-start.16 = (bf16[1,64,512]{2,1,0:T(8,128)(2,1)S(1)}, bf16[1,64,512]{2,1,0:T(8,128)(2,1)S(1)}, u32[]{:S(2)}, u32[]{:S(2)}) collective-permute-start(bf16[1,64,512]{2,1,0:T(8,128)(2,1)S(1)} %get-tuple-element.42), channel_id=1, source_target_pairs={{0,4},{1,5},{2,6},{3,7},{4,0},{5,1},{6,2},{7,3},{8,12},{9,13},{10,... | collective-permute-start | bytes 196616 | tf_op jit(solution)/shard_map/ppermute | solution.py:332
  153.3 3.1 %collective-permute-done.17.refs_5_ = bf16[1,64,512]{2,1,0:T(8,128)(2,1)S(1)} collective-permute-done((bf16[1,64,512]{2,1,0:T(8,128)(2,1)S(1)}, bf16[1,64,512]{2,1,0:T(8,128)(2,1)S(1)}, u32[]{:S(2)}, u32[]{:S(2)}) %collective-permute-start.17) | collective-permute-done | bytes 65568 | tf_op jit(solution)/shard_map/ppermute | solution.py:332
  156.3 1.8 collective-permute-start.13
  158.7 1.8 collective-permute-done.13.refs_1_
  161.3 3.2 %share.1 = (bf16[4,128,512]{2,1,0:T(8,128)(2,1)}, bf16[80,512]{1,0:T(8,128)(2,1)}, bf16[80,512]{1,0:T(8,128)(2,1)}, bf16[80,512]{1,0:T(8,128)(2,1)}, bf16[80,512...) custom-call(s32[4]{0:T(128)} %pad_add_fusion.2.tab_ref, ...), custom_call_target="tpu_custom_call" | custom-call | tf_op jit(solution)/shard_map/share/pallas_call | solution.py:268
  164.5 1.8 collective-permute-start.20
  168.7 3.5 %collective-permute-start.24 = (bf16[80,512]{1,0:T(8,128)(2,1)}, bf16[80,512]{1,0:T(8,128)(2,1)S(1)}, u32[]{:S(2)}, u32[]{:S(2)}) collective-permute-start(bf16[80,512]{1,0:T(8,128)(2,1)} %get-tuple-element.33), channel_id=1, source_target_pairs={{0,5},{1,4},{2,7},{3,6},{4,1},{5,0},{6,3},{7,2},{8,13},{9,12},{10,... | collective-permute-start | bytes 245768 | tf_op jit(solution)/shard_map/ppermute | solution.py:332
  172.2 1.8 collective-permute-start.25
  174.0 1.7 collective-permute-start.26
  176.4 4.5 %old_logits.1.old_ref = f32[64,512]{1,0:T(8,128)} custom-call(s32[16]{0:T(128)} %pad_add_fusion.1.tab_ref, bf16[16,64,256]{2,1,0:T(8,128)(2,1)} %get-tuple-element.21.roll_ref, bf16[4,256,512]{2,1,0:T(8,128)(2,1)} %copy-done, bf16[4,256,512]{2,1,0:T(8,128)(2,1)} %copy-done.2, bf16[4,256,512]{2,1,0:T(8,128)(2,1)} %copy-done.3, ...), custom_call_target="tpu_custom_call" | custom-call | tf_op jit(solution)/shard_map/old_logits/pallas_call | solution.py:228
  180.9 1.8 collective-permute-done.24.refs_5_
  183.4 2.9 %finish.1 = (bf16[512,512]{1,0:T(8,128)(2,1)}, f32[1,64]{1,0:T(1,128)}, f32[1,1]{1,0:T(1,128)}) custom-call(f32[64,512]{1,0:T(8,128)} %old_logits.1.old_ref, f32[64,512]{1,0:T(8,128)} %fusion.14.chosen_ref, bf16[512,512]{1,0:T(8,128)(2,1)} %head_ref.1, bf16[512,512]{1,0:T(8,128)(2,1)} %bitcast.13, bf16[80,512]{1,0:T(8,128)(2,1)} %get-tuple-element.28.refs_0_, ...), custom_call_target="tpu_custom_call" | custom-call | tf_op jit(solution)/shard_map/finish/pallas_call | solution.py:306
  (109 shorter events, 24.5 us)
Async XLA Ops:
  0.7 28.3 %copy-start.23 = (s32[64]{0:T(128)S(1)}, s32[64]{0:T(128)}, u32[]{:S(2)}) copy-start(s32[64]{0:T(128)} %param.25) | copy-start | bytes 772
  0.7 28.3 %copy-start.21 = (s32[1024]{0:T(1024)S(1)}, s32[1024]{0:T(1024)}, u32[]{:S(2)}) copy-start(s32[1024]{0:T(1024)} %param.20) | copy-start | bytes 12292
  1.7 16.1 %collective-permute-start = (bf16[1,256,512]{2,1,0:T(8,128)(2,1)S(1)}, bf16[1,256,512]{2,1,0:T(8,128)(2,1)S(1)}, u32[]{:S(2)}, u32[]{:S(2)}) collective-permute-start(bf16[1,256,512]{2,1,0:T(8,128)(2,1)S(1)} %dynamic-slice_bitcast_fusion), channel_id=1, source_target_pairs={{0,4},{1,5},{2,6},{3,7},{4,0},{5,1},{6,2},{7,3},{8,12},{9,13},{10,... | collective-permute-start | bytes 786440 | tf_op jit(solution)/shard_map/ppermute | solution.py:332
  17.8 9.2 %collective-permute-start.1 = (bf16[2,256,512]{2,1,0:T(8,128)(2,1)S(1)}, bf16[2,256,512]{2,1,0:T(8,128)(2,1)S(1)}, u32[]{:S(2)}, u32[]{:S(2)}) collective-permute-start(bf16[2,256,512]{2,1,0:T(8,128)(2,1)S(1)} %pad_maximum_fusion.1), channel_id=1, source_target_pairs={{0,2},{1,3},{2,0},{3,1},{4,6},{5,7},{6,4},{7,5},{8,9},{9,8},{10,11... | collective-permute-start | bytes 1572872 | tf_op jit(solution)/shard_map/ppermute | solution.py:332
  27.2 34.2 %copy-start = (bf16[4,256,512]{2,1,0:T(8,128)(2,1)}, bf16[4,256,512]{2,1,0:T(8,128)(2,1)S(1)}, u32[]{:S(2)}) copy-start(bf16[4,256,512]{2,1,0:T(8,128)(2,1)S(1)} %pad_maximum_fusion.refs_0_.refs_8_) | copy-start | bytes 3145732
  27.2 14.9 %collective-permute-start.3 = (bf16[4,256,512]{2,1,0:T(8,128)(2,1)S(1)}, bf16[4,256,512]{2,1,0:T(8,128)(2,1)S(1)}, u32[]{:S(2)}, u32[]{:S(2)}) collective-permute-start(bf16[4,256,512]{2,1,0:T(8,128)(2,1)S(1)} %pad_maximum_fusion.refs_0_.refs_8_), channel_id=1, source_target_pairs={{0,1},{1,0},{2,3},{3,2},{4,5},{5,4},{6,7},{7,6},{8,10},{9,11},{10,... | collective-permute-start | bytes 3145736 | tf_op jit(solution)/shard_map/ppermute | solution.py:332
  29.0 32.4 %collective-permute-start.2 = (bf16[4,256,512]{2,1,0:T(8,128)(2,1)S(1)}, bf16[4,256,512]{2,1,0:T(8,128)(2,1)S(1)}, u32[]{:S(2)}, u32[]{:S(2)}) collective-permute-start(bf16[4,256,512]{2,1,0:T(8,128)(2,1)S(1)} %pad_maximum_fusion.refs_0_.refs_8_), channel_id=1, source_target_pairs={{0,8},{1,9},{2,10},{3,11},{4,12},{5,13},{6,14},{7,15},{8,0},{9,1},... | collective-permute-start | bytes 3145736 | tf_op jit(solution)/shard_map/ppermute | solution.py:332
  42.0 32.4 %collective-permute-start.4 = (bf16[4,256,512]{2,1,0:T(8,128)(2,1)S(1)}, bf16[4,256,512]{2,1,0:T(8,128)(2,1)}, u32[]{:S(2)}, u32[]{:S(2)}) collective-permute-start(bf16[4,256,512]{2,1,0:T(8,128)(2,1)S(1)} %collective-permute-done.3.refs_2_.refs_4_), channel_id=1, source_target_pairs={{0,8},{1,9},{2,10},{3,11},{4,12},{5,13},{6,14},{7,15},{8,0},{9,1},... | collective-permute-start | bytes 3145736 | tf_op jit(solution)/shard_map/ppermute | solution.py:332
  85.0 10.0 %collective-permute-start.6 = (bf16[8,128,512]{2,1,0:T(8,128)(2,1)}, bf16[8,128,512]{2,1,0:T(8,128)(2,1)S(1)}, u32[]{:S(2)}, u32[]{:S(2)}) collective-permute-start(bf16[8,128,512]{2,1,0:T(8,128)(2,1)} %grad.7), channel_id=1, source_target_pairs={{0,8},{1,9},{2,10},{3,11},{4,12},{5,13},{6,14},{7,15},{8,0},{9,1},... | collective-permute-start | bytes 3145736 | tf_op jit(solution)/shard_map/ppermute | solution.py:332
  89.8 13.5 %collective-permute-start.5 = (bf16[8,128,512]{2,1,0:T(8,128)(2,1)}, bf16[8,128,512]{2,1,0:T(8,128)(2,1)S(1)}, u32[]{:S(2)}, u32[]{:S(2)}) collective-permute-start(bf16[8,128,512]{2,1,0:T(8,128)(2,1)} %grad.5), channel_id=1, source_target_pairs={{0,8},{1,9},{2,10},{3,11},{4,12},{5,13},{6,14},{7,15},{8,0},{9,1},... | collective-permute-start | bytes 3145736 | tf_op jit(solution)/shard_map/ppermute | solution.py:332
  96.9 14.9 %collective-permute-start.7 = (bf16[8,128,512]{2,1,0:T(8,128)(2,1)S(1)}, bf16[8,128,512]{2,1,0:T(8,128)(2,1)S(1)}, u32[]{:S(2)}, u32[]{:S(2)}) collective-permute-start(bf16[8,128,512]{2,1,0:T(8,128)(2,1)S(1)} %add_convert_fusion), channel_id=1, source_target_pairs={{0,1},{1,0},{2,3},{3,2},{4,5},{5,4},{6,7},{7,6},{8,24},{9,25},{10,... | collective-permute-start | bytes 3145736 | tf_op jit(solution)/shard_map/ppermute | solution.py:332
  113.2 28.5 %copy-start.5 = (bf16[8,64,512]{2,1,0:T(8,128)(2,1)S(1)}, bf16[8,64,512]{2,1,0:T(8,128)(2,1)}, u32[]{:S(2)}) copy-start(bf16[8,64,512]{2,1,0:T(8,128)(2,1)} %get-tuple-element.26) | copy-start | bytes 1572868
  113.2 9.2 %collective-permute-start.8 = (bf16[4,128,512]{2,1,0:T(8,128)(2,1)S(1)}, bf16[4,128,512]{2,1,0:T(8,128)(2,1)S(1)}, u32[]{:S(2)}, u32[]{:S(2)}) collective-permute-start(bf16[4,128,512]{2,1,0:T(8,128)(2,1)S(1)} %fusion.1), channel_id=1, source_target_pairs={{0,16},{1,17},{2,18},{3,19},{4,20},{5,21},{6,22},{7,23},{8,10},{9,... | collective-permute-start | bytes 1572872 | tf_op jit(solution)/shard_map/ppermute | solution.py:332
  122.6 53.1 %copy-start.22 = (s32[64]{0:T(128)S(1)}, s32[64]{0:T(128)}, u32[]{:S(2)}) copy-start(s32[64]{0:T(128)} %param.26) | copy-start | bytes 772
  122.6 6.4 %collective-permute-start.9 = (bf16[2,128,512]{2,1,0:T(8,128)(2,1)S(1)}, bf16[2,128,512]{2,1,0:T(8,128)(2,1)S(1)}, u32[]{:S(2)}, u32[]{:S(2)}) collective-permute-start(bf16[2,128,512]{2,1,0:T(8,128)(2,1)S(1)} %fusion.4), channel_id=1, source_target_pairs={{0,2},{1,3},{2,0},{3,1},{4,6},{5,7},{6,4},{7,5},{8,9},{9,8},{10,11... | collective-permute-start | bytes 786440 | tf_op jit(solution)/shard_map/ppermute | solution.py:332
  129.1 7.3 %collective-permute-start.10 = (bf16[1,128,512]{2,1,0:T(8,128)(2,1)S(1)}, bf16[1,128,512]{2,1,0:T(8,128)(2,1)S(1)}, u32[]{:S(2)}, u32[]{:S(2)}) collective-permute-start(bf16[1,128,512]{2,1,0:T(8,128)(2,1)S(1)} %fusion.8), channel_id=1, source_target_pairs={{0,4},{1,5},{2,6},{3,7},{4,0},{5,1},{6,2},{7,3},{8,12},{9,13},{10,... | collective-permute-start | bytes 393224 | tf_op jit(solution)/shard_map/ppermute | solution.py:332
  136.6 5.0 %collective-permute-start.11 = (bf16[1,128,512]{2,1,0:T(8,128)(2,1)S(1)}, bf16[1,128,512]{2,1,0:T(8,128)(2,1)S(1)}, u32[]{:S(2)}, u32[]{:S(2)}) collective-permute-start(bf16[1,128,512]{2,1,0:T(8,128)(2,1)S(1)} %fusion.13), channel_id=1, source_target_pairs={{0,16},{1,17},{2,18},{3,19},{4,20},{5,21},{6,22},{7,23},{8,24},{9,... | collective-permute-start | bytes 393224 | tf_op jit(solution)/shard_map/ppermute | solution.py:332
  141.6 18.9 %collective-permute-start.12 = (bf16[2,128,512]{2,1,0:T(8,128)(2,1)S(1)}, bf16[2,128,512]{2,1,0:T(8,128)(2,1)S(1)}, u32[]{:S(2)}, u32[]{:S(2)}) collective-permute-start(bf16[2,128,512]{2,1,0:T(8,128)(2,1)S(1)} %pad_maximum_fusion.2.own_ref), channel_id=1, source_target_pairs={{0,8},{1,9},{2,10},{3,11},{4,12},{5,13},{6,14},{7,15},{8,0},{9,1},... | collective-permute-start | bytes 786440 | tf_op jit(solution)/shard_map/ppermute | solution.py:332
  142.4 7.7 %collective-permute-start.19 = (bf16[1,64,512]{2,1,0:T(8,128)(2,1)S(1)}, bf16[1,64,512]{2,1,0:T(8,128)(2,1)S(1)}, u32[]{:S(2)}, u32[]{:S(2)}) collective-permute-start(bf16[1,64,512]{2,1,0:T(8,128)(2,1)S(1)} %get-tuple-element.39), channel_id=1, source_target_pairs={{0,7},{1,6},{2,5},{3,4},{4,3},{5,2},{6,1},{7,0},{8,15},{9,14},{10,... | collective-permute-start | bytes 196616 | tf_op jit(solution)/shard_map/ppermute | solution.py:332
  146.3 6.9 %collective-permute-start.18 = (bf16[1,64,512]{2,1,0:T(8,128)(2,1)S(1)}, bf16[1,64,512]{2,1,0:T(8,128)(2,1)S(1)}, u32[]{:S(2)}, u32[]{:S(2)}) collective-permute-start(bf16[1,64,512]{2,1,0:T(8,128)(2,1)S(1)} %get-tuple-element.40), channel_id=1, source_target_pairs={{0,6},{1,7},{2,4},{3,5},{4,2},{5,3},{6,0},{7,1},{8,14},{9,15},{10,... | collective-permute-start | bytes 196616 | tf_op jit(solution)/shard_map/ppermute | solution.py:332
  147.2 9.1 %collective-permute-start.17 = (bf16[1,64,512]{2,1,0:T(8,128)(2,1)S(1)}, bf16[1,64,512]{2,1,0:T(8,128)(2,1)S(1)}, u32[]{:S(2)}, u32[]{:S(2)}) collective-permute-start(bf16[1,64,512]{2,1,0:T(8,128)(2,1)S(1)} %get-tuple-element.41), channel_id=1, source_target_pairs={{0,5},{1,4},{2,7},{3,6},{4,1},{5,0},{6,3},{7,2},{8,13},{9,12},{10,... | collective-permute-start | bytes 196616 | tf_op jit(solution)/shard_map/ppermute | solution.py:332
  147.2 11.5 %collective-permute-start.16 = (bf16[1,64,512]{2,1,0:T(8,128)(2,1)S(1)}, bf16[1,64,512]{2,1,0:T(8,128)(2,1)S(1)}, u32[]{:S(2)}, u32[]{:S(2)}) collective-permute-start(bf16[1,64,512]{2,1,0:T(8,128)(2,1)S(1)} %get-tuple-element.42), channel_id=1, source_target_pairs={{0,4},{1,5},{2,6},{3,7},{4,0},{5,1},{6,2},{7,3},{8,12},{9,13},{10,... | collective-permute-start | bytes 196616 | tf_op jit(solution)/shard_map/ppermute | solution.py:332
  150.1 8.6 %collective-permute-start.15 = (bf16[1,64,512]{2,1,0:T(8,128)(2,1)S(1)}, bf16[1,64,512]{2,1,0:T(8,128)(2,1)S(1)}, u32[]{:S(2)}, u32[]{:S(2)}) collective-permute-start(bf16[1,64,512]{2,1,0:T(8,128)(2,1)S(1)} %get-tuple-element.43), channel_id=1, source_target_pairs={{0,3},{1,2},{2,1},{3,0},{4,7},{5,6},{6,5},{7,4},{8,11},{9,10},{10,... | collective-permute-start | bytes 196616 | tf_op jit(solution)/shard_map/ppermute | solution.py:332
  153.2 5.5 %collective-permute-start.14 = (bf16[1,64,512]{2,1,0:T(8,128)(2,1)S(1)}, bf16[1,64,512]{2,1,0:T(8,128)(2,1)S(1)}, u32[]{:S(2)}, u32[]{:S(2)}) collective-permute-start(bf16[1,64,512]{2,1,0:T(8,128)(2,1)S(1)} %get-tuple-element.44), channel_id=1, source_target_pairs={{0,2},{1,3},{2,0},{3,1},{4,6},{5,7},{6,4},{7,5},{8,10},{9,11},{10,... | collective-permute-start | bytes 196616 | tf_op jit(solution)/shard_map/ppermute | solution.py:332
  156.3 4.3 %collective-permute-start.13 = (bf16[1,64,512]{2,1,0:T(8,128)(2,1)S(1)}, bf16[1,64,512]{2,1,0:T(8,128)(2,1)S(1)}, u32[]{:S(2)}, u32[]{:S(2)}) collective-permute-start(bf16[1,64,512]{2,1,0:T(8,128)(2,1)S(1)} %get-tuple-element.45), channel_id=1, source_target_pairs={{0,1},{1,0},{2,3},{3,2},{4,5},{5,4},{6,7},{7,6},{8,9},{9,8},{10,11... | collective-permute-start | bytes 196616 | tf_op jit(solution)/shard_map/ppermute | solution.py:332
  164.5 7.7 %collective-permute-start.20 = (bf16[80,512]{1,0:T(8,128)(2,1)}, bf16[80,512]{1,0:T(8,128)(2,1)S(1)}, u32[]{:S(2)}, u32[]{:S(2)}) collective-permute-start(bf16[80,512]{1,0:T(8,128)(2,1)} %get-tuple-element.29), channel_id=1, source_target_pairs={{0,1},{1,0},{2,3},{3,2},{4,5},{5,4},{6,7},{7,6},{8,9},{9,8},{10,11... | collective-permute-start | bytes 245768 | tf_op jit(solution)/shard_map/ppermute | solution.py:332
  166.3 7.6 %collective-permute-start.21 = (bf16[80,512]{1,0:T(8,128)(2,1)}, bf16[80,512]{1,0:T(8,128)(2,1)S(1)}, u32[]{:S(2)}, u32[]{:S(2)}) collective-permute-start(bf16[80,512]{1,0:T(8,128)(2,1)} %get-tuple-element.30), channel_id=1, source_target_pairs={{0,2},{1,3},{2,0},{3,1},{4,6},{5,7},{6,4},{7,5},{8,10},{9,11},{10,... | collective-permute-start | bytes 245768 | tf_op jit(solution)/shard_map/ppermute | solution.py:332
  166.3 14.6 %collective-permute-start.22 = (bf16[80,512]{1,0:T(8,128)(2,1)}, bf16[80,512]{1,0:T(8,128)(2,1)S(1)}, u32[]{:S(2)}, u32[]{:S(2)}) collective-permute-start(bf16[80,512]{1,0:T(8,128)(2,1)} %get-tuple-element.31), channel_id=1, source_target_pairs={{0,3},{1,2},{2,1},{3,0},{4,7},{5,6},{6,5},{7,4},{8,11},{9,10},{10,... | collective-permute-start | bytes 245768 | tf_op jit(solution)/shard_map/ppermute | solution.py:332
  168.0 12.9 %collective-permute-start.23 = (bf16[80,512]{1,0:T(8,128)(2,1)}, bf16[80,512]{1,0:T(8,128)(2,1)S(1)}, u32[]{:S(2)}, u32[]{:S(2)}) collective-permute-start(bf16[80,512]{1,0:T(8,128)(2,1)} %get-tuple-element.32), channel_id=1, source_target_pairs={{0,4},{1,5},{2,6},{3,7},{4,0},{5,1},{6,2},{7,3},{8,12},{9,13},{10,... | collective-permute-start | bytes 245768 | tf_op jit(solution)/shard_map/ppermute | solution.py:332
  168.7 14.0 %collective-permute-start.24 = (bf16[80,512]{1,0:T(8,128)(2,1)}, bf16[80,512]{1,0:T(8,128)(2,1)S(1)}, u32[]{:S(2)}, u32[]{:S(2)}) collective-permute-start(bf16[80,512]{1,0:T(8,128)(2,1)} %get-tuple-element.33), channel_id=1, source_target_pairs={{0,5},{1,4},{2,7},{3,6},{4,1},{5,0},{6,3},{7,2},{8,13},{9,12},{10,... | collective-permute-start | bytes 245768 | tf_op jit(solution)/shard_map/ppermute | solution.py:332
  172.2 10.5 %collective-permute-start.25 = (bf16[80,512]{1,0:T(8,128)(2,1)}, bf16[80,512]{1,0:T(8,128)(2,1)S(1)}, u32[]{:S(2)}, u32[]{:S(2)}) collective-permute-start(bf16[80,512]{1,0:T(8,128)(2,1)} %get-tuple-element.34), channel_id=1, source_target_pairs={{0,6},{1,7},{2,4},{3,5},{4,2},{5,3},{6,0},{7,1},{8,14},{9,15},{10,... | collective-permute-start | bytes 245768 | tf_op jit(solution)/shard_map/ppermute | solution.py:332
  174.0 8.8 %collective-permute-start.26 = (bf16[80,512]{1,0:T(8,128)(2,1)}, bf16[80,512]{1,0:T(8,128)(2,1)S(1)}, u32[]{:S(2)}, u32[]{:S(2)}) collective-permute-start(bf16[80,512]{1,0:T(8,128)(2,1)} %get-tuple-element.35), channel_id=1, source_target_pairs={{0,7},{1,6},{2,5},{3,4},{4,3},{5,2},{6,1},{7,0},{8,15},{9,14},{10,... | collective-permute-start | bytes 245768 | tf_op jit(solution)/shard_map/ppermute | solution.py:332
  (23 other events, 221.7 us)

commit v2 on v1

v2 whole, which is shorter than its diff:
```python
import functools

import jax
import jax.numpy as jnp
import numpy as np
from jax import lax
from jax.experimental import pallas as pl
from jax.experimental.pallas import tpu as pltpu
from jax.sharding import PartitionSpec as P


EPI_BLK = 8
STEPS = 64
AXES = ("grp", "fsdp")
F32, BF16, I32 = jnp.float32, jnp.bfloat16, jnp.int32

step_length = 8.0


def room(mib):
    return pltpu.CompilerParams(vmem_limit_bytes=mib << 20)


def column(row):
    blocks = [jnp.broadcast_to(row[:, at : at + 128], (128, 128)) for at in range(0, row.shape[1], 128)]
    return jnp.concatenate([jnp.transpose(b) for b in blocks], axis=0)


SLOTS = 4


def features_kernel(start, last, tab_ref, hidden_ref, roll_ref, table_ref, *refs):
    small = [pltpu.make_async_copy(refs[k], refs[k - 7], refs[-1].at[k]) for k in range(6)]
    token_ref, roll_token_ref, gain_ref, return_ref, episode_ref, action_ref = refs[-7:-1]
    lookup_ref, mixed_ref, feats_stage, turned_stage, hidden_slots, roll_slots, table_slots, sems, out_sems = refs[-16:-7]
    outs = refs[6 + (2 if start else 0) : -16]
    feats_ref, turned_ref = outs[:2]
    rows, wide = hidden_slots.shape[1:]
    few, half, chunks = roll_slots.shape[1], wide // 2, mixed_ref.shape[0]
    groups = [(0, rows, hidden_slots)] + ([(rows, few, roll_slots)] if last else [])

    def fetch(chunk):
        slot, cut = chunk % SLOTS, slice(chunk * wide, (chunk + 1) * wide)
        moves = [(hidden_ref.at[start : start + rows, cut], hidden_slots), (table_ref.at[:, cut], table_slots)]
        if last:
            moves.append((roll_ref.at[:, cut], roll_slots))
        return [
            pltpu.make_async_copy(source, slots.at[slot], sems.at[k, slot]) for k, (source, slots) in enumerate(moves)
        ]

    def flush(chunk):
        slot = chunk % 2
        to = feats_ref.at[2 * chunk : 2 * chunk + 2, start : start + rows, :]
        turned_to = turned_ref.at[4 * chunk : 4 * chunk + 4, :, start : start + rows]
        return [
            pltpu.make_async_copy(feats_stage.at[slot], to, out_sems.at[0, slot]),
            pltpu.make_async_copy(turned_stage.at[slot], turned_to, out_sems.at[1, slot]),
        ]

    for copy in small:
        copy.start()
    for chunk in range(min(SLOTS, chunks)):
        for copy in fetch(chunk):
            copy.start()
    for copy in small:
        copy.wait()
    down = column(token_ref[:, start : start + rows])
    if last:
        here = lax.broadcasted_iota(I32, (few, few), 0) == lax.broadcasted_iota(I32, (few, few), 1)
        end = jnp.sum(jnp.where(here, roll_token_ref[...].astype(F32), 0.0), axis=1, keepdims=True).astype(I32)
        down = jnp.concatenate([down, jnp.broadcast_to(end, (few, 128))], axis=0)
    lane = lax.broadcasted_iota(I32, down.shape, 1)
    for at in range(0, table_ref.shape[0], 128):
        lookup_ref[:, at : at + 128] = jnp.where(down == lane + at, 1.0, 0.0).astype(BF16)
    powers = [jnp.zeros((n, 128), F32) for _, n, _ in groups]
    for chunk in range(chunks):
        slot = chunk % SLOTS
        for copy in fetch(chunk):
            copy.wait()
        embedded = jnp.dot(lookup_ref[...], table_slots[slot], preferred_element_type=F32)
        for g, (lo, n, ref) in enumerate(groups):
            mixed = ref[slot].astype(F32) + embedded[lo : lo + n]
            mixed_ref[chunk, lo : lo + n] = mixed
            square = mixed * mixed
            for at in range(0, wide, 128):
                powers[g] = powers[g] + square[:, at : at + 128]
        if chunk + SLOTS < chunks:
            for copy in fetch(chunk + SLOTS):
                copy.start()
    if last:
        returns, episode = return_ref[...], episode_ref[...]
        baseline = jnp.zeros_like(returns)
        for e in range(EPI_BLK):
            member = episode == e
            total = jnp.sum(jnp.where(member, returns, 0.0), axis=-1, keepdims=True)
            count = jnp.sum(jnp.where(member, 1.0, 0.0), axis=-1, keepdims=True)
            baseline = jnp.where(member, total / jnp.maximum(count, 1.0), baseline)
        outs[4][...] = column(returns - baseline)
        outs[5][...] = column(action_ref[...])
    scales = [lax.rsqrt(jnp.sum(p, axis=-1, keepdims=True) / (chunks * wide) + 1e-05) for p in powers]
    for chunk in range(chunks):
        slot, cut = chunk % 2, slice(chunk * wide, (chunk + 1) * wide)
        if chunk >= 2:
            for copy in flush(chunk - 2):
                copy.wait()
        value = (mixed_ref[chunk, :rows] * scales[0] * gain_ref[:, cut]).astype(BF16)
        feats_stage[slot, 0], feats_stage[slot, 1] = value[:, :half], value[:, half:]
        turned_stage[slot] = jnp.transpose(value).reshape(turned_stage.shape[1:])
        for copy in flush(chunk):
            copy.start()
        if last:
            value = (mixed_ref[chunk, rows:] * scales[1] * gain_ref[:, cut]).astype(BF16)
            roll_out_ref, roll_rel_ref = outs[2:4]
            roll_out_ref[2 * chunk], roll_out_ref[2 * chunk + 1] = value[:, :half], value[:, half:]
            roll_rel_ref[jnp.bitwise_xor(tab_ref[0], chunk)] = value
    for chunk in range(max(chunks - 2, 0), chunks):
        for copy in flush(chunk):
            copy.wait()


def features_call(shard, tab, start, rows, so_far, hidden, roll, table, tokens, roll_tokens, gain, returns, episode, action):
    tall, width = hidden.shape
    last = start + rows == tall
    half, few, chunks = shard // 2, roll.shape[0], width // shard
    quarter, all_rows = half // 2, rows + (few if last else 0)
    hbm, vmem = pl.BlockSpec(memory_space=pltpu.HBM), pl.BlockSpec(memory_space=pltpu.VMEM)
    anywhere = pl.BlockSpec(memory_space=pl.ANY)
    out_shape = [
        jax.ShapeDtypeStruct((2 * chunks, tall, half), BF16),
        jax.ShapeDtypeStruct((4 * chunks, quarter, tall), BF16),
        jax.ShapeDtypeStruct((2 * chunks, few, half), BF16),
        jax.ShapeDtypeStruct((chunks, few, shard), BF16),
        jax.ShapeDtypeStruct((tall, 128), F32),
        jax.ShapeDtypeStruct((tall, 128), I32),
    ]
    outs = 6 if last else 2
    args = (hidden, roll, table, tokens, roll_tokens, gain, returns, episode, action)
    args = [pltpu.with_memory_space_constraint(v, pltpu.HBM) for v in args]
    return pl.pallas_call(
        functools.partial(features_kernel, start, last),
        in_specs=[pl.BlockSpec(memory_space=pltpu.SMEM)] + [hbm] * 9 + [anywhere] * len(so_far),
        out_specs=([anywhere] * 2 + [vmem] * 4)[:outs],
        scratch_shapes=[
            pltpu.VMEM((all_rows, table.shape[0]), BF16),
            pltpu.VMEM((chunks, all_rows, shard), F32),
            pltpu.VMEM((2, 2, rows, half), BF16),
            pltpu.VMEM((2, 4, quarter, rows), BF16),
            pltpu.VMEM((SLOTS, rows, shard), BF16),
            pltpu.VMEM((SLOTS, few, shard), BF16),
            pltpu.VMEM((SLOTS, table.shape[0], shard), BF16),
            pltpu.SemaphoreType.DMA((3, SLOTS)),
            pltpu.SemaphoreType.DMA((2, 2)),
        ]
        + [pltpu.VMEM(v.shape, v.dtype) for v in args[3:]]
        + [pltpu.SemaphoreType.DMA((6,))],
        out_shape=out_shape[:outs],
        input_output_aliases={10 + k: k for k in range(len(so_far))},
        cost_estimate=pl.CostEstimate(
            flops=4 * rows * width * table.shape[0], transcendentals=0, bytes_accessed=8 * rows * width
        ),
        compiler_params=room(24),
        name="features",
    )(tab, *args, *so_far)


def join_heads(refs, pieces):
    halves = [
        jnp.concatenate([ref[p] for ref, n in zip(refs[c::2], pieces) for p in range(n)], axis=0) for c in range(2)
    ]
    return jnp.concatenate(halves, axis=1)


def logits_kernel(pieces, has_acc, last, tab_ref, *refs):
    count = sum(pieces)
    feats, refs = refs[:count], refs[count:]
    heads, refs = refs[: 2 * len(pieces)], refs[2 * len(pieces) :]
    left = jnp.concatenate([ref[0] for ref in feats], axis=1)
    right = join_heads(heads, pieces)
    logits = jnp.dot(left, right, preferred_element_type=F32)
    if has_acc:
        logits = logits + refs[0][...]
        refs = refs[1:]
    if not last:
        refs[0][...] = logits
        return
    advantage_ref, chosen_ref, out_ref = refs
    actions = logits.shape[1]
    top = jnp.max(logits, axis=1, keepdims=True)
    expo = jnp.exp(logits - top)
    probs = expo / jnp.sum(expo, axis=1, keepdims=True)
    advantage, action = advantage_ref[...], chosen_ref[...]
    lane = lax.broadcasted_iota(I32, action.shape, 1)
    for at in range(0, actions, 128):
        chosen = jnp.where(action == lane + at, 1.0, 0.0)
        out_ref[:, at : at + 128] = (advantage * (probs[:, at : at + 128] - chosen)).astype(BF16)


def logits_call(feats, tab, at, heads, acc=None, last=None):
    _, rows, half = feats.shape
    actions = 2 * heads[0][0].shape[2]
    pieces = tuple(h[0].shape[0] for h in heads)
    heads = [h for pair in heads for h in pair]
    count = sum(pieces)
    tall = 512
    block = pl.BlockSpec((tall, actions), lambda i, t: (i, 0))
    thin = pl.BlockSpec((tall, 128), lambda i, t: (i, 0))
    in_specs = [
        pl.BlockSpec((1, tall, half), functools.partial(lambda k, i, t: (t[k], i, 0), at + k)) for k in range(count)
    ]
    in_specs += [pl.BlockSpec(h.shape, lambda i, t: (0, 0, 0)) for h in heads]
    args = [feats] * count + list(heads)
    if acc is not None:
        in_specs.append(block)
        args.append(acc)
    if last is not None:
        in_specs += [thin, thin]
        args += list(last)
    return pl.pallas_call(
        functools.partial(logits_kernel, pieces, acc is not None, last is not None),
        grid_spec=pltpu.PrefetchScalarGridSpec(
            num_scalar_prefetch=1, grid=(rows // tall,), in_specs=in_specs, out_specs=block
        ),
        out_shape=jax.ShapeDtypeStruct((rows, actions), F32 if last is None else BF16),
        cost_estimate=pl.CostEstimate(
            flops=2 * rows * count * half * actions, transcendentals=0, bytes_accessed=2 * rows * count * half
        ),
        compiler_params=room(12),
        name="logits",
    )(tab, *args)


def grad_kernel(count, tab_ref, scores_ref, *refs):
    feats, extra, outs = refs[:count], refs[count:-2], refs[-2:]
    left = jnp.concatenate([ref[0] for ref in feats], axis=0)
    wide = outs[0].shape[2]
    for c, out_ref in enumerate(outs):
        right = scores_ref[:, c * wide : (c + 1) * wide]
        out = jnp.dot(left, right, preferred_element_type=F32).reshape(out_ref.shape)
        if extra:
            out = out + extra[c][...].astype(F32)
        out_ref[...] = out.astype(out_ref.dtype)


def grad_call(scores, turned, tab, at, count, dtype, *extra):
    _, quarter, rows = turned.shape
    actions = scores.shape[1]
    each = min(count, 4)
    block = pl.BlockSpec((each, quarter, actions // 2), lambda i, t: (i, 0, 0))
    return pl.pallas_call(
        functools.partial(grad_kernel, each),
        grid_spec=pltpu.PrefetchScalarGridSpec(
            num_scalar_prefetch=1,
            grid=(count // each,),
            in_specs=[pl.BlockSpec((rows, actions), lambda i, t: (0, 0))]
            + [
                pl.BlockSpec((1, quarter, rows), functools.partial(lambda k, i, t: (t[at + i * each + k], 0, 0), k))
                for k in range(each)
            ]
            + [block] * len(extra),
            out_specs=[block] * 2,
        ),
        out_shape=[jax.ShapeDtypeStruct((count, quarter, actions // 2), dtype)] * 2,
        cost_estimate=pl.CostEstimate(
            flops=2 * rows * count * quarter * actions, transcendentals=0, bytes_accessed=2 * rows * count * quarter
        ),
        compiler_params=room(10),
        name="grad",
    )(tab, scores, *[turned] * each, *extra)


def old_logits_kernel(pieces, tab_ref, roll_ref, *refs):
    heads, out_ref = refs[:-1], refs[-1]
    left = jnp.concatenate([roll_ref[tab_ref[ORDER + k]] for k in range(sum(pieces))], axis=1)
    out_ref[...] = jnp.dot(left, join_heads(heads, pieces), preferred_element_type=F32)


def old_logits_call(roll, tab, heads):
    pieces = tuple(h[0].shape[0] for h in heads)
    heads = [h for pair in heads for h in pair]
    full = lambda shape: pl.BlockSpec(shape, lambda i, t: (0,) * len(shape))
    out = (roll.shape[1], 2 * heads[0].shape[2])
    return pl.pallas_call(
        functools.partial(old_logits_kernel, pieces),
        grid_spec=pltpu.PrefetchScalarGridSpec(
            num_scalar_prefetch=1,
            grid=(1,),
            in_specs=[full(roll.shape)] + [full(h.shape) for h in heads],
            out_specs=full(out),
        ),
        out_shape=jax.ShapeDtypeStruct(out, F32),
        compiler_params=room(12),
        name="old_logits",
    )(tab, roll, *heads)


def split(value, wide):
    first = value.astype(BF16).astype(F32)
    second = (value - first).astype(BF16).astype(F32)
    line = lax.broadcasted_iota(I32, (16, wide), 0)
    third = jnp.where(line == 2, value - first - second, 0.0)
    return jnp.where(line == 0, first, jnp.where(line == 1, second, third)).astype(BF16)


def share_kernel(count, tab_ref, *refs):
    lines, rolls, grad_ref, outs = refs[:4], refs[4 : 4 + count], refs[4 + count], refs[5 + count :]
    quarter, actions = lines[0].shape[1:]
    for k, ref in enumerate(lines):
        grad_ref[tab_ref[LINES + k]] = ref[0]
    grad = grad_ref[...].reshape(4 * quarter, actions)
    wide = grad.astype(F32)
    square = jnp.sum(wide * wide, keepdims=True)
    rows = rolls[0].shape[1]
    left = jnp.concatenate([ref[0] for ref in rolls], axis=0)
    part = jnp.dot(left, grad, preferred_element_type=F32)
    foot = split(square, actions)
    far = count // 2
    for m in range(count):
        outs[m % far][m // far, :rows] = part[m * rows : (m + 1) * rows].astype(BF16)
        outs[m % far][m // far, rows:] = foot


def share_call(tab, lines, rolls):
    quarter, actions = lines[0].shape[1:]
    rows = rolls[0].shape[1]
    full = lambda shape: pl.BlockSpec(shape, lambda i, t: (0,) * len(shape))
    shape = (2, rows + 16, actions)
    return pl.pallas_call(
        functools.partial(share_kernel, len(rolls)),
        grid_spec=pltpu.PrefetchScalarGridSpec(
            num_scalar_prefetch=1,
            grid=(1,),
            in_specs=[full(lines[0].shape)] * 4 + [full(rolls[0].shape)] * len(rolls),
            out_specs=[full((4, quarter, actions))] + [full(shape)] * (len(rolls) // 2),
        ),
        out_shape=[jax.ShapeDtypeStruct((4, quarter, actions), BF16)]
        + [jax.ShapeDtypeStruct(shape, BF16)] * (len(rolls) // 2),
        compiler_params=room(6),
        name="share",
    )(tab, *lines, *rolls)


def join_kernel(*refs):
    parts, (stay_ref, send_ref) = refs[:-2], refs[-2:]
    rows = stay_ref.shape[0] - 16
    for k, out_ref in enumerate((stay_ref, send_ref)):
        total = parts[0][k].astype(F32)
        for ref in parts[1:]:
            total = total + ref[k].astype(F32)
        out_ref[:rows] = total[:rows].astype(out_ref.dtype)
        square = jnp.sum(total[rows:], axis=0, keepdims=True)
        if k == 0:
            out_ref[rows:] = jnp.broadcast_to(square, (16, square.shape[1]))
        else:
            out_ref[rows:] = split(square, square.shape[1])


def join_call(parts):
    shape = parts[0].shape[1:]
    return pl.pallas_call(
        join_kernel,
        out_shape=[jax.ShapeDtypeStruct(shape, F32), jax.ShapeDtypeStruct(shape, BF16)],
        compiler_params=room(4),
        name="join",
    )(*parts)


def finish_kernel(old_ref, chosen_ref, head_ref, grad_ref, stay_ref, far_ref, head_out, logp_out, episode_out):
    rows, _ = old_ref.shape
    update = stay_ref[:rows] + far_ref[:rows].astype(F32)
    square = stay_ref[rows : rows + 1] + jnp.sum(far_ref[rows:].astype(F32), axis=0, keepdims=True)
    gnorm = jnp.sqrt(square + 1e-06)
    logits = old_ref[...] - step_length * update / gnorm
    top = jnp.max(logits, axis=-1, keepdims=True)
    total = jnp.log(jnp.sum(jnp.exp(logits - top), axis=-1, keepdims=True)) + top
    logp = jnp.sum(logits * chosen_ref[...], axis=-1, keepdims=True) - total
    here = lax.broadcasted_iota(I32, (rows, rows), 0) == lax.broadcasted_iota(I32, (rows, rows), 1)
    logp_out[...] = jnp.sum(jnp.where(here, logp, 0.0), axis=0, keepdims=True)
    episodes = rows // STEPS
    mine = lax.broadcasted_iota(I32, (rows, episodes), 0) // STEPS == lax.broadcasted_iota(I32, (rows, episodes), 1)
    episode_out[...] = jnp.sum(jnp.where(mine, logp, 0.0), axis=0, keepdims=True)
    head_out[...] = (head_ref[...].astype(F32) - step_length * grad_ref[...].astype(F32) / gnorm).astype(BF16)


def finish_call(old, chosen, head, grad, stay, far):
    rows = old.shape[0]
    return pl.pallas_call(
        finish_kernel,
        out_shape=[
            jax.ShapeDtypeStruct(head.shape, BF16),
            jax.ShapeDtypeStruct((1, rows), F32),
            jax.ShapeDtypeStruct((1, rows // STEPS), F32),
        ],
        compiler_params=room(6),
        name="finish",
    )(old, chosen, head, grad, stay, far)


X, NEAR, FAR, CORE, Y = 1, 2, 4, 8, 16
GATHER = ((FAR, NEAR, X), (FAR, X, NEAR))
REDUCE = ((FAR, NEAR, Y, X), (FAR, X, NEAR, Y))


def span(basis):
    return [
        functools.reduce(lambda a, b: a ^ b, [m for k, m in enumerate(basis) if address >> k & 1], 0)
        for address in range(1 << len(basis))
    ]


ORDER, BLOCKS, LINES = 1, 17, 49


def tables():
    rows = []
    for level in range(2):
        for core in range(2):
            for place in range(8):
                halves, quarters = [], []
                for side in (core, 1 - core):
                    halves.append([2 * (place ^ m) + side for m in span(GATHER[side])])
                    quarters.append([4 * (place ^ m & 7) + 2 * side + (level ^ m >> 4) for m in span(REDUCE[side])])
                order = [h[lo : lo + 4] for lo in (0, 4) for h in halves]
                blocks = [q[lo : lo + 8] for lo in (8, 0) for q in quarters[::-1]]
                lines = [2 * (core ^ c) + (level ^ u) for c, u in ((0, 0), (0, 1), (1, 0), (1, 1))]
                rows.append([place] + sum(order, []) + sum(blocks, []) + lines)
    return np.array(rows, np.int32)


def swap(value, mask):
    masks = mask if isinstance(mask, tuple) else (mask, mask)
    shards, devices = lax.axis_size("fsdp"), lax.axis_size(AXES)
    return lax.ppermute(value, AXES, [(i, i ^ masks[i // shards & 1]) for i in range(devices)])


def local_cube(
    traj_hidden, traj_tokens, traj_action, traj_return, traj_episode,
    roll_hidden, roll_tokens, roll_action, station_table, norm_gain, head_weight,
):
    shard, actions = head_weight.shape
    half = shard // 2
    core = lax.axis_index("grp") % 2
    tab = lax.dynamic_index_in_dim(jnp.array(tables()), lax.axis_index(AXES), keepdims=False)

    wide = actions // 2
    held = [lax.dynamic_slice(head_weight, (core * half, c * wide), (half, wide))[None] for c in range(2)]
    came = [None, None]
    for k in range(3):
        for c in range(2):
            came[c] = swap(held[c], tuple(g[k] for g in GATHER))
            if k < 2:
                held[c] = jnp.concatenate([held[c], came[c]], axis=0)
    other_held, other_came = [], []
    for c in range(2):
        other_held.append(swap(held[c], CORE))
        other_came.append(swap(came[c], CORE))

    so_far, start, tall = (), 0, traj_hidden.shape[0]
    for rows in (tall * 3 // 8, tall * 3 // 8, tall // 4):
        so_far = features_call(
            shard, tab, start, rows, tuple(so_far), traj_hidden, roll_hidden, station_table,
            traj_tokens.reshape(1, -1), roll_tokens.reshape(1, -1), norm_gain.reshape(1, -1),
            traj_return.reshape(1, -1), traj_episode, traj_action.reshape(1, -1),
        )
        start += rows
    features, turned, roll_blocks, roll_parts, advantage, chosen = so_far
    logits = logits_call(features, tab, ORDER, [held, other_held])
    logits = logits_call(features, tab, ORDER + 8, [came], acc=logits)
    scores = logits_call(features, tab, ORDER + 12, [other_came], acc=logits, last=(advantage, chosen))

    crossed = []
    for part in range(2):
        outs = grad_call(scores, turned, tab, BLOCKS + 16 * part, 8, BF16)
        crossed.append([swap(out, CORE) for out in outs])
    sends = grad_call(scores, turned, tab, BLOCKS + 8, 8, BF16, *crossed[0])
    came_back = []
    for c in range(2):
        came_back.append(swap(sends[c], tuple(r[3] for r in REDUCE)))
    keeps = grad_call(scores, turned, tab, BLOCKS + 24, 8, F32, *crossed[1])
    parts = [[keeps[c], came_back[c]] for c in range(2)]
    for k in (2, 1, 0):
        n = 1 << k
        for c in range(2):
            send = sum(t[n : 2 * n].astype(F32) for t in parts[c]).astype(BF16)
            parts[c] = [t[:n] for t in parts[c]] + [swap(send, tuple(r[k] for r in REDUCE))]
    own = jnp.concatenate([sum(t.astype(F32) for t in p) for p in parts], axis=2).astype(BF16)
    lines = [own]
    for k, mask in enumerate((Y, CORE, CORE | Y)):
        lines.append(swap(own, mask))

    rolls = [roll_parts[0:1]]
    for m in range(1, 8):
        rolls.append(swap(roll_parts[m : m + 1], m))
    grad, *shares = share_call(tab, lines, rolls)
    for m in range(1, 4):
        shares[m] = swap(shares[m], m)
    stay, send = join_call(shares)
    far = swap(send, FAR)
    old = old_logits_call(roll_blocks, tab, [held, other_held, came, other_came])
    picked = (roll_action[:, None] == jnp.arange(actions, dtype=I32)[None, :]).astype(F32)
    new_head, action_logp, episode_logp = finish_call(old, picked, head_weight, grad.reshape(shard, actions), stay, far)
    return new_head, action_logp.reshape(-1), episode_logp.reshape(-1)


def station_rows(hidden, tokens, table, gain):
    stations = table.shape[0]
    lookup = (tokens[:, None] == jnp.arange(stations, dtype=I32)[None, :]).astype(BF16)
    embedded = jnp.dot(lookup, table, preferred_element_type=F32)
    mixed = hidden.astype(F32) + embedded
    power = jnp.mean(mixed * mixed, axis=-1, keepdims=True)
    return (mixed * lax.rsqrt(power + 1e-05) * gain).astype(BF16)


def picked_logp(logits, actions):
    top = jnp.max(logits, axis=-1, keepdims=True)
    total = jnp.log(jnp.sum(jnp.exp(logits - top), axis=-1)) + top[:, 0]
    chosen = (actions[:, None] == jnp.arange(logits.shape[1], dtype=I32)[None, :]).astype(F32)
    return jnp.sum(logits * chosen, axis=-1) - total


def episode_advantage(returns, episode):
    member = (episode[:, None] == jnp.arange(EPI_BLK, dtype=I32)[None, :]).astype(F32)
    sums = jnp.dot(member.T, returns, precision=lax.Precision.HIGHEST)
    counts = jnp.sum(member, axis=0)
    baseline = jnp.dot(member, sums / counts, precision=lax.Precision.HIGHEST)
    return returns - baseline


def local_plain(
    traj_hidden, traj_tokens, traj_action, traj_return, traj_episode,
    roll_hidden, roll_tokens, roll_action, station_table, norm_gain, head_weight,
):
    shard, actions = head_weight.shape
    features = station_rows(traj_hidden, traj_tokens, station_table, norm_gain)
    rollout = station_rows(roll_hidden, roll_tokens, station_table, norm_gain)
    advantage = episode_advantage(traj_return, traj_episode[0])
    full_old = lax.all_gather(head_weight, "fsdp", axis=0, tiled=True)
    logits = jnp.dot(features, full_old, preferred_element_type=F32)
    top = jnp.max(logits, axis=-1, keepdims=True)
    expo = jnp.exp(logits - top)
    probs = expo / jnp.sum(expo, axis=-1, keepdims=True)
    chosen = (traj_action[:, None] == jnp.arange(actions, dtype=I32)[None, :]).astype(F32)
    scores = (advantage[:, None] * (probs - chosen)).astype(BF16)
    local_grad = lax.dot_general(features, scores, (((0,), (0,)), ((), ())), preferred_element_type=F32)
    grad = lax.psum(local_grad, AXES)
    gnorm = jnp.sqrt(jnp.sum(grad * grad) + 1e-06)
    new_full = (full_old.astype(F32) - step_length * grad / gnorm).astype(BF16)
    new_head = lax.dynamic_slice_in_dim(new_full, lax.axis_index("fsdp") * shard, shard, 0)
    roll_logits = jnp.dot(rollout, new_full, preferred_element_type=F32)
    action_logp = picked_logp(roll_logits, roll_action)
    return new_head, action_logp, jnp.sum(action_logp.reshape(-1, STEPS), axis=1)


def fits(args, groups, shards):
    hidden, episode, roll, table, head = args[0], args[4], args[5], args[8], args[10]
    if (groups, shards) != (4, 8) or episode.shape[0] != 1:
        return False
    aligned = head.shape[0] % 512 == 0 and head.shape[1] % 128 == 0 and table.shape[0] % 128 == 0
    whole = hidden.shape[1] == shards * head.shape[0] and hidden.shape[0] % 1024 == 0
    return aligned and whole and roll.shape[0] <= 128 and roll.shape[0] % STEPS == 0


def solution(mesh):
    groups, shards = mesh.shape["grp"], mesh.shape["fsdp"]

    def local(*args):
        if not fits(args, groups, shards):
            return local_plain(*args)
        return local_cube(*args)

    both = P(AXES)
    wide = P(AXES, None)
    return jax.shard_map(
        local,
        mesh=mesh,
        in_specs=(wide, both, both, both, wide, wide, both, both, P(), P(), P("fsdp", None)),
        out_specs=(P("fsdp", None), both, both),
        check_vma=False,
    )
```

time: 187 us -> 146 us (0.78)
  Pallas kernels: 66.6 us -> 44.2 us
  other arithmetic: 6.42 us -> 0.61 us
  waiting for transfers between devices: 70.1 us -> 64.7 us
  starting transfers between devices: 37.2 us -> 33.4 us
  local copies, waits for them, and re-layouts: 4.9 us -> 1.73 us
    pallas_call x4, Pallas kernels: 18.9 us -> 8.15 us  [grad_call(): pl.pallas_call(functools.partial(grad_kernel, each), grid_spec=pltpu.Pref...]
    pallas_call x3, Pallas kernels: 17.9 us -> 7.77 us  [logits_call(): pl.pallas_call(functools.partial(logits_kernel, pieces, acc is not None,...]
    ppermute x27 -> x36, waiting for transfers between devices: 70.1 us -> 64.7 us  [swap(): lax.ppermute(value, AXES, [(i, i ^ masks[i // shards & 1]) for i in range...]
    ppermute x27 -> x36, starting transfers between devices: 37.2 us -> 33.4 us  [swap(): lax.ppermute(value, AXES, [(i, i ^ masks[i // shards & 1]) for i in range...]
    pallas_call x2 -> x5, Pallas kernels: 22.2 us -> 25.9 us  [the longest x3 24.4 us: features_call(): pl.pallas_call(functools.partial(features_kernel, start, last), in_specs=...]
    convert_element_type x5 -> x6, other arithmetic: 3.7 us -> 0.28 us  [local_cube(): send = sum((t[n:2 * n].astype(F32) for t in parts[c])).astype(BF16)]
    pallas_call x1, Pallas kernels: 4.48 us -> 1.38 us  [old_logits_call(): pl.pallas_call(functools.partial(old_logits_kernel, pieces), grid_spec=pl...]
    unnamed x56 -> x4, local copies, waits for them, and re-layouts: 2.51 us -> 0.01 us
  transfers between devices with their start and end apart: 27 -> 36, of which waited for: 12 -> 17; matrix products, arithmetic and copies ran while one was open for 3% -> 1% of each run, Pallas kernels for 27% -> 25%
where the time goes in v2:
time: 146 us
  waiting for transfers between devices  64.7 us (44%)
  Pallas kernels  44.2 us (30%)
  starting transfers between devices  33.4 us (23%)
  local copies, waits for them, and re-layouts  1.73 us (1%)
    ppermute x36, waiting for transfers between devices, swap(): lax.ppermute(value, AXES, [(i, i ^ masks[i // shards & 1]) for i in range...  64.7 us
    ppermute x36, starting transfers between devices, swap(): lax.ppermute(value, AXES, [(i, i ^ masks[i // shards & 1]) for i in range...  33.4 us
    pallas_call x3, Pallas kernels, features_call(): pl.pallas_call(functools.partial(features_kernel, start, last), in_specs=...  24.4 us
    pallas_call x4, Pallas kernels, grad_call(): pl.pallas_call(functools.partial(grad_kernel, each), grid_spec=pltpu.Pref...  8.15 us
    pallas_call x3, Pallas kernels, logits_call(): pl.pallas_call(functools.partial(logits_kernel, pieces, acc is not None,...  7.77 us
  transfers between devices with their start and end apart: 36, of which 17 were waited for; matrix products, arithmetic and copies ran while one was open for 1% of the time, Pallas kernels for 25%

profile of v2, /device:TPU:0, one launch (start us, length us, event | category | flops | bytes accessed | tf_op | source)
XLA Modules:
  0.0 145.6 jit_solution(8739481609358335653)
XLA Ops:
  1.6 4.1 %collective-permute-start = (bf16[1,256,256]{2,1,0:T(8,128)(2,1)S(1)}, bf16[1,256,256]{2,1,0:T(8,128)(2,1)S(1)}, u32[]{:S(2)}, u32[]{:S(2)}) collective-permute-start(bf16[1,256,256]{2,1,0:T(8,128)(2,1)S(1)} %get-tuple-element.68), channel_id=1, source_target_pairs={{0,4},{1,5},{2,6},{3,7},{4,0},{5,1},{6,2},{7,3},{8,12},{9,13},{10,... | collective-permute-start | bytes 393224 | tf_op jit(solution)/shard_map/ppermute | solution.py:432
  5.8 9.9 %collective-permute-done = bf16[1,256,256]{2,1,0:T(8,128)(2,1)S(1)} collective-permute-done((bf16[1,256,256]{2,1,0:T(8,128)(2,1)S(1)}, bf16[1,256,256]{2,1,0:T(8,128)(2,1)S(1)}, u32[]{:S(2)}, u32[]{:S(2)}) %collective-permute-start) | collective-permute-done | bytes 131104 | tf_op jit(solution)/shard_map/ppermute | solution.py:432
  15.8 1.8 %collective-permute-done.2 = bf16[1,256,256]{2,1,0:T(8,128)(2,1)S(1)} collective-permute-done((bf16[1,256,256]{2,1,0:T(8,128)(2,1)S(1)}, bf16[1,256,256]{2,1,0:T(8,128)(2,1)S(1)}, u32[]{:S(2)}, u32[]{:S(2)}) %collective-permute-start.2) | collective-permute-done | bytes 131104 | tf_op jit(solution)/shard_map/ppermute | solution.py:432
  18.5 3.7 %collective-permute-done.1 = bf16[2,256,256]{2,1,0:T(8,128)(2,1)S(1)} collective-permute-done((bf16[2,256,256]{2,1,0:T(8,128)(2,1)S(1)}, bf16[2,256,256]{2,1,0:T(8,128)(2,1)S(1)}, u32[]{:S(2)}, u32[]{:S(2)}) %collective-permute-start.1) | collective-permute-done | bytes 262176 | tf_op jit(solution)/shard_map/ppermute | solution.py:432
  22.3 2.2 %collective-permute-start.6 = (bf16[4,256,256]{2,1,0:T(8,128)(2,1)S(1)}, bf16[4,256,256]{2,1,0:T(8,128)(2,1)S(1)}, u32[]{:S(2)}, u32[]{:S(2)}) collective-permute-start(bf16[4,256,256]{2,1,0:T(8,128)(2,1)S(1)} %pad_maximum_fusion.refs_0_.refs_8_), channel_id=1, source_target_pairs={{0,1},{1,0},{2,3},{3,2},{4,5},{5,4},{6,7},{7,6},{8,10},{9,11},{10,... | collective-permute-start | bytes 1572872 | tf_op jit(solution)/shard_map/ppermute | solution.py:432
  24.4 3.1 %collective-permute-done.3 = bf16[2,256,256]{2,1,0:T(8,128)(2,1)S(1)} collective-permute-done((bf16[2,256,256]{2,1,0:T(8,128)(2,1)S(1)}, bf16[2,256,256]{2,1,0:T(8,128)(2,1)S(1)}, u32[]{:S(2)}, u32[]{:S(2)}) %collective-permute-start.3) | collective-permute-done | bytes 262176 | tf_op jit(solution)/shard_map/ppermute | solution.py:432
  27.6 2.4 %collective-permute-start.7 = (bf16[4,256,256]{2,1,0:T(8,128)(2,1)S(1)}, bf16[4,256,256]{2,1,0:T(8,128)(2,1)S(1)}, u32[]{:S(2)}, u32[]{:S(2)}) collective-permute-start(bf16[4,256,256]{2,1,0:T(8,128)(2,1)S(1)} %pad_maximum_fusion.1.refs_1_.refs_9_), channel_id=1, source_target_pairs={{0,1},{1,0},{2,3},{3,2},{4,5},{5,4},{6,7},{7,6},{8,10},{9,11},{10,... | collective-permute-start | bytes 1572872 | tf_op jit(solution)/shard_map/ppermute | solution.py:432
  31.2 8.6 %features.3 = (bf16[16,1024,256]{2,1,0:T(8,128)(2,1)S(1)}, bf16[32,128,1024]{2,1,0:T(8,128)(2,1)S(1)}) custom-call(s32[53]{0:T(128)S(1)} %dynamic-slice_bitcast_fusion.2.tab_ref, bf16[1024,4096]{1,0:T(8,128)(2,1)} %hidden_ref.5, bf16[64,4096]{1,0:T(8,128)(2,1)} %roll_ref.5, bf16[512,4096]{1,0:T(8,128)(2,1)} %table_ref.5, s32[1,1024]{1,0:T(1,128)} %bitcast.18, ...), custom_call_target="tpu_custom_call" | custom-call | flops 3221225472 | bytes 12582912 | tf_op jit(solution)/shard_map/features/pallas_call | solution.py:139
  40.5 8.4 %features.4 = (bf16[16,1024,256]{2,1,0:T(8,128)(2,1)S(1)}, bf16[32,128,1024]{2,1,0:T(8,128)(2,1)S(1)}) custom-call(s32[53]{0:T(128)S(1)} %dynamic-slice_bitcast_fusion.2.tab_ref, bf16[1024,4096]{1,0:T(8,128)(2,1)} %hidden_ref.5, bf16[64,4096]{1,0:T(8,128)(2,1)} %roll_ref.5, ...), custom_call_target="tpu_custom_call", output_to_operand_aliasing={{0}: (10, {}), {1}: (11, {})} | custom-call | flops 3221225472 | bytes 12582912 | tf_op jit(solution)/shard_map/features/pallas_call | solution.py:139
  48.9 7.4 %features.5 = (bf16[16,1024,256]{2,1,0:T(8,128)(2,1)S(1)}, bf16[32,128,1024]{2,1,0:T(8,128)(2,1)S(1)}, bf16[16,64,256]{2,1,0:T(8,128)(2,1)S(1)}, bf16[8,64,512]{...) custom-call(s32[53]{0:T(128)S(1)} %dynamic-slice_bitcast_fusion.2.ta, ...), custom_call_target="tpu_custom_call", output_to_operand_aliasing={{0}: (10, {}), {1}: (11, {})} | custom-call | flops 2147483648 | bytes 8388608 | tf_op jit(solution)/shard_map/features/pallas_call | solution.py:139
  56.3 3.1 %logits.3.refs_6_ = f32[1024,512]{1,0:T(8,128)S(1)} custom-call(s32[53]{0:T(128)S(1)} %dynamic-slice_bitcast_fusion.2.tab_ref, bf16[16,1024,256]{2,1,0:T(8,128)(2,1)S(1)} %get-tuple-element.36.refs_0_.refs_1_.refs_2_.refs_3_.refs_4_.refs_5_.refs_6_.refs_7_, ...), custom_call_target="tpu_custom_call" | custom-call | flops 2147483648 | bytes 4194304 | tf_op jit(solution)/shard_map/logits/pallas_call | solution.py:218
  59.4 2.0 %logits.4.refs_6_ = f32[1024,512]{1,0:T(8,128)S(1)} custom-call(s32[53]{0:T(128)S(1)} %dynamic-slice_bitcast_fusion.2.tab_ref, bf16[16,1024,256]{2,1,0:T(8,128)(2,1)S(1)} %get-tuple-element.36.refs_0_.refs_1_.refs_2_.refs_3_.refs_4_.refs_5_.refs_6_.refs_7_, ...), custom_call_target="tpu_custom_call" | custom-call | flops 1073741824 | bytes 2097152 | tf_op jit(solution)/shard_map/logits/pallas_call | solution.py:218
  61.4 2.7 %logits.5.scores_ref = bf16[1024,512]{1,0:T(8,128)(2,1)S(1)} custom-call(s32[53]{0:T(128)S(1)} %dynamic-slice_bitcast_fusion.2.tab_ref, bf16[16,1024,256]{2,1,0:T(8,128)(2,1)S(1)} %get-tuple-element.36.refs_0_.refs_1_.refs_2_.refs_3_.refs_4_.refs_5_.refs_6_.refs_7_, ...), custom_call_target="tpu_custom_call" | custom-call | flops 1073741824 | bytes 2097152 | tf_op jit(solution)/shard_map/logits/pallas_call | solution.py:218
  64.1 2.0 %grad.6 = (bf16[8,128,256]{2,1,0:T(8,128)(2,1)S(1)}, bf16[8,128,256]{2,1,0:T(8,128)(2,1)S(1)}) custom-call(s32[53]{0:T(128)S(1)} %dynamic-slice_bitcast_fusion.2.tab_ref, bf16[1024,512]{1,0:T(8,128)(2,1)S(1)} %logits.5.scores_ref, bf16[32,128,1024]{2,1,0:T(8,128)(2,1)S(1)} %get-tuple-element.39.refs_0_.refs_1_.refs_2_.refs_3_, ...), custom_call_target="tpu_custom_call" | custom-call | flops 1073741824 | bytes 2097152 | tf_op jit(solution)/shard_map/grad/pallas_call | solution.py:249
  66.7 2.0 %grad.4 = (bf16[8,128,256]{2,1,0:T(8,128)(2,1)S(1)}, bf16[8,128,256]{2,1,0:T(8,128)(2,1)S(1)}) custom-call(s32[53]{0:T(128)S(1)} %dynamic-slice_bitcast_fusion.2.tab_ref, bf16[1024,512]{1,0:T(8,128)(2,1)S(1)} %logits.5.scores_ref, bf16[32,128,1024]{2,1,0:T(8,128)(2,1)S(1)} %get-tuple-element.39.refs_0_.refs_1_.refs_2_.refs_3_, ...), custom_call_target="tpu_custom_call" | custom-call | flops 1073741824 | bytes 2097152 | tf_op jit(solution)/shard_map/grad/pallas_call | solution.py:249
  69.3 2.2 %grad.7 = (bf16[8,128,256]{2,1,0:T(8,128)(2,1)S(1)}, bf16[8,128,256]{2,1,0:T(8,128)(2,1)S(1)}) custom-call(s32[53]{0:T(128)S(1)} %dynamic-slice_bitcast_fusion.2.tab_ref, bf16[1024,512]{1,0:T(8,128)(2,1)S(1)} %logits.5.scores_ref, bf16[32,128,1024]{2,1,0:T(8,128)(2,1)S(1)} %get-tuple-element.39.refs_0_.refs_1_.refs_2_.refs_3_, ...), custom_call_target="tpu_custom_call" | custom-call | flops 1073741824 | bytes 2097152 | tf_op jit(solution)/shard_map/grad/pallas_call | solution.py:249
  71.6 2.0 %collective-permute-start.18 = (bf16[8,128,256]{2,1,0:T(8,128)(2,1)S(1)}, bf16[8,128,256]{2,1,0:T(8,128)(2,1)S(1)}, u32[]{:S(2)}, u32[]{:S(2)}) collective-permute-start(bf16[8,128,256]{2,1,0:T(8,128)(2,1)S(1)} %get-tuple-element.47), channel_id=1, source_target_pairs={{0,1},{1,0},{2,3},{3,2},{4,5},{5,4},{6,7},{7,6},{8,24},{9,25},{10,... | collective-permute-start | bytes 1572872 | tf_op jit(solution)/shard_map/ppermute | solution.py:432
  73.6 2.0 %grad.5 = (f32[8,128,256]{2,1,0:T(8,128)S(1)}, f32[8,128,256]{2,1,0:T(8,128)S(1)}) custom-call(s32[53]{0:T(128)S(1)} %dynamic-slice_bitcast_fusion.2.tab_ref, bf16[1024,512]{1,0:T(8,128)(2,1)S(1)} %logits.5.scores_ref, bf16[32,128,1024]{2,1,0:T(8,128)(2,1)S(1)} %get-tuple-element.39.refs_0_.refs_1_.refs_2_.refs_3_, ...), custom_call_target="tpu_custom_call" | custom-call | flops 1073741824 | bytes 2097152 | tf_op jit(solution)/shard_map/grad/pallas_call | solution.py:249
  75.6 5.1 %collective-permute-done.14 = bf16[8,128,256]{2,1,0:T(8,128)(2,1)S(1)} collective-permute-done((bf16[8,128,256]{2,1,0:T(8,128)(2,1)S(1)}, bf16[8,128,256]{2,1,0:T(8,128)(2,1)S(1)}, u32[]{:S(2)}, u32[]{:S(2)}) %collective-permute-start.14) | collective-permute-done | bytes 524320 | tf_op jit(solution)/shard_map/ppermute | solution.py:432
  82.4 4.0 %collective-permute-done.18 = bf16[8,128,256]{2,1,0:T(8,128)(2,1)S(1)} collective-permute-done((bf16[8,128,256]{2,1,0:T(8,128)(2,1)S(1)}, bf16[8,128,256]{2,1,0:T(8,128)(2,1)S(1)}, u32[]{:S(2)}, u32[]{:S(2)}) %collective-permute-start.18) | collective-permute-done | bytes 524320 | tf_op jit(solution)/shard_map/ppermute | solution.py:432
  88.6 2.9 %collective-permute-start.27 = (bf16[1,64,512]{2,1,0:T(8,128)(2,1)S(1)}, bf16[1,64,512]{2,1,0:T(8,128)(2,1)S(1)}, u32[]{:S(2)}, u32[]{:S(2)}) collective-permute-start(bf16[1,64,512]{2,1,0:T(8,128)(2,1)S(1)} %get-tuple-element.63), channel_id=1, source_target_pairs={{0,3},{1,2},{2,1},{3,0},{4,7},{5,6},{6,5},{7,4},{8,11},{9,10},{10,... | collective-permute-start | bytes 196616 | tf_op jit(solution)/shard_map/ppermute | solution.py:432
  92.9 5.4 %collective-permute-done.16 = bf16[2,128,256]{2,1,0:T(8,128)(2,1)S(1)} collective-permute-done((bf16[2,128,256]{2,1,0:T(8,128)(2,1)S(1)}, bf16[2,128,256]{2,1,0:T(8,128)(2,1)S(1)}, u32[]{:S(2)}, u32[]{:S(2)}) %collective-permute-start.16) | collective-permute-done | bytes 131104 | tf_op jit(solution)/shard_map/ppermute | solution.py:432
  98.3 4.9 %collective-permute-done.20 = bf16[2,128,256]{2,1,0:T(8,128)(2,1)S(1)} collective-permute-done((bf16[2,128,256]{2,1,0:T(8,128)(2,1)S(1)}, bf16[2,128,256]{2,1,0:T(8,128)(2,1)S(1)}, u32[]{:S(2)}, u32[]{:S(2)}) %collective-permute-start.20) | collective-permute-done | bytes 131104 | tf_op jit(solution)/shard_map/ppermute | solution.py:432
  104.6 5.0 %collective-permute-done.17 = bf16[1,128,256]{2,1,0:T(8,128)(2,1)S(1)} collective-permute-done((bf16[1,128,256]{2,1,0:T(8,128)(2,1)S(1)}, bf16[1,128,256]{2,1,0:T(8,128)(2,1)S(1)}, u32[]{:S(2)}, u32[]{:S(2)}) %collective-permute-start.17) | collective-permute-done | bytes 65568 | tf_op jit(solution)/shard_map/ppermute | solution.py:432
  110.4 4.8 %collective-permute-done.21 = bf16[1,128,256]{2,1,0:T(8,128)(2,1)S(1)} collective-permute-done((bf16[1,128,256]{2,1,0:T(8,128)(2,1)S(1)}, bf16[1,128,256]{2,1,0:T(8,128)(2,1)S(1)}, u32[]{:S(2)}, u32[]{:S(2)}) %collective-permute-start.21) | collective-permute-done | bytes 65568 | tf_op jit(solution)/shard_map/ppermute | solution.py:432
  118.1 3.2 %collective-permute-done.29.refs_9_ = bf16[1,64,512]{2,1,0:T(8,128)(2,1)S(1)} collective-permute-done((bf16[1,64,512]{2,1,0:T(8,128)(2,1)S(1)}, bf16[1,64,512]{2,1,0:T(8,128)(2,1)S(1)}, u32[]{:S(2)}, u32[]{:S(2)}) %collective-permute-start.29) | collective-permute-done | bytes 65568 | tf_op jit(solution)/shard_map/ppermute | solution.py:432
  123.6 4.6 %collective-permute-done.31.refs_11_ = bf16[1,64,512]{2,1,0:T(8,128)(2,1)S(1)} collective-permute-done((bf16[1,64,512]{2,1,0:T(8,128)(2,1)S(1)}, bf16[1,64,512]{2,1,0:T(8,128)(2,1)S(1)}, u32[]{:S(2)}, u32[]{:S(2)}) %collective-permute-start.31) | collective-permute-done | bytes 65568 | tf_op jit(solution)/shard_map/ppermute | solution.py:432
  129.4 3.4 %collective-permute-start.34 = (bf16[2,80,512]{2,1,0:T(8,128)(2,1)S(1)}, bf16[2,80,512]{2,1,0:T(8,128)(2,1)S(1)}, u32[]{:S(2)}, u32[]{:S(2)}) collective-permute-start(bf16[2,80,512]{2,1,0:T(8,128)(2,1)S(1)} %get-tuple-element.53), channel_id=1, source_target_pairs={{0,3},{1,2},{2,1},{3,0},{4,7},{5,6},{6,5},{7,4},{8,11},{9,10},{10,... | collective-permute-start | bytes 491528 | tf_op jit(solution)/shard_map/ppermute | solution.py:432
  132.8 2.8 %collective-permute-done.32.refs_1_ = bf16[2,80,512]{2,1,0:T(8,128)(2,1)S(1)} collective-permute-done((bf16[2,80,512]{2,1,0:T(8,128)(2,1)S(1)}, bf16[2,80,512]{2,1,0:T(8,128)(2,1)S(1)}, u32[]{:S(2)}, u32[]{:S(2)}) %collective-permute-start.32) | collective-permute-done | bytes 163872 | tf_op jit(solution)/shard_map/ppermute | solution.py:432
  135.6 2.3 %collective-permute-done.34.refs_3_ = bf16[2,80,512]{2,1,0:T(8,128)(2,1)S(1)} collective-permute-done((bf16[2,80,512]{2,1,0:T(8,128)(2,1)S(1)}, bf16[2,80,512]{2,1,0:T(8,128)(2,1)S(1)}, u32[]{:S(2)}, u32[]{:S(2)}) %collective-permute-start.34) | collective-permute-done | bytes 163872 | tf_op jit(solution)/shard_map/ppermute | solution.py:432
  138.0 2.9 %collective-permute-start.35 = (bf16[80,512]{1,0:T(8,128)(2,1)S(1)}, bf16[80,512]{1,0:T(8,128)(2,1)S(1)}, u32[]{:S(2)}, u32[]{:S(2)}) collective-permute-start(bf16[80,512]{1,0:T(8,128)(2,1)S(1)} %get-tuple-element.55), channel_id=1, source_target_pairs={{0,4},{1,5},{2,6},{3,7},{4,0},{5,1},{6,2},{7,3},{8,12},{9,13},{10,... | collective-permute-start | bytes 245768 | tf_op jit(solution)/shard_map/ppermute | solution.py:432
  142.3 1.9 %collective-permute-done.35.far_ref = bf16[80,512]{1,0:T(8,128)(2,1)S(1)} collective-permute-done((bf16[80,512]{1,0:T(8,128)(2,1)S(1)}, bf16[80,512]{1,0:T(8,128)(2,1)S(1)}, u32[]{:S(2)}, u32[]{:S(2)}) %collective-permute-start.35) | collective-permute-done | bytes 81952 | tf_op jit(solution)/shard_map/ppermute | solution.py:432
  (75 shorter events, 21.9 us)
Async XLA Ops:
  1.6 14.1 %collective-permute-start = (bf16[1,256,256]{2,1,0:T(8,128)(2,1)S(1)}, bf16[1,256,256]{2,1,0:T(8,128)(2,1)S(1)}, u32[]{:S(2)}, u32[]{:S(2)}) collective-permute-start(bf16[1,256,256]{2,1,0:T(8,128)(2,1)S(1)} %get-tuple-element.68), channel_id=1, source_target_pairs={{0,4},{1,5},{2,6},{3,7},{4,0},{5,1},{6,2},{7,3},{8,12},{9,13},{10,... | collective-permute-start | bytes 393224 | tf_op jit(solution)/shard_map/ppermute | solution.py:432
  5.8 11.9 %collective-permute-start.2 = (bf16[1,256,256]{2,1,0:T(8,128)(2,1)S(1)}, bf16[1,256,256]{2,1,0:T(8,128)(2,1)S(1)}, u32[]{:S(2)}, u32[]{:S(2)}) collective-permute-start(bf16[1,256,256]{2,1,0:T(8,128)(2,1)S(1)} %get-tuple-element.67), channel_id=1, source_target_pairs={{0,4},{1,5},{2,6},{3,7},{4,0},{5,1},{6,2},{7,3},{8,12},{9,13},{10,... | collective-permute-start | bytes 393224 | tf_op jit(solution)/shard_map/ppermute | solution.py:432
  15.8 6.4 %collective-permute-start.1 = (bf16[2,256,256]{2,1,0:T(8,128)(2,1)S(1)}, bf16[2,256,256]{2,1,0:T(8,128)(2,1)S(1)}, u32[]{:S(2)}, u32[]{:S(2)}) collective-permute-start(bf16[2,256,256]{2,1,0:T(8,128)(2,1)S(1)} %pad_maximum_fusion.2), channel_id=1, source_target_pairs={{0,2},{1,3},{2,0},{3,1},{4,6},{5,7},{6,4},{7,5},{8,9},{9,8},{10,11... | collective-permute-start | bytes 786440 | tf_op jit(solution)/shard_map/ppermute | solution.py:432
  17.7 9.8 %collective-permute-start.3 = (bf16[2,256,256]{2,1,0:T(8,128)(2,1)S(1)}, bf16[2,256,256]{2,1,0:T(8,128)(2,1)S(1)}, u32[]{:S(2)}, u32[]{:S(2)}) collective-permute-start(bf16[2,256,256]{2,1,0:T(8,128)(2,1)S(1)} %pad_maximum_fusion.3), channel_id=1, source_target_pairs={{0,2},{1,3},{2,0},{3,1},{4,6},{5,7},{6,4},{7,5},{8,9},{9,8},{10,11... | collective-permute-start | bytes 786440 | tf_op jit(solution)/shard_map/ppermute | solution.py:432
  22.3 17.6 %collective-permute-start.6 = (bf16[4,256,256]{2,1,0:T(8,128)(2,1)S(1)}, bf16[4,256,256]{2,1,0:T(8,128)(2,1)S(1)}, u32[]{:S(2)}, u32[]{:S(2)}) collective-permute-start(bf16[4,256,256]{2,1,0:T(8,128)(2,1)S(1)} %pad_maximum_fusion.refs_0_.refs_8_), channel_id=1, source_target_pairs={{0,1},{1,0},{2,3},{3,2},{4,5},{5,4},{6,7},{7,6},{8,10},{9,11},{10,... | collective-permute-start | bytes 1572872 | tf_op jit(solution)/shard_map/ppermute | solution.py:432
  27.6 12.4 %collective-permute-start.7 = (bf16[4,256,256]{2,1,0:T(8,128)(2,1)S(1)}, bf16[4,256,256]{2,1,0:T(8,128)(2,1)S(1)}, u32[]{:S(2)}, u32[]{:S(2)}) collective-permute-start(bf16[4,256,256]{2,1,0:T(8,128)(2,1)S(1)} %pad_maximum_fusion.1.refs_1_.refs_9_), channel_id=1, source_target_pairs={{0,1},{1,0},{2,3},{3,2},{4,5},{5,4},{6,7},{7,6},{8,10},{9,11},{10,... | collective-permute-start | bytes 1572872 | tf_op jit(solution)/shard_map/ppermute | solution.py:432
  30.7 25.6 %collective-permute-start.4 = (bf16[4,256,256]{2,1,0:T(8,128)(2,1)S(1)}, bf16[4,256,256]{2,1,0:T(8,128)(2,1)S(1)}, u32[]{:S(2)}, u32[]{:S(2)}) collective-permute-start(bf16[4,256,256]{2,1,0:T(8,128)(2,1)S(1)} %pad_maximum_fusion.refs_0_.refs_8_), channel_id=1, source_target_pairs={{0,8},{1,9},{2,10},{3,11},{4,12},{5,13},{6,14},{7,15},{8,0},{9,1},... | collective-permute-start | bytes 1572872 | tf_op jit(solution)/shard_map/ppermute | solution.py:432
  30.7 25.6 %collective-permute-start.5 = (bf16[4,256,256]{2,1,0:T(8,128)(2,1)S(1)}, bf16[4,256,256]{2,1,0:T(8,128)(2,1)S(1)}, u32[]{:S(2)}, u32[]{:S(2)}) collective-permute-start(bf16[4,256,256]{2,1,0:T(8,128)(2,1)S(1)} %pad_maximum_fusion.1.refs_1_.refs_9_), channel_id=1, source_target_pairs={{0,8},{1,9},{2,10},{3,11},{4,12},{5,13},{6,14},{7,15},{8,0},{9,1},... | collective-permute-start | bytes 1572872 | tf_op jit(solution)/shard_map/ppermute | solution.py:432
  39.9 21.5 %collective-permute-start.8 = (bf16[4,256,256]{2,1,0:T(8,128)(2,1)S(1)}, bf16[4,256,256]{2,1,0:T(8,128)(2,1)S(1)}, u32[]{:S(2)}, u32[]{:S(2)}) collective-permute-start(bf16[4,256,256]{2,1,0:T(8,128)(2,1)S(1)} %collective-permute-done.6.refs_4_), channel_id=1, source_target_pairs={{0,8},{1,9},{2,10},{3,11},{4,12},{5,13},{6,14},{7,15},{8,0},{9,1},... | collective-permute-start | bytes 1572872 | tf_op jit(solution)/shard_map/ppermute | solution.py:432
  40.0 21.4 %collective-permute-start.9 = (bf16[4,256,256]{2,1,0:T(8,128)(2,1)S(1)}, bf16[4,256,256]{2,1,0:T(8,128)(2,1)S(1)}, u32[]{:S(2)}, u32[]{:S(2)}) collective-permute-start(bf16[4,256,256]{2,1,0:T(8,128)(2,1)S(1)} %collective-permute-done.7.refs_5_), channel_id=1, source_target_pairs={{0,8},{1,9},{2,10},{3,11},{4,12},{5,13},{6,14},{7,15},{8,0},{9,1},... | collective-permute-start | bytes 1572872 | tf_op jit(solution)/shard_map/ppermute | solution.py:432
  71.5 9.2 %collective-permute-start.14 = (bf16[8,128,256]{2,1,0:T(8,128)(2,1)S(1)}, bf16[8,128,256]{2,1,0:T(8,128)(2,1)S(1)}, u32[]{:S(2)}, u32[]{:S(2)}) collective-permute-start(bf16[8,128,256]{2,1,0:T(8,128)(2,1)S(1)} %get-tuple-element.45), channel_id=1, source_target_pairs={{0,1},{1,0},{2,3},{3,2},{4,5},{5,4},{6,7},{7,6},{8,24},{9,25},{10,... | collective-permute-start | bytes 1572872 | tf_op jit(solution)/shard_map/ppermute | solution.py:432
  71.6 14.8 %collective-permute-start.18 = (bf16[8,128,256]{2,1,0:T(8,128)(2,1)S(1)}, bf16[8,128,256]{2,1,0:T(8,128)(2,1)S(1)}, u32[]{:S(2)}, u32[]{:S(2)}) collective-permute-start(bf16[8,128,256]{2,1,0:T(8,128)(2,1)S(1)} %get-tuple-element.47), channel_id=1, source_target_pairs={{0,1},{1,0},{2,3},{3,2},{4,5},{5,4},{6,7},{7,6},{8,24},{9,25},{10,... | collective-permute-start | bytes 1572872 | tf_op jit(solution)/shard_map/ppermute | solution.py:432
  80.8 10.8 %collective-permute-start.15 = (bf16[4,128,256]{2,1,0:T(8,128)(2,1)S(1)}, bf16[4,128,256]{2,1,0:T(8,128)(2,1)S(1)}, u32[]{:S(2)}, u32[]{:S(2)}) collective-permute-start(bf16[4,128,256]{2,1,0:T(8,128)(2,1)S(1)} %add_convert_fusion.1), channel_id=1, source_target_pairs={{0,16},{1,17},{2,18},{3,19},{4,20},{5,21},{6,22},{7,23},{8,10},{9,... | collective-permute-start | bytes 786440 | tf_op jit(solution)/shard_map/ppermute | solution.py:432
  86.4 6.4 %collective-permute-start.19 = (bf16[4,128,256]{2,1,0:T(8,128)(2,1)S(1)}, bf16[4,128,256]{2,1,0:T(8,128)(2,1)S(1)}, u32[]{:S(2)}, u32[]{:S(2)}) collective-permute-start(bf16[4,128,256]{2,1,0:T(8,128)(2,1)S(1)} %add_convert_fusion), channel_id=1, source_target_pairs={{0,16},{1,17},{2,18},{3,19},{4,20},{5,21},{6,22},{7,23},{8,10},{9,... | collective-permute-start | bytes 786440 | tf_op jit(solution)/shard_map/ppermute | solution.py:432
  88.0 27.2 %collective-permute-start.25 = (bf16[1,64,512]{2,1,0:T(8,128)(2,1)S(1)}, bf16[1,64,512]{2,1,0:T(8,128)(2,1)S(1)}, u32[]{:S(2)}, u32[]{:S(2)}) collective-permute-start(bf16[1,64,512]{2,1,0:T(8,128)(2,1)S(1)} %get-tuple-element.65), channel_id=1, source_target_pairs={{0,1},{1,0},{2,3},{3,2},{4,5},{5,4},{6,7},{7,6},{8,9},{9,8},{10,11... | collective-permute-start | bytes 196616 | tf_op jit(solution)/shard_map/ppermute | solution.py:432
  88.6 27.9 %collective-permute-start.26 = (bf16[1,64,512]{2,1,0:T(8,128)(2,1)S(1)}, bf16[1,64,512]{2,1,0:T(8,128)(2,1)S(1)}, u32[]{:S(2)}, u32[]{:S(2)}) collective-permute-start(bf16[1,64,512]{2,1,0:T(8,128)(2,1)S(1)} %get-tuple-element.64), channel_id=1, source_target_pairs={{0,2},{1,3},{2,0},{3,1},{4,6},{5,7},{6,4},{7,5},{8,10},{9,11},{10,... | collective-permute-start | bytes 196616 | tf_op jit(solution)/shard_map/ppermute | solution.py:432
  88.6 27.9 %collective-permute-start.27 = (bf16[1,64,512]{2,1,0:T(8,128)(2,1)S(1)}, bf16[1,64,512]{2,1,0:T(8,128)(2,1)S(1)}, u32[]{:S(2)}, u32[]{:S(2)}) collective-permute-start(bf16[1,64,512]{2,1,0:T(8,128)(2,1)S(1)} %get-tuple-element.63), channel_id=1, source_target_pairs={{0,3},{1,2},{2,1},{3,0},{4,7},{5,6},{6,5},{7,4},{8,11},{9,10},{10,... | collective-permute-start | bytes 196616 | tf_op jit(solution)/shard_map/ppermute | solution.py:432
  91.6 25.9 %collective-permute-start.28 = (bf16[1,64,512]{2,1,0:T(8,128)(2,1)S(1)}, bf16[1,64,512]{2,1,0:T(8,128)(2,1)S(1)}, u32[]{:S(2)}, u32[]{:S(2)}) collective-permute-start(bf16[1,64,512]{2,1,0:T(8,128)(2,1)S(1)} %get-tuple-element.62), channel_id=1, source_target_pairs={{0,4},{1,5},{2,6},{3,7},{4,0},{5,1},{6,2},{7,3},{8,12},{9,13},{10,... | collective-permute-start | bytes 196616 | tf_op jit(solution)/shard_map/ppermute | solution.py:432
  92.9 5.5 %collective-permute-start.16 = (bf16[2,128,256]{2,1,0:T(8,128)(2,1)S(1)}, bf16[2,128,256]{2,1,0:T(8,128)(2,1)S(1)}, u32[]{:S(2)}, u32[]{:S(2)}) collective-permute-start(bf16[2,128,256]{2,1,0:T(8,128)(2,1)S(1)} %add_convert_fusion.3), channel_id=1, source_target_pairs={{0,2},{1,3},{2,0},{3,1},{4,6},{5,7},{6,4},{7,5},{8,9},{9,8},{10,11... | collective-permute-start | bytes 393224 | tf_op jit(solution)/shard_map/ppermute | solution.py:432
  98.3 5.0 %collective-permute-start.20 = (bf16[2,128,256]{2,1,0:T(8,128)(2,1)S(1)}, bf16[2,128,256]{2,1,0:T(8,128)(2,1)S(1)}, u32[]{:S(2)}, u32[]{:S(2)}) collective-permute-start(bf16[2,128,256]{2,1,0:T(8,128)(2,1)S(1)} %add_convert_fusion.2), channel_id=1, source_target_pairs={{0,2},{1,3},{2,0},{3,1},{4,6},{5,7},{6,4},{7,5},{8,9},{9,8},{10,11... | collective-permute-start | bytes 393224 | tf_op jit(solution)/shard_map/ppermute | solution.py:432
  103.3 6.3 %collective-permute-start.17 = (bf16[1,128,256]{2,1,0:T(8,128)(2,1)S(1)}, bf16[1,128,256]{2,1,0:T(8,128)(2,1)S(1)}, u32[]{:S(2)}, u32[]{:S(2)}) collective-permute-start(bf16[1,128,256]{2,1,0:T(8,128)(2,1)S(1)} %add_convert_fusion.7), channel_id=1, source_target_pairs={{0,4},{1,5},{2,6},{3,7},{4,0},{5,1},{6,2},{7,3},{8,12},{9,13},{10,... | collective-permute-start | bytes 196616 | tf_op jit(solution)/shard_map/ppermute | solution.py:432
  109.6 5.6 %collective-permute-start.21 = (bf16[1,128,256]{2,1,0:T(8,128)(2,1)S(1)}, bf16[1,128,256]{2,1,0:T(8,128)(2,1)S(1)}, u32[]{:S(2)}, u32[]{:S(2)}) collective-permute-start(bf16[1,128,256]{2,1,0:T(8,128)(2,1)S(1)} %add_convert_fusion.5), channel_id=1, source_target_pairs={{0,4},{1,5},{2,6},{3,7},{4,0},{5,1},{6,2},{7,3},{8,12},{9,13},{10,... | collective-permute-start | bytes 196616 | tf_op jit(solution)/shard_map/ppermute | solution.py:432
  115.2 6.1 %collective-permute-start.29 = (bf16[1,64,512]{2,1,0:T(8,128)(2,1)S(1)}, bf16[1,64,512]{2,1,0:T(8,128)(2,1)S(1)}, u32[]{:S(2)}, u32[]{:S(2)}) collective-permute-start(bf16[1,64,512]{2,1,0:T(8,128)(2,1)S(1)} %get-tuple-element.61), channel_id=1, source_target_pairs={{0,5},{1,4},{2,7},{3,6},{4,1},{5,0},{6,3},{7,2},{8,13},{9,12},{10,... | collective-permute-start | bytes 196616 | tf_op jit(solution)/shard_map/ppermute | solution.py:432
  115.3 12.9 %collective-permute-start.22 = (bf16[1,128,512]{2,1,0:T(8,128)(2,1)S(1)}, bf16[1,128,512]{2,1,0:T(8,128)(2,1)S(1)}, u32[]{:S(2)}, u32[]{:S(2)}) collective-permute-start(bf16[1,128,512]{2,1,0:T(8,128)(2,1)S(1)} %pad_maximum_fusion.4.refs_0_), channel_id=1, source_target_pairs={{0,16},{1,17},{2,18},{3,19},{4,20},{5,21},{6,22},{7,23},{8,24},{9,... | collective-permute-start | bytes 393224 | tf_op jit(solution)/shard_map/ppermute | solution.py:432
  116.5 11.7 %collective-permute-start.23 = (bf16[1,128,512]{2,1,0:T(8,128)(2,1)S(1)}, bf16[1,128,512]{2,1,0:T(8,128)(2,1)S(1)}, u32[]{:S(2)}, u32[]{:S(2)}) collective-permute-start(bf16[1,128,512]{2,1,0:T(8,128)(2,1)S(1)} %pad_maximum_fusion.4.refs_0_), channel_id=1, source_target_pairs={{0,8},{1,9},{2,10},{3,11},{4,12},{5,13},{6,14},{7,15},{8,0},{9,1},... | collective-permute-start | bytes 393224 | tf_op jit(solution)/shard_map/ppermute | solution.py:432
  116.5 11.7 %collective-permute-start.24 = (bf16[1,128,512]{2,1,0:T(8,128)(2,1)S(1)}, bf16[1,128,512]{2,1,0:T(8,128)(2,1)S(1)}, u32[]{:S(2)}, u32[]{:S(2)}) collective-permute-start(bf16[1,128,512]{2,1,0:T(8,128)(2,1)S(1)} %pad_maximum_fusion.4.refs_0_), channel_id=1, source_target_pairs={{0,24},{1,25},{2,26},{3,27},{4,28},{5,29},{6,30},{7,31},{8,16},{9,... | collective-permute-start | bytes 393224 | tf_op jit(solution)/shard_map/ppermute | solution.py:432
  117.5 6.1 %collective-permute-start.30 = (bf16[1,64,512]{2,1,0:T(8,128)(2,1)S(1)}, bf16[1,64,512]{2,1,0:T(8,128)(2,1)S(1)}, u32[]{:S(2)}, u32[]{:S(2)}) collective-permute-start(bf16[1,64,512]{2,1,0:T(8,128)(2,1)S(1)} %get-tuple-element.60), channel_id=1, source_target_pairs={{0,6},{1,7},{2,4},{3,5},{4,2},{5,3},{6,0},{7,1},{8,14},{9,15},{10,... | collective-permute-start | bytes 196616 | tf_op jit(solution)/shard_map/ppermute | solution.py:432
  121.2 7.0 %collective-permute-start.31 = (bf16[1,64,512]{2,1,0:T(8,128)(2,1)S(1)}, bf16[1,64,512]{2,1,0:T(8,128)(2,1)S(1)}, u32[]{:S(2)}, u32[]{:S(2)}) collective-permute-start(bf16[1,64,512]{2,1,0:T(8,128)(2,1)S(1)} %get-tuple-element.59), channel_id=1, source_target_pairs={{0,7},{1,6},{2,5},{3,4},{4,3},{5,2},{6,1},{7,0},{8,15},{9,14},{10,... | collective-permute-start | bytes 196616 | tf_op jit(solution)/shard_map/ppermute | solution.py:432
  129.2 6.3 %collective-permute-start.32 = (bf16[2,80,512]{2,1,0:T(8,128)(2,1)S(1)}, bf16[2,80,512]{2,1,0:T(8,128)(2,1)S(1)}, u32[]{:S(2)}, u32[]{:S(2)}) collective-permute-start(bf16[2,80,512]{2,1,0:T(8,128)(2,1)S(1)} %get-tuple-element.51), channel_id=1, source_target_pairs={{0,1},{1,0},{2,3},{3,2},{4,5},{5,4},{6,7},{7,6},{8,9},{9,8},{10,11... | collective-permute-start | bytes 491528 | tf_op jit(solution)/shard_map/ppermute | solution.py:432
  129.3 6.3 %collective-permute-start.33 = (bf16[2,80,512]{2,1,0:T(8,128)(2,1)S(1)}, bf16[2,80,512]{2,1,0:T(8,128)(2,1)S(1)}, u32[]{:S(2)}, u32[]{:S(2)}) collective-permute-start(bf16[2,80,512]{2,1,0:T(8,128)(2,1)S(1)} %get-tuple-element.52), channel_id=1, source_target_pairs={{0,2},{1,3},{2,0},{3,1},{4,6},{5,7},{6,4},{7,5},{8,10},{9,11},{10,... | collective-permute-start | bytes 491528 | tf_op jit(solution)/shard_map/ppermute | solution.py:432
  129.4 8.4 %collective-permute-start.34 = (bf16[2,80,512]{2,1,0:T(8,128)(2,1)S(1)}, bf16[2,80,512]{2,1,0:T(8,128)(2,1)S(1)}, u32[]{:S(2)}, u32[]{:S(2)}) collective-permute-start(bf16[2,80,512]{2,1,0:T(8,128)(2,1)S(1)} %get-tuple-element.53), channel_id=1, source_target_pairs={{0,3},{1,2},{2,1},{3,0},{4,7},{5,6},{6,5},{7,4},{8,11},{9,10},{10,... | collective-permute-start | bytes 491528 | tf_op jit(solution)/shard_map/ppermute | solution.py:432
  138.0 6.3 %collective-permute-start.35 = (bf16[80,512]{1,0:T(8,128)(2,1)S(1)}, bf16[80,512]{1,0:T(8,128)(2,1)S(1)}, u32[]{:S(2)}, u32[]{:S(2)}) collective-permute-start(bf16[80,512]{1,0:T(8,128)(2,1)S(1)} %get-tuple-element.55), channel_id=1, source_target_pairs={{0,4},{1,5},{2,6},{3,7},{4,0},{5,1},{6,2},{7,3},{8,12},{9,13},{10,... | collective-permute-start | bytes 245768 | tf_op jit(solution)/shard_map/ppermute | solution.py:432
  (6 other events, 153.7 us)

commit v3 on v2

--- a/solution.py
+++ b/solution.py
@@ -27,6 +27,7 @@
 
 
 SLOTS = 4
+FOOT = 8
 
 
 def features_kernel(start, last, tab_ref, hidden_ref, roll_ref, table_ref, *refs):
@@ -296,7 +297,7 @@
 def split(value, wide):
     first = value.astype(BF16).astype(F32)
     second = (value - first).astype(BF16).astype(F32)
-    line = lax.broadcasted_iota(I32, (16, wide), 0)
+    line = lax.broadcasted_iota(I32, (FOOT, wide), 0)
     third = jnp.where(line == 2, value - first - second, 0.0)
     return jnp.where(line == 0, first, jnp.where(line == 1, second, third)).astype(BF16)
 
@@ -323,7 +324,7 @@
     quarter, actions = lines[0].shape[1:]
     rows = rolls[0].shape[1]
     full = lambda shape: pl.BlockSpec(shape, lambda i, t: (0,) * len(shape))
-    shape = (2, rows + 16, actions)
+    shape = (2, rows + FOOT, actions)
     return pl.pallas_call(
         functools.partial(share_kernel, len(rolls)),
         grid_spec=pltpu.PrefetchScalarGridSpec(
@@ -341,7 +342,7 @@
 
 def join_kernel(*refs):
     parts, (stay_ref, send_ref) = refs[:-2], refs[-2:]
-    rows = stay_ref.shape[0] - 16
+    rows = stay_ref.shape[0] - FOOT
     for k, out_ref in enumerate((stay_ref, send_ref)):
         total = parts[0][k].astype(F32)
         for ref in parts[1:]:
@@ -349,7 +350,7 @@
         out_ref[:rows] = total[:rows].astype(out_ref.dtype)
         square = jnp.sum(total[rows:], axis=0, keepdims=True)
         if k == 0:
-            out_ref[rows:] = jnp.broadcast_to(square, (16, square.shape[1]))
+            out_ref[rows:] = jnp.broadcast_to(square, (FOOT, square.shape[1]))
         else:
             out_ref[rows:] = split(square, square.shape[1])
 
@@ -455,7 +456,7 @@
         other_came.append(swap(came[c], CORE))
 
     so_far, start, tall = (), 0, traj_hidden.shape[0]
-    for rows in (tall * 3 // 8, tall * 3 // 8, tall // 4):
+    for rows in (tall // 2, tall // 4, tall // 4):
         so_far = features_call(
             shard, tab, start, rows, tuple(so_far), traj_hidden, roll_hidden, station_table,
             traj_tokens.reshape(1, -1), roll_tokens.reshape(1, -1), norm_gain.reshape(1, -1),

time: 146 us -> 144 us (0.986)
  no operation moved by 1% of the time
where the time goes in v3:
time: 144 us; the launch traced here: 143 us
  waiting for transfers between devices  64.4 us (45%)
  Pallas kernels  42.9 us (30%)
  starting transfers between devices  32.9 us (23%)
  local copies, waits for them, and re-layouts  1.73 us (1%)
    ppermute x36, waiting for transfers between devices, swap(): lax.ppermute(value, AXES, [(i, i ^ masks[i // shards & 1]) for i in range...  64.4 us
    ppermute x36, starting transfers between devices, swap(): lax.ppermute(value, AXES, [(i, i ^ masks[i // shards & 1]) for i in range...  32.9 us
    pallas_call x3, Pallas kernels, features_call(): pl.pallas_call(functools.partial(features_kernel, start, last), in_specs=...  23.1 us
    pallas_call x4, Pallas kernels, grad_call(): pl.pallas_call(functools.partial(grad_kernel, each), grid_spec=pltpu.Pref...  8.14 us
    pallas_call x3, Pallas kernels, logits_call(): pl.pallas_call(functools.partial(logits_kernel, pieces, acc is not None,...  7.77 us
  transfers between devices with their start and end apart: 36, of which 17 were waited for; matrix products, arithmetic and copies ran while one was open for 1% of the time, Pallas kernels for 25%

profile of v3, /device:TPU:0, one launch (start us, length us, event | category | flops | bytes accessed | tf_op | source)
XLA Modules:
  0.0 143.5 jit_solution(17109885366596164033)
XLA Ops:
  1.6 4.1 %collective-permute-start = (bf16[1,256,256]{2,1,0:T(8,128)(2,1)S(1)}, bf16[1,256,256]{2,1,0:T(8,128)(2,1)S(1)}, u32[]{:S(2)}, u32[]{:S(2)}) collective-permute-start(bf16[1,256,256]{2,1,0:T(8,128)(2,1)S(1)} %get-tuple-element.68), channel_id=1, source_target_pairs={{0,4},{1,5},{2,6},{3,7},{4,0},{5,1},{6,2},{7,3},{8,12},{9,13},{10,... | collective-permute-start | bytes 393224 | tf_op jit(solution)/shard_map/ppermute | solution.py:433
  5.8 9.9 %collective-permute-done = bf16[1,256,256]{2,1,0:T(8,128)(2,1)S(1)} collective-permute-done((bf16[1,256,256]{2,1,0:T(8,128)(2,1)S(1)}, bf16[1,256,256]{2,1,0:T(8,128)(2,1)S(1)}, u32[]{:S(2)}, u32[]{:S(2)}) %collective-permute-start) | collective-permute-done | bytes 131104 | tf_op jit(solution)/shard_map/ppermute | solution.py:433
  15.8 1.8 %collective-permute-done.2 = bf16[1,256,256]{2,1,0:T(8,128)(2,1)S(1)} collective-permute-done((bf16[1,256,256]{2,1,0:T(8,128)(2,1)S(1)}, bf16[1,256,256]{2,1,0:T(8,128)(2,1)S(1)}, u32[]{:S(2)}, u32[]{:S(2)}) %collective-permute-start.2) | collective-permute-done | bytes 131104 | tf_op jit(solution)/shard_map/ppermute | solution.py:433
  18.5 3.7 %collective-permute-done.1 = bf16[2,256,256]{2,1,0:T(8,128)(2,1)S(1)} collective-permute-done((bf16[2,256,256]{2,1,0:T(8,128)(2,1)S(1)}, bf16[2,256,256]{2,1,0:T(8,128)(2,1)S(1)}, u32[]{:S(2)}, u32[]{:S(2)}) %collective-permute-start.1) | collective-permute-done | bytes 262176 | tf_op jit(solution)/shard_map/ppermute | solution.py:433
  22.3 2.2 %collective-permute-start.6 = (bf16[4,256,256]{2,1,0:T(8,128)(2,1)S(1)}, bf16[4,256,256]{2,1,0:T(8,128)(2,1)S(1)}, u32[]{:S(2)}, u32[]{:S(2)}) collective-permute-start(bf16[4,256,256]{2,1,0:T(8,128)(2,1)S(1)} %pad_maximum_fusion.refs_0_.refs_8_), channel_id=1, source_target_pairs={{0,1},{1,0},{2,3},{3,2},{4,5},{5,4},{6,7},{7,6},{8,10},{9,11},{10,... | collective-permute-start | bytes 1572872 | tf_op jit(solution)/shard_map/ppermute | solution.py:433
  24.4 3.1 %collective-permute-done.3 = bf16[2,256,256]{2,1,0:T(8,128)(2,1)S(1)} collective-permute-done((bf16[2,256,256]{2,1,0:T(8,128)(2,1)S(1)}, bf16[2,256,256]{2,1,0:T(8,128)(2,1)S(1)}, u32[]{:S(2)}, u32[]{:S(2)}) %collective-permute-start.3) | collective-permute-done | bytes 262176 | tf_op jit(solution)/shard_map/ppermute | solution.py:433
  27.6 2.4 %collective-permute-start.7 = (bf16[4,256,256]{2,1,0:T(8,128)(2,1)S(1)}, bf16[4,256,256]{2,1,0:T(8,128)(2,1)S(1)}, u32[]{:S(2)}, u32[]{:S(2)}) collective-permute-start(bf16[4,256,256]{2,1,0:T(8,128)(2,1)S(1)} %pad_maximum_fusion.1.refs_1_.refs_9_), channel_id=1, source_target_pairs={{0,1},{1,0},{2,3},{3,2},{4,5},{5,4},{6,7},{7,6},{8,10},{9,11},{10,... | collective-permute-start | bytes 1572872 | tf_op jit(solution)/shard_map/ppermute | solution.py:433
  31.2 9.1 %features.3 = (bf16[16,1024,256]{2,1,0:T(8,128)(2,1)S(1)}, bf16[32,128,1024]{2,1,0:T(8,128)(2,1)S(1)}) custom-call(s32[53]{0:T(128)S(1)} %dynamic-slice_bitcast_fusion.2.tab_ref, bf16[1024,4096]{1,0:T(8,128)(2,1)} %hidden_ref.5, bf16[64,4096]{1,0:T(8,128)(2,1)} %roll_ref.5, bf16[512,4096]{1,0:T(8,128)(2,1)} %table_ref.5, s32[1,1024]{1,0:T(1,128)} %bitcast.18, ...), custom_call_target="tpu_custom_call" | custom-call | flops 4294967296 | bytes 16777216 | tf_op jit(solution)/shard_map/features/pallas_call | solution.py:140
  40.9 6.7 %features.4 = (bf16[16,1024,256]{2,1,0:T(8,128)(2,1)S(1)}, bf16[32,128,1024]{2,1,0:T(8,128)(2,1)S(1)}) custom-call(s32[53]{0:T(128)S(1)} %dynamic-slice_bitcast_fusion.2.tab_ref, bf16[1024,4096]{1,0:T(8,128)(2,1)} %hidden_ref.5, bf16[64,4096]{1,0:T(8,128)(2,1)} %roll_ref.5, ...), custom_call_target="tpu_custom_call", output_to_operand_aliasing={{0}: (10, {}), {1}: (11, {})} | custom-call | flops 2147483648 | bytes 8388608 | tf_op jit(solution)/shard_map/features/pallas_call | solution.py:140
  47.6 7.4 %features.5 = (bf16[16,1024,256]{2,1,0:T(8,128)(2,1)S(1)}, bf16[32,128,1024]{2,1,0:T(8,128)(2,1)S(1)}, bf16[16,64,256]{2,1,0:T(8,128)(2,1)S(1)}, bf16[8,64,512]{...) custom-call(s32[53]{0:T(128)S(1)} %dynamic-slice_bitcast_fusion.2.ta, ...), custom_call_target="tpu_custom_call", output_to_operand_aliasing={{0}: (10, {}), {1}: (11, {})} | custom-call | flops 2147483648 | bytes 8388608 | tf_op jit(solution)/shard_map/features/pallas_call | solution.py:140
  55.0 3.1 %logits.3.refs_6_ = f32[1024,512]{1,0:T(8,128)S(1)} custom-call(s32[53]{0:T(128)S(1)} %dynamic-slice_bitcast_fusion.2.tab_ref, bf16[16,1024,256]{2,1,0:T(8,128)(2,1)S(1)} %get-tuple-element.36.refs_0_.refs_1_.refs_2_.refs_3_.refs_4_.refs_5_.refs_6_.refs_7_, ...), custom_call_target="tpu_custom_call" | custom-call | flops 2147483648 | bytes 4194304 | tf_op jit(solution)/shard_map/logits/pallas_call | solution.py:219
  58.0 2.0 %logits.4.refs_6_ = f32[1024,512]{1,0:T(8,128)S(1)} custom-call(s32[53]{0:T(128)S(1)} %dynamic-slice_bitcast_fusion.2.tab_ref, bf16[16,1024,256]{2,1,0:T(8,128)(2,1)S(1)} %get-tuple-element.36.refs_0_.refs_1_.refs_2_.refs_3_.refs_4_.refs_5_.refs_6_.refs_7_, ...), custom_call_target="tpu_custom_call" | custom-call | flops 1073741824 | bytes 2097152 | tf_op jit(solution)/shard_map/logits/pallas_call | solution.py:219
  60.1 2.7 %logits.5.scores_ref = bf16[1024,512]{1,0:T(8,128)(2,1)S(1)} custom-call(s32[53]{0:T(128)S(1)} %dynamic-slice_bitcast_fusion.2.tab_ref, bf16[16,1024,256]{2,1,0:T(8,128)(2,1)S(1)} %get-tuple-element.36.refs_0_.refs_1_.refs_2_.refs_3_.refs_4_.refs_5_.refs_6_.refs_7_, ...), custom_call_target="tpu_custom_call" | custom-call | flops 1073741824 | bytes 2097152 | tf_op jit(solution)/shard_map/logits/pallas_call | solution.py:219
  62.8 2.0 %grad.6 = (bf16[8,128,256]{2,1,0:T(8,128)(2,1)S(1)}, bf16[8,128,256]{2,1,0:T(8,128)(2,1)S(1)}) custom-call(s32[53]{0:T(128)S(1)} %dynamic-slice_bitcast_fusion.2.tab_ref, bf16[1024,512]{1,0:T(8,128)(2,1)S(1)} %logits.5.scores_ref, bf16[32,128,1024]{2,1,0:T(8,128)(2,1)S(1)} %get-tuple-element.39.refs_0_.refs_1_.refs_2_.refs_3_, ...), custom_call_target="tpu_custom_call" | custom-call | flops 1073741824 | bytes 2097152 | tf_op jit(solution)/shard_map/grad/pallas_call | solution.py:250
  65.3 2.0 %grad.4 = (bf16[8,128,256]{2,1,0:T(8,128)(2,1)S(1)}, bf16[8,128,256]{2,1,0:T(8,128)(2,1)S(1)}) custom-call(s32[53]{0:T(128)S(1)} %dynamic-slice_bitcast_fusion.2.tab_ref, bf16[1024,512]{1,0:T(8,128)(2,1)S(1)} %logits.5.scores_ref, bf16[32,128,1024]{2,1,0:T(8,128)(2,1)S(1)} %get-tuple-element.39.refs_0_.refs_1_.refs_2_.refs_3_, ...), custom_call_target="tpu_custom_call" | custom-call | flops 1073741824 | bytes 2097152 | tf_op jit(solution)/shard_map/grad/pallas_call | solution.py:250
  67.9 2.0 %grad.7 = (bf16[8,128,256]{2,1,0:T(8,128)(2,1)S(1)}, bf16[8,128,256]{2,1,0:T(8,128)(2,1)S(1)}) custom-call(s32[53]{0:T(128)S(1)} %dynamic-slice_bitcast_fusion.2.tab_ref, bf16[1024,512]{1,0:T(8,128)(2,1)S(1)} %logits.5.scores_ref, bf16[32,128,1024]{2,1,0:T(8,128)(2,1)S(1)} %get-tuple-element.39.refs_0_.refs_1_.refs_2_.refs_3_, ...), custom_call_target="tpu_custom_call" | custom-call | flops 1073741824 | bytes 2097152 | tf_op jit(solution)/shard_map/grad/pallas_call | solution.py:250
  70.0 2.0 %collective-permute-start.18 = (bf16[8,128,256]{2,1,0:T(8,128)(2,1)S(1)}, bf16[8,128,256]{2,1,0:T(8,128)(2,1)S(1)}, u32[]{:S(2)}, u32[]{:S(2)}) collective-permute-start(bf16[8,128,256]{2,1,0:T(8,128)(2,1)S(1)} %get-tuple-element.47), channel_id=1, source_target_pairs={{0,1},{1,0},{2,3},{3,2},{4,5},{5,4},{6,7},{7,6},{8,24},{9,25},{10,... | collective-permute-start | bytes 1572872 | tf_op jit(solution)/shard_map/ppermute | solution.py:433
  72.0 2.2 %grad.5 = (f32[8,128,256]{2,1,0:T(8,128)S(1)}, f32[8,128,256]{2,1,0:T(8,128)S(1)}) custom-call(s32[53]{0:T(128)S(1)} %dynamic-slice_bitcast_fusion.2.tab_ref, bf16[1024,512]{1,0:T(8,128)(2,1)S(1)} %logits.5.scores_ref, bf16[32,128,1024]{2,1,0:T(8,128)(2,1)S(1)} %get-tuple-element.39.refs_0_.refs_1_.refs_2_.refs_3_, ...), custom_call_target="tpu_custom_call" | custom-call | flops 1073741824 | bytes 2097152 | tf_op jit(solution)/shard_map/grad/pallas_call | solution.py:250
  74.2 4.9 %collective-permute-done.14 = bf16[8,128,256]{2,1,0:T(8,128)(2,1)S(1)} collective-permute-done((bf16[8,128,256]{2,1,0:T(8,128)(2,1)S(1)}, bf16[8,128,256]{2,1,0:T(8,128)(2,1)S(1)}, u32[]{:S(2)}, u32[]{:S(2)}) %collective-permute-start.14) | collective-permute-done | bytes 524320 | tf_op jit(solution)/shard_map/ppermute | solution.py:433
  80.8 4.0 %collective-permute-done.18 = bf16[8,128,256]{2,1,0:T(8,128)(2,1)S(1)} collective-permute-done((bf16[8,128,256]{2,1,0:T(8,128)(2,1)S(1)}, bf16[8,128,256]{2,1,0:T(8,128)(2,1)S(1)}, u32[]{:S(2)}, u32[]{:S(2)}) %collective-permute-start.18) | collective-permute-done | bytes 524320 | tf_op jit(solution)/shard_map/ppermute | solution.py:433
  87.1 3.0 %collective-permute-start.27 = (bf16[1,64,512]{2,1,0:T(8,128)(2,1)S(1)}, bf16[1,64,512]{2,1,0:T(8,128)(2,1)S(1)}, u32[]{:S(2)}, u32[]{:S(2)}) collective-permute-start(bf16[1,64,512]{2,1,0:T(8,128)(2,1)S(1)} %get-tuple-element.63), channel_id=1, source_target_pairs={{0,3},{1,2},{2,1},{3,0},{4,7},{5,6},{6,5},{7,4},{8,11},{9,10},{10,... | collective-permute-start | bytes 196616 | tf_op jit(solution)/shard_map/ppermute | solution.py:433
  91.3 5.4 %collective-permute-done.16 = bf16[2,128,256]{2,1,0:T(8,128)(2,1)S(1)} collective-permute-done((bf16[2,128,256]{2,1,0:T(8,128)(2,1)S(1)}, bf16[2,128,256]{2,1,0:T(8,128)(2,1)S(1)}, u32[]{:S(2)}, u32[]{:S(2)}) %collective-permute-start.16) | collective-permute-done | bytes 131104 | tf_op jit(solution)/shard_map/ppermute | solution.py:433
  96.8 4.9 %collective-permute-done.20 = bf16[2,128,256]{2,1,0:T(8,128)(2,1)S(1)} collective-permute-done((bf16[2,128,256]{2,1,0:T(8,128)(2,1)S(1)}, bf16[2,128,256]{2,1,0:T(8,128)(2,1)S(1)}, u32[]{:S(2)}, u32[]{:S(2)}) %collective-permute-start.20) | collective-permute-done | bytes 131104 | tf_op jit(solution)/shard_map/ppermute | solution.py:433
  103.0 5.0 %collective-permute-done.17 = bf16[1,128,256]{2,1,0:T(8,128)(2,1)S(1)} collective-permute-done((bf16[1,128,256]{2,1,0:T(8,128)(2,1)S(1)}, bf16[1,128,256]{2,1,0:T(8,128)(2,1)S(1)}, u32[]{:S(2)}, u32[]{:S(2)}) %collective-permute-start.17) | collective-permute-done | bytes 65568 | tf_op jit(solution)/shard_map/ppermute | solution.py:433
  108.8 4.8 %collective-permute-done.21 = bf16[1,128,256]{2,1,0:T(8,128)(2,1)S(1)} collective-permute-done((bf16[1,128,256]{2,1,0:T(8,128)(2,1)S(1)}, bf16[1,128,256]{2,1,0:T(8,128)(2,1)S(1)}, u32[]{:S(2)}, u32[]{:S(2)}) %collective-permute-start.21) | collective-permute-done | bytes 65568 | tf_op jit(solution)/shard_map/ppermute | solution.py:433
  116.5 3.2 %collective-permute-done.29.refs_9_ = bf16[1,64,512]{2,1,0:T(8,128)(2,1)S(1)} collective-permute-done((bf16[1,64,512]{2,1,0:T(8,128)(2,1)S(1)}, bf16[1,64,512]{2,1,0:T(8,128)(2,1)S(1)}, u32[]{:S(2)}, u32[]{:S(2)}) %collective-permute-start.29) | collective-permute-done | bytes 65568 | tf_op jit(solution)/shard_map/ppermute | solution.py:433
  122.0 4.6 %collective-permute-done.31.refs_11_ = bf16[1,64,512]{2,1,0:T(8,128)(2,1)S(1)} collective-permute-done((bf16[1,64,512]{2,1,0:T(8,128)(2,1)S(1)}, bf16[1,64,512]{2,1,0:T(8,128)(2,1)S(1)}, u32[]{:S(2)}, u32[]{:S(2)}) %collective-permute-start.31) | collective-permute-done | bytes 65568 | tf_op jit(solution)/shard_map/ppermute | solution.py:433
  127.8 3.4 %collective-permute-start.34 = (bf16[2,72,512]{2,1,0:T(8,128)(2,1)S(1)}, bf16[2,72,512]{2,1,0:T(8,128)(2,1)S(1)}, u32[]{:S(2)}, u32[]{:S(2)}) collective-permute-start(bf16[2,72,512]{2,1,0:T(8,128)(2,1)S(1)} %get-tuple-element.53), channel_id=1, source_target_pairs={{0,3},{1,2},{2,1},{3,0},{4,7},{5,6},{6,5},{7,4},{8,11},{9,10},{10,... | collective-permute-start | bytes 442376 | tf_op jit(solution)/shard_map/ppermute | solution.py:433
  131.2 2.3 %collective-permute-done.32.refs_1_ = bf16[2,72,512]{2,1,0:T(8,128)(2,1)S(1)} collective-permute-done((bf16[2,72,512]{2,1,0:T(8,128)(2,1)S(1)}, bf16[2,72,512]{2,1,0:T(8,128)(2,1)S(1)}, u32[]{:S(2)}, u32[]{:S(2)}) %collective-permute-start.32) | collective-permute-done | bytes 147488 | tf_op jit(solution)/shard_map/ppermute | solution.py:433
  133.5 2.4 %collective-permute-done.34.refs_3_ = bf16[2,72,512]{2,1,0:T(8,128)(2,1)S(1)} collective-permute-done((bf16[2,72,512]{2,1,0:T(8,128)(2,1)S(1)}, bf16[2,72,512]{2,1,0:T(8,128)(2,1)S(1)}, u32[]{:S(2)}, u32[]{:S(2)}) %collective-permute-start.34) | collective-permute-done | bytes 147488 | tf_op jit(solution)/shard_map/ppermute | solution.py:433
  136.0 2.6 %collective-permute-start.35 = (bf16[72,512]{1,0:T(8,128)(2,1)S(1)}, bf16[72,512]{1,0:T(8,128)(2,1)S(1)}, u32[]{:S(2)}, u32[]{:S(2)}) collective-permute-start(bf16[72,512]{1,0:T(8,128)(2,1)S(1)} %get-tuple-element.55), channel_id=1, source_target_pairs={{0,4},{1,5},{2,6},{3,7},{4,0},{5,1},{6,2},{7,3},{8,12},{9,13},{10,... | collective-permute-start | bytes 221192 | tf_op jit(solution)/shard_map/ppermute | solution.py:433
  140.0 2.1 %collective-permute-done.35.far_ref = bf16[72,512]{1,0:T(8,128)(2,1)S(1)} collective-permute-done((bf16[72,512]{1,0:T(8,128)(2,1)S(1)}, bf16[72,512]{1,0:T(8,128)(2,1)S(1)}, u32[]{:S(2)}, u32[]{:S(2)}) %collective-permute-start.35) | collective-permute-done | bytes 73760 | tf_op jit(solution)/shard_map/ppermute | solution.py:433
  (75 shorter events, 21.8 us)
Async XLA Ops:
  1.6 14.1 %collective-permute-start = (bf16[1,256,256]{2,1,0:T(8,128)(2,1)S(1)}, bf16[1,256,256]{2,1,0:T(8,128)(2,1)S(1)}, u32[]{:S(2)}, u32[]{:S(2)}) collective-permute-start(bf16[1,256,256]{2,1,0:T(8,128)(2,1)S(1)} %get-tuple-element.68), channel_id=1, source_target_pairs={{0,4},{1,5},{2,6},{3,7},{4,0},{5,1},{6,2},{7,3},{8,12},{9,13},{10,... | collective-permute-start | bytes 393224 | tf_op jit(solution)/shard_map/ppermute | solution.py:433
  5.8 11.9 %collective-permute-start.2 = (bf16[1,256,256]{2,1,0:T(8,128)(2,1)S(1)}, bf16[1,256,256]{2,1,0:T(8,128)(2,1)S(1)}, u32[]{:S(2)}, u32[]{:S(2)}) collective-permute-start(bf16[1,256,256]{2,1,0:T(8,128)(2,1)S(1)} %get-tuple-element.67), channel_id=1, source_target_pairs={{0,4},{1,5},{2,6},{3,7},{4,0},{5,1},{6,2},{7,3},{8,12},{9,13},{10,... | collective-permute-start | bytes 393224 | tf_op jit(solution)/shard_map/ppermute | solution.py:433
  15.8 6.4 %collective-permute-start.1 = (bf16[2,256,256]{2,1,0:T(8,128)(2,1)S(1)}, bf16[2,256,256]{2,1,0:T(8,128)(2,1)S(1)}, u32[]{:S(2)}, u32[]{:S(2)}) collective-permute-start(bf16[2,256,256]{2,1,0:T(8,128)(2,1)S(1)} %pad_maximum_fusion.2), channel_id=1, source_target_pairs={{0,2},{1,3},{2,0},{3,1},{4,6},{5,7},{6,4},{7,5},{8,9},{9,8},{10,11... | collective-permute-start | bytes 786440 | tf_op jit(solution)/shard_map/ppermute | solution.py:433
  17.7 9.8 %collective-permute-start.3 = (bf16[2,256,256]{2,1,0:T(8,128)(2,1)S(1)}, bf16[2,256,256]{2,1,0:T(8,128)(2,1)S(1)}, u32[]{:S(2)}, u32[]{:S(2)}) collective-permute-start(bf16[2,256,256]{2,1,0:T(8,128)(2,1)S(1)} %pad_maximum_fusion.3), channel_id=1, source_target_pairs={{0,2},{1,3},{2,0},{3,1},{4,6},{5,7},{6,4},{7,5},{8,9},{9,8},{10,11... | collective-permute-start | bytes 786440 | tf_op jit(solution)/shard_map/ppermute | solution.py:433
  22.3 18.0 %collective-permute-start.6 = (bf16[4,256,256]{2,1,0:T(8,128)(2,1)S(1)}, bf16[4,256,256]{2,1,0:T(8,128)(2,1)S(1)}, u32[]{:S(2)}, u32[]{:S(2)}) collective-permute-start(bf16[4,256,256]{2,1,0:T(8,128)(2,1)S(1)} %pad_maximum_fusion.refs_0_.refs_8_), channel_id=1, source_target_pairs={{0,1},{1,0},{2,3},{3,2},{4,5},{5,4},{6,7},{7,6},{8,10},{9,11},{10,... | collective-permute-start | bytes 1572872 | tf_op jit(solution)/shard_map/ppermute | solution.py:433
  27.6 12.8 %collective-permute-start.7 = (bf16[4,256,256]{2,1,0:T(8,128)(2,1)S(1)}, bf16[4,256,256]{2,1,0:T(8,128)(2,1)S(1)}, u32[]{:S(2)}, u32[]{:S(2)}) collective-permute-start(bf16[4,256,256]{2,1,0:T(8,128)(2,1)S(1)} %pad_maximum_fusion.1.refs_1_.refs_9_), channel_id=1, source_target_pairs={{0,1},{1,0},{2,3},{3,2},{4,5},{5,4},{6,7},{7,6},{8,10},{9,11},{10,... | collective-permute-start | bytes 1572872 | tf_op jit(solution)/shard_map/ppermute | solution.py:433
  30.7 24.2 %collective-permute-start.4 = (bf16[4,256,256]{2,1,0:T(8,128)(2,1)S(1)}, bf16[4,256,256]{2,1,0:T(8,128)(2,1)S(1)}, u32[]{:S(2)}, u32[]{:S(2)}) collective-permute-start(bf16[4,256,256]{2,1,0:T(8,128)(2,1)S(1)} %pad_maximum_fusion.refs_0_.refs_8_), channel_id=1, source_target_pairs={{0,8},{1,9},{2,10},{3,11},{4,12},{5,13},{6,14},{7,15},{8,0},{9,1},... | collective-permute-start | bytes 1572872 | tf_op jit(solution)/shard_map/ppermute | solution.py:433
  30.7 24.2 %collective-permute-start.5 = (bf16[4,256,256]{2,1,0:T(8,128)(2,1)S(1)}, bf16[4,256,256]{2,1,0:T(8,128)(2,1)S(1)}, u32[]{:S(2)}, u32[]{:S(2)}) collective-permute-start(bf16[4,256,256]{2,1,0:T(8,128)(2,1)S(1)} %pad_maximum_fusion.1.refs_1_.refs_9_), channel_id=1, source_target_pairs={{0,8},{1,9},{2,10},{3,11},{4,12},{5,13},{6,14},{7,15},{8,0},{9,1},... | collective-permute-start | bytes 1572872 | tf_op jit(solution)/shard_map/ppermute | solution.py:433
  40.3 19.7 %collective-permute-start.8 = (bf16[4,256,256]{2,1,0:T(8,128)(2,1)S(1)}, bf16[4,256,256]{2,1,0:T(8,128)(2,1)S(1)}, u32[]{:S(2)}, u32[]{:S(2)}) collective-permute-start(bf16[4,256,256]{2,1,0:T(8,128)(2,1)S(1)} %collective-permute-done.6.refs_4_), channel_id=1, source_target_pairs={{0,8},{1,9},{2,10},{3,11},{4,12},{5,13},{6,14},{7,15},{8,0},{9,1},... | collective-permute-start | bytes 1572872 | tf_op jit(solution)/shard_map/ppermute | solution.py:433
  40.4 19.7 %collective-permute-start.9 = (bf16[4,256,256]{2,1,0:T(8,128)(2,1)S(1)}, bf16[4,256,256]{2,1,0:T(8,128)(2,1)S(1)}, u32[]{:S(2)}, u32[]{:S(2)}) collective-permute-start(bf16[4,256,256]{2,1,0:T(8,128)(2,1)S(1)} %collective-permute-done.7.refs_5_), channel_id=1, source_target_pairs={{0,8},{1,9},{2,10},{3,11},{4,12},{5,13},{6,14},{7,15},{8,0},{9,1},... | collective-permute-start | bytes 1572872 | tf_op jit(solution)/shard_map/ppermute | solution.py:433
  69.9 9.2 %collective-permute-start.14 = (bf16[8,128,256]{2,1,0:T(8,128)(2,1)S(1)}, bf16[8,128,256]{2,1,0:T(8,128)(2,1)S(1)}, u32[]{:S(2)}, u32[]{:S(2)}) collective-permute-start(bf16[8,128,256]{2,1,0:T(8,128)(2,1)S(1)} %get-tuple-element.45), channel_id=1, source_target_pairs={{0,1},{1,0},{2,3},{3,2},{4,5},{5,4},{6,7},{7,6},{8,24},{9,25},{10,... | collective-permute-start | bytes 1572872 | tf_op jit(solution)/shard_map/ppermute | solution.py:433
  70.0 14.8 %collective-permute-start.18 = (bf16[8,128,256]{2,1,0:T(8,128)(2,1)S(1)}, bf16[8,128,256]{2,1,0:T(8,128)(2,1)S(1)}, u32[]{:S(2)}, u32[]{:S(2)}) collective-permute-start(bf16[8,128,256]{2,1,0:T(8,128)(2,1)S(1)} %get-tuple-element.47), channel_id=1, source_target_pairs={{0,1},{1,0},{2,3},{3,2},{4,5},{5,4},{6,7},{7,6},{8,24},{9,25},{10,... | collective-permute-start | bytes 1572872 | tf_op jit(solution)/shard_map/ppermute | solution.py:433
  79.2 10.8 %collective-permute-start.15 = (bf16[4,128,256]{2,1,0:T(8,128)(2,1)S(1)}, bf16[4,128,256]{2,1,0:T(8,128)(2,1)S(1)}, u32[]{:S(2)}, u32[]{:S(2)}) collective-permute-start(bf16[4,128,256]{2,1,0:T(8,128)(2,1)S(1)} %add_convert_fusion.1), channel_id=1, source_target_pairs={{0,16},{1,17},{2,18},{3,19},{4,20},{5,21},{6,22},{7,23},{8,10},{9,... | collective-permute-start | bytes 786440 | tf_op jit(solution)/shard_map/ppermute | solution.py:433
  84.8 6.4 %collective-permute-start.19 = (bf16[4,128,256]{2,1,0:T(8,128)(2,1)S(1)}, bf16[4,128,256]{2,1,0:T(8,128)(2,1)S(1)}, u32[]{:S(2)}, u32[]{:S(2)}) collective-permute-start(bf16[4,128,256]{2,1,0:T(8,128)(2,1)S(1)} %add_convert_fusion), channel_id=1, source_target_pairs={{0,16},{1,17},{2,18},{3,19},{4,20},{5,21},{6,22},{7,23},{8,10},{9,... | collective-permute-start | bytes 786440 | tf_op jit(solution)/shard_map/ppermute | solution.py:433
  86.5 27.2 %collective-permute-start.25 = (bf16[1,64,512]{2,1,0:T(8,128)(2,1)S(1)}, bf16[1,64,512]{2,1,0:T(8,128)(2,1)S(1)}, u32[]{:S(2)}, u32[]{:S(2)}) collective-permute-start(bf16[1,64,512]{2,1,0:T(8,128)(2,1)S(1)} %get-tuple-element.65), channel_id=1, source_target_pairs={{0,1},{1,0},{2,3},{3,2},{4,5},{5,4},{6,7},{7,6},{8,9},{9,8},{10,11... | collective-permute-start | bytes 196616 | tf_op jit(solution)/shard_map/ppermute | solution.py:433
  87.1 27.9 %collective-permute-start.26 = (bf16[1,64,512]{2,1,0:T(8,128)(2,1)S(1)}, bf16[1,64,512]{2,1,0:T(8,128)(2,1)S(1)}, u32[]{:S(2)}, u32[]{:S(2)}) collective-permute-start(bf16[1,64,512]{2,1,0:T(8,128)(2,1)S(1)} %get-tuple-element.64), channel_id=1, source_target_pairs={{0,2},{1,3},{2,0},{3,1},{4,6},{5,7},{6,4},{7,5},{8,10},{9,11},{10,... | collective-permute-start | bytes 196616 | tf_op jit(solution)/shard_map/ppermute | solution.py:433
  87.1 27.9 %collective-permute-start.27 = (bf16[1,64,512]{2,1,0:T(8,128)(2,1)S(1)}, bf16[1,64,512]{2,1,0:T(8,128)(2,1)S(1)}, u32[]{:S(2)}, u32[]{:S(2)}) collective-permute-start(bf16[1,64,512]{2,1,0:T(8,128)(2,1)S(1)} %get-tuple-element.63), channel_id=1, source_target_pairs={{0,3},{1,2},{2,1},{3,0},{4,7},{5,6},{6,5},{7,4},{8,11},{9,10},{10,... | collective-permute-start | bytes 196616 | tf_op jit(solution)/shard_map/ppermute | solution.py:433
  90.0 25.9 %collective-permute-start.28 = (bf16[1,64,512]{2,1,0:T(8,128)(2,1)S(1)}, bf16[1,64,512]{2,1,0:T(8,128)(2,1)S(1)}, u32[]{:S(2)}, u32[]{:S(2)}) collective-permute-start(bf16[1,64,512]{2,1,0:T(8,128)(2,1)S(1)} %get-tuple-element.62), channel_id=1, source_target_pairs={{0,4},{1,5},{2,6},{3,7},{4,0},{5,1},{6,2},{7,3},{8,12},{9,13},{10,... | collective-permute-start | bytes 196616 | tf_op jit(solution)/shard_map/ppermute | solution.py:433
  91.3 5.5 %collective-permute-start.16 = (bf16[2,128,256]{2,1,0:T(8,128)(2,1)S(1)}, bf16[2,128,256]{2,1,0:T(8,128)(2,1)S(1)}, u32[]{:S(2)}, u32[]{:S(2)}) collective-permute-start(bf16[2,128,256]{2,1,0:T(8,128)(2,1)S(1)} %add_convert_fusion.3), channel_id=1, source_target_pairs={{0,2},{1,3},{2,0},{3,1},{4,6},{5,7},{6,4},{7,5},{8,9},{9,8},{10,11... | collective-permute-start | bytes 393224 | tf_op jit(solution)/shard_map/ppermute | solution.py:433
  96.7 5.0 %collective-permute-start.20 = (bf16[2,128,256]{2,1,0:T(8,128)(2,1)S(1)}, bf16[2,128,256]{2,1,0:T(8,128)(2,1)S(1)}, u32[]{:S(2)}, u32[]{:S(2)}) collective-permute-start(bf16[2,128,256]{2,1,0:T(8,128)(2,1)S(1)} %add_convert_fusion.2), channel_id=1, source_target_pairs={{0,2},{1,3},{2,0},{3,1},{4,6},{5,7},{6,4},{7,5},{8,9},{9,8},{10,11... | collective-permute-start | bytes 393224 | tf_op jit(solution)/shard_map/ppermute | solution.py:433
  101.7 6.3 %collective-permute-start.17 = (bf16[1,128,256]{2,1,0:T(8,128)(2,1)S(1)}, bf16[1,128,256]{2,1,0:T(8,128)(2,1)S(1)}, u32[]{:S(2)}, u32[]{:S(2)}) collective-permute-start(bf16[1,128,256]{2,1,0:T(8,128)(2,1)S(1)} %add_convert_fusion.7), channel_id=1, source_target_pairs={{0,4},{1,5},{2,6},{3,7},{4,0},{5,1},{6,2},{7,3},{8,12},{9,13},{10,... | collective-permute-start | bytes 196616 | tf_op jit(solution)/shard_map/ppermute | solution.py:433
  108.0 5.6 %collective-permute-start.21 = (bf16[1,128,256]{2,1,0:T(8,128)(2,1)S(1)}, bf16[1,128,256]{2,1,0:T(8,128)(2,1)S(1)}, u32[]{:S(2)}, u32[]{:S(2)}) collective-permute-start(bf16[1,128,256]{2,1,0:T(8,128)(2,1)S(1)} %add_convert_fusion.5), channel_id=1, source_target_pairs={{0,4},{1,5},{2,6},{3,7},{4,0},{5,1},{6,2},{7,3},{8,12},{9,13},{10,... | collective-permute-start | bytes 196616 | tf_op jit(solution)/shard_map/ppermute | solution.py:433
  113.6 6.1 %collective-permute-start.29 = (bf16[1,64,512]{2,1,0:T(8,128)(2,1)S(1)}, bf16[1,64,512]{2,1,0:T(8,128)(2,1)S(1)}, u32[]{:S(2)}, u32[]{:S(2)}) collective-permute-start(bf16[1,64,512]{2,1,0:T(8,128)(2,1)S(1)} %get-tuple-element.61), channel_id=1, source_target_pairs={{0,5},{1,4},{2,7},{3,6},{4,1},{5,0},{6,3},{7,2},{8,13},{9,12},{10,... | collective-permute-start | bytes 196616 | tf_op jit(solution)/shard_map/ppermute | solution.py:433
  113.7 12.9 %collective-permute-start.22 = (bf16[1,128,512]{2,1,0:T(8,128)(2,1)S(1)}, bf16[1,128,512]{2,1,0:T(8,128)(2,1)S(1)}, u32[]{:S(2)}, u32[]{:S(2)}) collective-permute-start(bf16[1,128,512]{2,1,0:T(8,128)(2,1)S(1)} %pad_maximum_fusion.4.refs_0_), channel_id=1, source_target_pairs={{0,16},{1,17},{2,18},{3,19},{4,20},{5,21},{6,22},{7,23},{8,24},{9,... | collective-permute-start | bytes 393224 | tf_op jit(solution)/shard_map/ppermute | solution.py:433
  114.9 11.7 %collective-permute-start.23 = (bf16[1,128,512]{2,1,0:T(8,128)(2,1)S(1)}, bf16[1,128,512]{2,1,0:T(8,128)(2,1)S(1)}, u32[]{:S(2)}, u32[]{:S(2)}) collective-permute-start(bf16[1,128,512]{2,1,0:T(8,128)(2,1)S(1)} %pad_maximum_fusion.4.refs_0_), channel_id=1, source_target_pairs={{0,8},{1,9},{2,10},{3,11},{4,12},{5,13},{6,14},{7,15},{8,0},{9,1},... | collective-permute-start | bytes 393224 | tf_op jit(solution)/shard_map/ppermute | solution.py:433
  114.9 11.7 %collective-permute-start.24 = (bf16[1,128,512]{2,1,0:T(8,128)(2,1)S(1)}, bf16[1,128,512]{2,1,0:T(8,128)(2,1)S(1)}, u32[]{:S(2)}, u32[]{:S(2)}) collective-permute-start(bf16[1,128,512]{2,1,0:T(8,128)(2,1)S(1)} %pad_maximum_fusion.4.refs_0_), channel_id=1, source_target_pairs={{0,24},{1,25},{2,26},{3,27},{4,28},{5,29},{6,30},{7,31},{8,16},{9,... | collective-permute-start | bytes 393224 | tf_op jit(solution)/shard_map/ppermute | solution.py:433
  115.9 6.1 %collective-permute-start.30 = (bf16[1,64,512]{2,1,0:T(8,128)(2,1)S(1)}, bf16[1,64,512]{2,1,0:T(8,128)(2,1)S(1)}, u32[]{:S(2)}, u32[]{:S(2)}) collective-permute-start(bf16[1,64,512]{2,1,0:T(8,128)(2,1)S(1)} %get-tuple-element.60), channel_id=1, source_target_pairs={{0,6},{1,7},{2,4},{3,5},{4,2},{5,3},{6,0},{7,1},{8,14},{9,15},{10,... | collective-permute-start | bytes 196616 | tf_op jit(solution)/shard_map/ppermute | solution.py:433
  119.6 7.0 %collective-permute-start.31 = (bf16[1,64,512]{2,1,0:T(8,128)(2,1)S(1)}, bf16[1,64,512]{2,1,0:T(8,128)(2,1)S(1)}, u32[]{:S(2)}, u32[]{:S(2)}) collective-permute-start(bf16[1,64,512]{2,1,0:T(8,128)(2,1)S(1)} %get-tuple-element.59), channel_id=1, source_target_pairs={{0,7},{1,6},{2,5},{3,4},{4,3},{5,2},{6,1},{7,0},{8,15},{9,14},{10,... | collective-permute-start | bytes 196616 | tf_op jit(solution)/shard_map/ppermute | solution.py:433
  127.7 5.8 %collective-permute-start.32 = (bf16[2,72,512]{2,1,0:T(8,128)(2,1)S(1)}, bf16[2,72,512]{2,1,0:T(8,128)(2,1)S(1)}, u32[]{:S(2)}, u32[]{:S(2)}) collective-permute-start(bf16[2,72,512]{2,1,0:T(8,128)(2,1)S(1)} %get-tuple-element.51), channel_id=1, source_target_pairs={{0,1},{1,0},{2,3},{3,2},{4,5},{5,4},{6,7},{7,6},{8,9},{9,8},{10,11... | collective-permute-start | bytes 442376 | tf_op jit(solution)/shard_map/ppermute | solution.py:433
  127.7 5.7 %collective-permute-start.33 = (bf16[2,72,512]{2,1,0:T(8,128)(2,1)S(1)}, bf16[2,72,512]{2,1,0:T(8,128)(2,1)S(1)}, u32[]{:S(2)}, u32[]{:S(2)}) collective-permute-start(bf16[2,72,512]{2,1,0:T(8,128)(2,1)S(1)} %get-tuple-element.52), channel_id=1, source_target_pairs={{0,2},{1,3},{2,0},{3,1},{4,6},{5,7},{6,4},{7,5},{8,10},{9,11},{10,... | collective-permute-start | bytes 442376 | tf_op jit(solution)/shard_map/ppermute | solution.py:433
  127.8 8.1 %collective-permute-start.34 = (bf16[2,72,512]{2,1,0:T(8,128)(2,1)S(1)}, bf16[2,72,512]{2,1,0:T(8,128)(2,1)S(1)}, u32[]{:S(2)}, u32[]{:S(2)}) collective-permute-start(bf16[2,72,512]{2,1,0:T(8,128)(2,1)S(1)} %get-tuple-element.53), channel_id=1, source_target_pairs={{0,3},{1,2},{2,1},{3,0},{4,7},{5,6},{6,5},{7,4},{8,11},{9,10},{10,... | collective-permute-start | bytes 442376 | tf_op jit(solution)/shard_map/ppermute | solution.py:433
  136.0 6.1 %collective-permute-start.35 = (bf16[72,512]{1,0:T(8,128)(2,1)S(1)}, bf16[72,512]{1,0:T(8,128)(2,1)S(1)}, u32[]{:S(2)}, u32[]{:S(2)}) collective-permute-start(bf16[72,512]{1,0:T(8,128)(2,1)S(1)} %get-tuple-element.55), channel_id=1, source_target_pairs={{0,4},{1,5},{2,6},{3,7},{4,0},{5,1},{6,2},{7,3},{8,12},{9,13},{10,... | collective-permute-start | bytes 221192 | tf_op jit(solution)/shard_map/ppermute | solution.py:433
  (6 other events, 151.8 us)

commit v4 on v3

--- a/solution.py
+++ b/solution.py
@@ -303,10 +303,10 @@
 
 
 def share_kernel(count, tab_ref, *refs):
-    lines, rolls, grad_ref, outs = refs[:4], refs[4 : 4 + count], refs[4 + count], refs[5 + count :]
+    lines, rolls, grad_ref, outs = refs[:3], refs[3 : 3 + count], refs[3 + count], refs[4 + count :]
     quarter, actions = lines[0].shape[1:]
-    for k, ref in enumerate(lines):
-        grad_ref[tab_ref[LINES + k]] = ref[0]
+    for k, (ref, at) in enumerate(((lines[0], 0), (lines[1], 0), (lines[2], 0), (lines[2], 1))):
+        grad_ref[tab_ref[LINES + k]] = ref[at]
     grad = grad_ref[...].reshape(4 * quarter, actions)
     wide = grad.astype(F32)
     square = jnp.sum(wide * wide, keepdims=True)
@@ -330,7 +330,7 @@
         grid_spec=pltpu.PrefetchScalarGridSpec(
             num_scalar_prefetch=1,
             grid=(1,),
-            in_specs=[full(lines[0].shape)] * 4 + [full(rolls[0].shape)] * len(rolls),
+            in_specs=[full(v.shape) for v in (*lines, *rolls)],
             out_specs=[full((4, quarter, actions))] + [full(shape)] * (len(rolls) // 2),
         ),
         out_shape=[jax.ShapeDtypeStruct((4, quarter, actions), BF16)]
@@ -484,9 +484,8 @@
             send = sum(t[n : 2 * n].astype(F32) for t in parts[c]).astype(BF16)
             parts[c] = [t[:n] for t in parts[c]] + [swap(send, tuple(r[k] for r in REDUCE))]
     own = jnp.concatenate([sum(t.astype(F32) for t in p) for p in parts], axis=2).astype(BF16)
-    lines = [own]
-    for k, mask in enumerate((Y, CORE, CORE | Y)):
-        lines.append(swap(own, mask))
+    level = swap(own, Y)
+    lines = [own, level, swap(jnp.concatenate([own, level], axis=0), CORE)]
 
     rolls = [roll_parts[0:1]]
     for m in range(1, 8):

time: 144 us -> 143 us (level)
  waiting for transfers between devices: 64.4 us -> 61.5 us
  starting transfers between devices: 32.9 us -> 34.9 us
    ppermute x36 -> x35, waiting for transfers between devices: 64.4 us -> 61.5 us  [swap(): lax.ppermute(value, AXES, [(i, i ^ masks[i // shards & 1]) for i in range...]
    ppermute x36 -> x35, starting transfers between devices: 32.9 us -> 34.9 us  [swap(): lax.ppermute(value, AXES, [(i, i ^ masks[i // shards & 1]) for i in range...]
  transfers between devices with their start and end apart: 36 -> 35, of which waited for: 17 -> 20; matrix products, arithmetic and copies ran while one was open for 1% -> 1% of each run, Pallas kernels for 25% -> 25%
where the time goes in v4:
time: 143 us
  waiting for transfers between devices  61.5 us (43%)
  Pallas kernels  42.9 us (30%)
  starting transfers between devices  34.9 us (24%)
  local copies, waits for them, and re-layouts  1.74 us (1%)
    ppermute x35, waiting for transfers between devices, swap(): lax.ppermute(value, AXES, [(i, i ^ masks[i // shards & 1]) for i in range...  61.5 us
    ppermute x35, starting transfers between devices, swap(): lax.ppermute(value, AXES, [(i, i ^ masks[i // shards & 1]) for i in range...  34.9 us
    pallas_call x3, Pallas kernels, features_call(): pl.pallas_call(functools.partial(features_kernel, start, last), in_specs=...  23.1 us
    pallas_call x4, Pallas kernels, grad_call(): pl.pallas_call(functools.partial(grad_kernel, each), grid_spec=pltpu.Pref...  8.14 us
    pallas_call x3, Pallas kernels, logits_call(): pl.pallas_call(functools.partial(logits_kernel, pieces, acc is not None,...  7.77 us
  transfers between devices with their start and end apart: 35, of which 20 were waited for; matrix products, arithmetic and copies ran while one was open for 1% of the time, Pallas kernels for 25%

profile of v4, /device:TPU:0, one launch (start us, length us, event | category | flops | bytes accessed | tf_op | source)
XLA Modules:
  0.0 142.5 jit_solution(9496069255474942865)
XLA Ops:
  1.6 4.1 %collective-permute-start = (bf16[1,256,256]{2,1,0:T(8,128)(2,1)S(1)}, bf16[1,256,256]{2,1,0:T(8,128)(2,1)S(1)}, u32[]{:S(2)}, u32[]{:S(2)}) collective-permute-start(bf16[1,256,256]{2,1,0:T(8,128)(2,1)S(1)} %get-tuple-element.68), channel_id=1, source_target_pairs={{0,4},{1,5},{2,6},{3,7},{4,0},{5,1},{6,2},{7,3},{8,12},{9,13},{10,... | collective-permute-start | bytes 393224 | tf_op jit(solution)/shard_map/ppermute | solution.py:433
  5.8 9.9 %collective-permute-done = bf16[1,256,256]{2,1,0:T(8,128)(2,1)S(1)} collective-permute-done((bf16[1,256,256]{2,1,0:T(8,128)(2,1)S(1)}, bf16[1,256,256]{2,1,0:T(8,128)(2,1)S(1)}, u32[]{:S(2)}, u32[]{:S(2)}) %collective-permute-start) | collective-permute-done | bytes 131104 | tf_op jit(solution)/shard_map/ppermute | solution.py:433
  15.8 1.8 %collective-permute-done.2 = bf16[1,256,256]{2,1,0:T(8,128)(2,1)S(1)} collective-permute-done((bf16[1,256,256]{2,1,0:T(8,128)(2,1)S(1)}, bf16[1,256,256]{2,1,0:T(8,128)(2,1)S(1)}, u32[]{:S(2)}, u32[]{:S(2)}) %collective-permute-start.2) | collective-permute-done | bytes 131104 | tf_op jit(solution)/shard_map/ppermute | solution.py:433
  18.5 3.7 %collective-permute-done.1 = bf16[2,256,256]{2,1,0:T(8,128)(2,1)S(1)} collective-permute-done((bf16[2,256,256]{2,1,0:T(8,128)(2,1)S(1)}, bf16[2,256,256]{2,1,0:T(8,128)(2,1)S(1)}, u32[]{:S(2)}, u32[]{:S(2)}) %collective-permute-start.1) | collective-permute-done | bytes 262176 | tf_op jit(solution)/shard_map/ppermute | solution.py:433
  22.3 2.2 %collective-permute-start.6 = (bf16[4,256,256]{2,1,0:T(8,128)(2,1)S(1)}, bf16[4,256,256]{2,1,0:T(8,128)(2,1)S(1)}, u32[]{:S(2)}, u32[]{:S(2)}) collective-permute-start(bf16[4,256,256]{2,1,0:T(8,128)(2,1)S(1)} %pad_maximum_fusion.refs_0_.refs_8_), channel_id=1, source_target_pairs={{0,1},{1,0},{2,3},{3,2},{4,5},{5,4},{6,7},{7,6},{8,10},{9,11},{10,... | collective-permute-start | bytes 1572872 | tf_op jit(solution)/shard_map/ppermute | solution.py:433
  24.4 3.1 %collective-permute-done.3 = bf16[2,256,256]{2,1,0:T(8,128)(2,1)S(1)} collective-permute-done((bf16[2,256,256]{2,1,0:T(8,128)(2,1)S(1)}, bf16[2,256,256]{2,1,0:T(8,128)(2,1)S(1)}, u32[]{:S(2)}, u32[]{:S(2)}) %collective-permute-start.3) | collective-permute-done | bytes 262176 | tf_op jit(solution)/shard_map/ppermute | solution.py:433
  27.6 2.4 %collective-permute-start.7 = (bf16[4,256,256]{2,1,0:T(8,128)(2,1)S(1)}, bf16[4,256,256]{2,1,0:T(8,128)(2,1)S(1)}, u32[]{:S(2)}, u32[]{:S(2)}) collective-permute-start(bf16[4,256,256]{2,1,0:T(8,128)(2,1)S(1)} %pad_maximum_fusion.1.refs_1_.refs_9_), channel_id=1, source_target_pairs={{0,1},{1,0},{2,3},{3,2},{4,5},{5,4},{6,7},{7,6},{8,10},{9,11},{10,... | collective-permute-start | bytes 1572872 | tf_op jit(solution)/shard_map/ppermute | solution.py:433
  31.2 9.1 %features.3 = (bf16[16,1024,256]{2,1,0:T(8,128)(2,1)S(1)}, bf16[32,128,1024]{2,1,0:T(8,128)(2,1)S(1)}) custom-call(s32[53]{0:T(128)S(1)} %dynamic-slice_bitcast_fusion.2.tab_ref, bf16[1024,4096]{1,0:T(8,128)(2,1)} %hidden_ref.5, bf16[64,4096]{1,0:T(8,128)(2,1)} %roll_ref.5, bf16[512,4096]{1,0:T(8,128)(2,1)} %table_ref.5, s32[1,1024]{1,0:T(1,128)} %bitcast.18, ...), custom_call_target="tpu_custom_call" | custom-call | flops 4294967296 | bytes 16777216 | tf_op jit(solution)/shard_map/features/pallas_call | solution.py:140
  40.9 6.7 %features.4 = (bf16[16,1024,256]{2,1,0:T(8,128)(2,1)S(1)}, bf16[32,128,1024]{2,1,0:T(8,128)(2,1)S(1)}) custom-call(s32[53]{0:T(128)S(1)} %dynamic-slice_bitcast_fusion.2.tab_ref, bf16[1024,4096]{1,0:T(8,128)(2,1)} %hidden_ref.5, bf16[64,4096]{1,0:T(8,128)(2,1)} %roll_ref.5, ...), custom_call_target="tpu_custom_call", output_to_operand_aliasing={{0}: (10, {}), {1}: (11, {})} | custom-call | flops 2147483648 | bytes 8388608 | tf_op jit(solution)/shard_map/features/pallas_call | solution.py:140
  47.6 7.4 %features.5 = (bf16[16,1024,256]{2,1,0:T(8,128)(2,1)S(1)}, bf16[32,128,1024]{2,1,0:T(8,128)(2,1)S(1)}, bf16[16,64,256]{2,1,0:T(8,128)(2,1)S(1)}, bf16[8,64,512]{...) custom-call(s32[53]{0:T(128)S(1)} %dynamic-slice_bitcast_fusion.2.ta, ...), custom_call_target="tpu_custom_call", output_to_operand_aliasing={{0}: (10, {}), {1}: (11, {})} | custom-call | flops 2147483648 | bytes 8388608 | tf_op jit(solution)/shard_map/features/pallas_call | solution.py:140
  55.0 3.1 %logits.3.refs_6_ = f32[1024,512]{1,0:T(8,128)S(1)} custom-call(s32[53]{0:T(128)S(1)} %dynamic-slice_bitcast_fusion.2.tab_ref, bf16[16,1024,256]{2,1,0:T(8,128)(2,1)S(1)} %get-tuple-element.36.refs_0_.refs_1_.refs_2_.refs_3_.refs_4_.refs_5_.refs_6_.refs_7_, ...), custom_call_target="tpu_custom_call" | custom-call | flops 2147483648 | bytes 4194304 | tf_op jit(solution)/shard_map/logits/pallas_call | solution.py:219
  58.0 2.0 %logits.4.refs_6_ = f32[1024,512]{1,0:T(8,128)S(1)} custom-call(s32[53]{0:T(128)S(1)} %dynamic-slice_bitcast_fusion.2.tab_ref, bf16[16,1024,256]{2,1,0:T(8,128)(2,1)S(1)} %get-tuple-element.36.refs_0_.refs_1_.refs_2_.refs_3_.refs_4_.refs_5_.refs_6_.refs_7_, ...), custom_call_target="tpu_custom_call" | custom-call | flops 1073741824 | bytes 2097152 | tf_op jit(solution)/shard_map/logits/pallas_call | solution.py:219
  60.1 2.7 %logits.5.scores_ref = bf16[1024,512]{1,0:T(8,128)(2,1)S(1)} custom-call(s32[53]{0:T(128)S(1)} %dynamic-slice_bitcast_fusion.2.tab_ref, bf16[16,1024,256]{2,1,0:T(8,128)(2,1)S(1)} %get-tuple-element.36.refs_0_.refs_1_.refs_2_.refs_3_.refs_4_.refs_5_.refs_6_.refs_7_, ...), custom_call_target="tpu_custom_call" | custom-call | flops 1073741824 | bytes 2097152 | tf_op jit(solution)/shard_map/logits/pallas_call | solution.py:219
  62.8 2.0 %grad.6 = (bf16[8,128,256]{2,1,0:T(8,128)(2,1)S(1)}, bf16[8,128,256]{2,1,0:T(8,128)(2,1)S(1)}) custom-call(s32[53]{0:T(128)S(1)} %dynamic-slice_bitcast_fusion.2.tab_ref, bf16[1024,512]{1,0:T(8,128)(2,1)S(1)} %logits.5.scores_ref, bf16[32,128,1024]{2,1,0:T(8,128)(2,1)S(1)} %get-tuple-element.39.refs_0_.refs_1_.refs_2_.refs_3_, ...), custom_call_target="tpu_custom_call" | custom-call | flops 1073741824 | bytes 2097152 | tf_op jit(solution)/shard_map/grad/pallas_call | solution.py:250
  65.3 2.0 %grad.4 = (bf16[8,128,256]{2,1,0:T(8,128)(2,1)S(1)}, bf16[8,128,256]{2,1,0:T(8,128)(2,1)S(1)}) custom-call(s32[53]{0:T(128)S(1)} %dynamic-slice_bitcast_fusion.2.tab_ref, bf16[1024,512]{1,0:T(8,128)(2,1)S(1)} %logits.5.scores_ref, bf16[32,128,1024]{2,1,0:T(8,128)(2,1)S(1)} %get-tuple-element.39.refs_0_.refs_1_.refs_2_.refs_3_, ...), custom_call_target="tpu_custom_call" | custom-call | flops 1073741824 | bytes 2097152 | tf_op jit(solution)/shard_map/grad/pallas_call | solution.py:250
  67.9 2.0 %grad.7 = (bf16[8,128,256]{2,1,0:T(8,128)(2,1)S(1)}, bf16[8,128,256]{2,1,0:T(8,128)(2,1)S(1)}) custom-call(s32[53]{0:T(128)S(1)} %dynamic-slice_bitcast_fusion.2.tab_ref, bf16[1024,512]{1,0:T(8,128)(2,1)S(1)} %logits.5.scores_ref, bf16[32,128,1024]{2,1,0:T(8,128)(2,1)S(1)} %get-tuple-element.39.refs_0_.refs_1_.refs_2_.refs_3_, ...), custom_call_target="tpu_custom_call" | custom-call | flops 1073741824 | bytes 2097152 | tf_op jit(solution)/shard_map/grad/pallas_call | solution.py:250
  70.0 2.0 %collective-permute-start.18 = (bf16[8,128,256]{2,1,0:T(8,128)(2,1)S(1)}, bf16[8,128,256]{2,1,0:T(8,128)(2,1)S(1)}, u32[]{:S(2)}, u32[]{:S(2)}) collective-permute-start(bf16[8,128,256]{2,1,0:T(8,128)(2,1)S(1)} %get-tuple-element.47), channel_id=1, source_target_pairs={{0,1},{1,0},{2,3},{3,2},{4,5},{5,4},{6,7},{7,6},{8,24},{9,25},{10,... | collective-permute-start | bytes 1572872 | tf_op jit(solution)/shard_map/ppermute | solution.py:433
  72.0 2.2 %grad.5 = (f32[8,128,256]{2,1,0:T(8,128)S(1)}, f32[8,128,256]{2,1,0:T(8,128)S(1)}) custom-call(s32[53]{0:T(128)S(1)} %dynamic-slice_bitcast_fusion.2.tab_ref, bf16[1024,512]{1,0:T(8,128)(2,1)S(1)} %logits.5.scores_ref, bf16[32,128,1024]{2,1,0:T(8,128)(2,1)S(1)} %get-tuple-element.39.refs_0_.refs_1_.refs_2_.refs_3_, ...), custom_call_target="tpu_custom_call" | custom-call | flops 1073741824 | bytes 2097152 | tf_op jit(solution)/shard_map/grad/pallas_call | solution.py:250
  74.2 4.9 %collective-permute-done.14 = bf16[8,128,256]{2,1,0:T(8,128)(2,1)S(1)} collective-permute-done((bf16[8,128,256]{2,1,0:T(8,128)(2,1)S(1)}, bf16[8,128,256]{2,1,0:T(8,128)(2,1)S(1)}, u32[]{:S(2)}, u32[]{:S(2)}) %collective-permute-start.14) | collective-permute-done | bytes 524320 | tf_op jit(solution)/shard_map/ppermute | solution.py:433
  80.8 4.0 %collective-permute-done.18 = bf16[8,128,256]{2,1,0:T(8,128)(2,1)S(1)} collective-permute-done((bf16[8,128,256]{2,1,0:T(8,128)(2,1)S(1)}, bf16[8,128,256]{2,1,0:T(8,128)(2,1)S(1)}, u32[]{:S(2)}, u32[]{:S(2)}) %collective-permute-start.18) | collective-permute-done | bytes 524320 | tf_op jit(solution)/shard_map/ppermute | solution.py:433
  86.8 4.5 %collective-permute-done.19 = bf16[4,128,256]{2,1,0:T(8,128)(2,1)S(1)} collective-permute-done((bf16[4,128,256]{2,1,0:T(8,128)(2,1)S(1)}, bf16[4,128,256]{2,1,0:T(8,128)(2,1)S(1)}, u32[]{:S(2)}, u32[]{:S(2)}) %collective-permute-start.19) | collective-permute-done | bytes 262176 | tf_op jit(solution)/shard_map/ppermute | solution.py:433
  92.4 5.3 %collective-permute-done.20 = bf16[2,128,256]{2,1,0:T(8,128)(2,1)S(1)} collective-permute-done((bf16[2,128,256]{2,1,0:T(8,128)(2,1)S(1)}, bf16[2,128,256]{2,1,0:T(8,128)(2,1)S(1)}, u32[]{:S(2)}, u32[]{:S(2)}) %collective-permute-start.20) | collective-permute-done | bytes 131104 | tf_op jit(solution)/shard_map/ppermute | solution.py:433
  97.9 5.1 %collective-permute-done.21 = bf16[1,128,256]{2,1,0:T(8,128)(2,1)S(1)} collective-permute-done((bf16[1,128,256]{2,1,0:T(8,128)(2,1)S(1)}, bf16[1,128,256]{2,1,0:T(8,128)(2,1)S(1)}, u32[]{:S(2)}, u32[]{:S(2)}) %collective-permute-start.21) | collective-permute-done | bytes 65568 | tf_op jit(solution)/shard_map/ppermute | solution.py:433
  104.6 3.5 %collective-permute-done.22.refs_1_ = bf16[1,128,512]{2,1,0:T(8,128)(2,1)S(1)} collective-permute-done((bf16[1,128,512]{2,1,0:T(8,128)(2,1)S(1)}, bf16[1,128,512]{2,1,0:T(8,128)(2,1)S(1)}, u32[]{:S(2)}, u32[]{:S(2)}) %collective-permute-start.22) | collective-permute-done | bytes 131104 | tf_op jit(solution)/shard_map/ppermute | solution.py:433
  108.4 3.4 %collective-permute-start.26 = (bf16[1,64,512]{2,1,0:T(8,128)(2,1)S(1)}, bf16[1,64,512]{2,1,0:T(8,128)(2,1)S(1)}, u32[]{:S(2)}, u32[]{:S(2)}) collective-permute-start(bf16[1,64,512]{2,1,0:T(8,128)(2,1)S(1)} %get-tuple-element.63), channel_id=1, source_target_pairs={{0,3},{1,2},{2,1},{3,0},{4,7},{5,6},{6,5},{7,4},{8,11},{9,10},{10,... | collective-permute-start | bytes 196616 | tf_op jit(solution)/shard_map/ppermute | solution.py:433
  115.6 3.8 %collective-permute-start.30 = (bf16[1,64,512]{2,1,0:T(8,128)(2,1)S(1)}, bf16[1,64,512]{2,1,0:T(8,128)(2,1)S(1)}, u32[]{:S(2)}, u32[]{:S(2)}) collective-permute-start(bf16[1,64,512]{2,1,0:T(8,128)(2,1)S(1)} %get-tuple-element.59), channel_id=1, source_target_pairs={{0,7},{1,6},{2,5},{3,4},{4,3},{5,2},{6,1},{7,0},{8,15},{9,14},{10,... | collective-permute-start | bytes 196616 | tf_op jit(solution)/shard_map/ppermute | solution.py:433
  119.5 2.3 %collective-permute-done.27.refs_7_ = bf16[1,64,512]{2,1,0:T(8,128)(2,1)S(1)} collective-permute-done((bf16[1,64,512]{2,1,0:T(8,128)(2,1)S(1)}, bf16[1,64,512]{2,1,0:T(8,128)(2,1)S(1)}, u32[]{:S(2)}, u32[]{:S(2)}) %collective-permute-start.27) | collective-permute-done | bytes 65568 | tf_op jit(solution)/shard_map/ppermute | solution.py:433
  121.8 1.6 %collective-permute-done.28.refs_8_ = bf16[1,64,512]{2,1,0:T(8,128)(2,1)S(1)} collective-permute-done((bf16[1,64,512]{2,1,0:T(8,128)(2,1)S(1)}, bf16[1,64,512]{2,1,0:T(8,128)(2,1)S(1)}, u32[]{:S(2)}, u32[]{:S(2)}) %collective-permute-start.28) | collective-permute-done | bytes 65568 | tf_op jit(solution)/shard_map/ppermute | solution.py:433
  125.8 3.3 %collective-permute-start.32 = (bf16[2,72,512]{2,1,0:T(8,128)(2,1)S(1)}, bf16[2,72,512]{2,1,0:T(8,128)(2,1)S(1)}, u32[]{:S(2)}, u32[]{:S(2)}) collective-permute-start(bf16[2,72,512]{2,1,0:T(8,128)(2,1)S(1)} %get-tuple-element.52), channel_id=1, source_target_pairs={{0,2},{1,3},{2,0},{3,1},{4,6},{5,7},{6,4},{7,5},{8,10},{9,11},{10,... | collective-permute-start | bytes 442376 | tf_op jit(solution)/shard_map/ppermute | solution.py:433
  129.8 3.9 %collective-permute-done.32.refs_2_ = bf16[2,72,512]{2,1,0:T(8,128)(2,1)S(1)} collective-permute-done((bf16[2,72,512]{2,1,0:T(8,128)(2,1)S(1)}, bf16[2,72,512]{2,1,0:T(8,128)(2,1)S(1)}, u32[]{:S(2)}, u32[]{:S(2)}) %collective-permute-start.32) | collective-permute-done | bytes 147488 | tf_op jit(solution)/shard_map/ppermute | solution.py:433
  133.8 2.0 %collective-permute-done.33.refs_3_ = bf16[2,72,512]{2,1,0:T(8,128)(2,1)S(1)} collective-permute-done((bf16[2,72,512]{2,1,0:T(8,128)(2,1)S(1)}, bf16[2,72,512]{2,1,0:T(8,128)(2,1)S(1)}, u32[]{:S(2)}, u32[]{:S(2)}) %collective-permute-start.33) | collective-permute-done | bytes 147488 | tf_op jit(solution)/shard_map/ppermute | solution.py:433
  138.8 2.5 %collective-permute-done.34.far_ref = bf16[72,512]{1,0:T(8,128)(2,1)S(1)} collective-permute-done((bf16[72,512]{1,0:T(8,128)(2,1)S(1)}, bf16[72,512]{1,0:T(8,128)(2,1)S(1)}, u32[]{:S(2)}, u32[]{:S(2)}) %collective-permute-start.34) | collective-permute-done | bytes 73760 | tf_op jit(solution)/shard_map/ppermute | solution.py:433
  (74 shorter events, 23.2 us)
Async XLA Ops:
  1.6 14.1 %collective-permute-start = (bf16[1,256,256]{2,1,0:T(8,128)(2,1)S(1)}, bf16[1,256,256]{2,1,0:T(8,128)(2,1)S(1)}, u32[]{:S(2)}, u32[]{:S(2)}) collective-permute-start(bf16[1,256,256]{2,1,0:T(8,128)(2,1)S(1)} %get-tuple-element.68), channel_id=1, source_target_pairs={{0,4},{1,5},{2,6},{3,7},{4,0},{5,1},{6,2},{7,3},{8,12},{9,13},{10,... | collective-permute-start | bytes 393224 | tf_op jit(solution)/shard_map/ppermute | solution.py:433
  5.8 11.9 %collective-permute-start.2 = (bf16[1,256,256]{2,1,0:T(8,128)(2,1)S(1)}, bf16[1,256,256]{2,1,0:T(8,128)(2,1)S(1)}, u32[]{:S(2)}, u32[]{:S(2)}) collective-permute-start(bf16[1,256,256]{2,1,0:T(8,128)(2,1)S(1)} %get-tuple-element.67), channel_id=1, source_target_pairs={{0,4},{1,5},{2,6},{3,7},{4,0},{5,1},{6,2},{7,3},{8,12},{9,13},{10,... | collective-permute-start | bytes 393224 | tf_op jit(solution)/shard_map/ppermute | solution.py:433
  15.8 6.4 %collective-permute-start.1 = (bf16[2,256,256]{2,1,0:T(8,128)(2,1)S(1)}, bf16[2,256,256]{2,1,0:T(8,128)(2,1)S(1)}, u32[]{:S(2)}, u32[]{:S(2)}) collective-permute-start(bf16[2,256,256]{2,1,0:T(8,128)(2,1)S(1)} %pad_maximum_fusion.2), channel_id=1, source_target_pairs={{0,2},{1,3},{2,0},{3,1},{4,6},{5,7},{6,4},{7,5},{8,9},{9,8},{10,11... | collective-permute-start | bytes 786440 | tf_op jit(solution)/shard_map/ppermute | solution.py:433
  17.7 9.8 %collective-permute-start.3 = (bf16[2,256,256]{2,1,0:T(8,128)(2,1)S(1)}, bf16[2,256,256]{2,1,0:T(8,128)(2,1)S(1)}, u32[]{:S(2)}, u32[]{:S(2)}) collective-permute-start(bf16[2,256,256]{2,1,0:T(8,128)(2,1)S(1)} %pad_maximum_fusion.3), channel_id=1, source_target_pairs={{0,2},{1,3},{2,0},{3,1},{4,6},{5,7},{6,4},{7,5},{8,9},{9,8},{10,11... | collective-permute-start | bytes 786440 | tf_op jit(solution)/shard_map/ppermute | solution.py:433
  22.3 18.0 %collective-permute-start.6 = (bf16[4,256,256]{2,1,0:T(8,128)(2,1)S(1)}, bf16[4,256,256]{2,1,0:T(8,128)(2,1)S(1)}, u32[]{:S(2)}, u32[]{:S(2)}) collective-permute-start(bf16[4,256,256]{2,1,0:T(8,128)(2,1)S(1)} %pad_maximum_fusion.refs_0_.refs_8_), channel_id=1, source_target_pairs={{0,1},{1,0},{2,3},{3,2},{4,5},{5,4},{6,7},{7,6},{8,10},{9,11},{10,... | collective-permute-start | bytes 1572872 | tf_op jit(solution)/shard_map/ppermute | solution.py:433
  27.6 12.8 %collective-permute-start.7 = (bf16[4,256,256]{2,1,0:T(8,128)(2,1)S(1)}, bf16[4,256,256]{2,1,0:T(8,128)(2,1)S(1)}, u32[]{:S(2)}, u32[]{:S(2)}) collective-permute-start(bf16[4,256,256]{2,1,0:T(8,128)(2,1)S(1)} %pad_maximum_fusion.1.refs_1_.refs_9_), channel_id=1, source_target_pairs={{0,1},{1,0},{2,3},{3,2},{4,5},{5,4},{6,7},{7,6},{8,10},{9,11},{10,... | collective-permute-start | bytes 1572872 | tf_op jit(solution)/shard_map/ppermute | solution.py:433
  30.7 24.2 %collective-permute-start.4 = (bf16[4,256,256]{2,1,0:T(8,128)(2,1)S(1)}, bf16[4,256,256]{2,1,0:T(8,128)(2,1)S(1)}, u32[]{:S(2)}, u32[]{:S(2)}) collective-permute-start(bf16[4,256,256]{2,1,0:T(8,128)(2,1)S(1)} %pad_maximum_fusion.refs_0_.refs_8_), channel_id=1, source_target_pairs={{0,8},{1,9},{2,10},{3,11},{4,12},{5,13},{6,14},{7,15},{8,0},{9,1},... | collective-permute-start | bytes 1572872 | tf_op jit(solution)/shard_map/ppermute | solution.py:433
  30.7 24.2 %collective-permute-start.5 = (bf16[4,256,256]{2,1,0:T(8,128)(2,1)S(1)}, bf16[4,256,256]{2,1,0:T(8,128)(2,1)S(1)}, u32[]{:S(2)}, u32[]{:S(2)}) collective-permute-start(bf16[4,256,256]{2,1,0:T(8,128)(2,1)S(1)} %pad_maximum_fusion.1.refs_1_.refs_9_), channel_id=1, source_target_pairs={{0,8},{1,9},{2,10},{3,11},{4,12},{5,13},{6,14},{7,15},{8,0},{9,1},... | collective-permute-start | bytes 1572872 | tf_op jit(solution)/shard_map/ppermute | solution.py:433
  40.3 19.7 %collective-permute-start.8 = (bf16[4,256,256]{2,1,0:T(8,128)(2,1)S(1)}, bf16[4,256,256]{2,1,0:T(8,128)(2,1)S(1)}, u32[]{:S(2)}, u32[]{:S(2)}) collective-permute-start(bf16[4,256,256]{2,1,0:T(8,128)(2,1)S(1)} %collective-permute-done.6.refs_4_), channel_id=1, source_target_pairs={{0,8},{1,9},{2,10},{3,11},{4,12},{5,13},{6,14},{7,15},{8,0},{9,1},... | collective-permute-start | bytes 1572872 | tf_op jit(solution)/shard_map/ppermute | solution.py:433
  40.4 19.7 %collective-permute-start.9 = (bf16[4,256,256]{2,1,0:T(8,128)(2,1)S(1)}, bf16[4,256,256]{2,1,0:T(8,128)(2,1)S(1)}, u32[]{:S(2)}, u32[]{:S(2)}) collective-permute-start(bf16[4,256,256]{2,1,0:T(8,128)(2,1)S(1)} %collective-permute-done.7.refs_5_), channel_id=1, source_target_pairs={{0,8},{1,9},{2,10},{3,11},{4,12},{5,13},{6,14},{7,15},{8,0},{9,1},... | collective-permute-start | bytes 1572872 | tf_op jit(solution)/shard_map/ppermute | solution.py:433
  67.3 4.7 %collective-permute-start.10 = (bf16[8,128,256]{2,1,0:T(8,128)(2,1)S(1)}, bf16[8,128,256]{2,1,0:T(8,128)(2,1)S(1)}, u32[]{:S(2)}, u32[]{:S(2)}) collective-permute-start(bf16[8,128,256]{2,1,0:T(8,128)(2,1)S(1)} %get-tuple-element.40), channel_id=1, source_target_pairs={{0,8},{1,9},{2,10},{3,11},{4,12},{5,13},{6,14},{7,15},{8,0},{9,1},... | collective-permute-start | bytes 1572872 | tf_op jit(solution)/shard_map/ppermute | solution.py:433
  69.9 9.2 %collective-permute-start.14 = (bf16[8,128,256]{2,1,0:T(8,128)(2,1)S(1)}, bf16[8,128,256]{2,1,0:T(8,128)(2,1)S(1)}, u32[]{:S(2)}, u32[]{:S(2)}) collective-permute-start(bf16[8,128,256]{2,1,0:T(8,128)(2,1)S(1)} %get-tuple-element.45), channel_id=1, source_target_pairs={{0,1},{1,0},{2,3},{3,2},{4,5},{5,4},{6,7},{7,6},{8,24},{9,25},{10,... | collective-permute-start | bytes 1572872 | tf_op jit(solution)/shard_map/ppermute | solution.py:433
  70.0 14.8 %collective-permute-start.18 = (bf16[8,128,256]{2,1,0:T(8,128)(2,1)S(1)}, bf16[8,128,256]{2,1,0:T(8,128)(2,1)S(1)}, u32[]{:S(2)}, u32[]{:S(2)}) collective-permute-start(bf16[8,128,256]{2,1,0:T(8,128)(2,1)S(1)} %get-tuple-element.47), channel_id=1, source_target_pairs={{0,1},{1,0},{2,3},{3,2},{4,5},{5,4},{6,7},{7,6},{8,24},{9,25},{10,... | collective-permute-start | bytes 1572872 | tf_op jit(solution)/shard_map/ppermute | solution.py:433
  79.2 7.5 %collective-permute-start.15 = (bf16[4,128,256]{2,1,0:T(8,128)(2,1)S(1)}, bf16[4,128,256]{2,1,0:T(8,128)(2,1)S(1)}, u32[]{:S(2)}, u32[]{:S(2)}) collective-permute-start(bf16[4,128,256]{2,1,0:T(8,128)(2,1)S(1)} %add_convert_fusion.1), channel_id=1, source_target_pairs={{0,16},{1,17},{2,18},{3,19},{4,20},{5,21},{6,22},{7,23},{8,10},{9,... | collective-permute-start | bytes 786440 | tf_op jit(solution)/shard_map/ppermute | solution.py:433
  84.8 6.4 %collective-permute-start.19 = (bf16[4,128,256]{2,1,0:T(8,128)(2,1)S(1)}, bf16[4,128,256]{2,1,0:T(8,128)(2,1)S(1)}, u32[]{:S(2)}, u32[]{:S(2)}) collective-permute-start(bf16[4,128,256]{2,1,0:T(8,128)(2,1)S(1)} %add_convert_fusion), channel_id=1, source_target_pairs={{0,16},{1,17},{2,18},{3,19},{4,20},{5,21},{6,22},{7,23},{8,10},{9,... | collective-permute-start | bytes 786440 | tf_op jit(solution)/shard_map/ppermute | solution.py:433
  86.7 5.2 %collective-permute-start.16 = (bf16[2,128,256]{2,1,0:T(8,128)(2,1)S(1)}, bf16[2,128,256]{2,1,0:T(8,128)(2,1)S(1)}, u32[]{:S(2)}, u32[]{:S(2)}) collective-permute-start(bf16[2,128,256]{2,1,0:T(8,128)(2,1)S(1)} %add_convert_fusion.3), channel_id=1, source_target_pairs={{0,2},{1,3},{2,0},{3,1},{4,6},{5,7},{6,4},{7,5},{8,9},{9,8},{10,11... | collective-permute-start | bytes 393224 | tf_op jit(solution)/shard_map/ppermute | solution.py:433
  91.3 6.4 %collective-permute-start.20 = (bf16[2,128,256]{2,1,0:T(8,128)(2,1)S(1)}, bf16[2,128,256]{2,1,0:T(8,128)(2,1)S(1)}, u32[]{:S(2)}, u32[]{:S(2)}) collective-permute-start(bf16[2,128,256]{2,1,0:T(8,128)(2,1)S(1)} %add_convert_fusion.2), channel_id=1, source_target_pairs={{0,2},{1,3},{2,0},{3,1},{4,6},{5,7},{6,4},{7,5},{8,9},{9,8},{10,11... | collective-permute-start | bytes 393224 | tf_op jit(solution)/shard_map/ppermute | solution.py:433
  92.0 5.9 %collective-permute-start.17 = (bf16[1,128,256]{2,1,0:T(8,128)(2,1)S(1)}, bf16[1,128,256]{2,1,0:T(8,128)(2,1)S(1)}, u32[]{:S(2)}, u32[]{:S(2)}) collective-permute-start(bf16[1,128,256]{2,1,0:T(8,128)(2,1)S(1)} %add_convert_fusion.7), channel_id=1, source_target_pairs={{0,4},{1,5},{2,6},{3,7},{4,0},{5,1},{6,2},{7,3},{8,12},{9,13},{10,... | collective-permute-start | bytes 196616 | tf_op jit(solution)/shard_map/ppermute | solution.py:433
  97.8 5.2 %collective-permute-start.21 = (bf16[1,128,256]{2,1,0:T(8,128)(2,1)S(1)}, bf16[1,128,256]{2,1,0:T(8,128)(2,1)S(1)}, u32[]{:S(2)}, u32[]{:S(2)}) collective-permute-start(bf16[1,128,256]{2,1,0:T(8,128)(2,1)S(1)} %add_convert_fusion.5), channel_id=1, source_target_pairs={{0,4},{1,5},{2,6},{3,7},{4,0},{5,1},{6,2},{7,3},{8,12},{9,13},{10,... | collective-permute-start | bytes 196616 | tf_op jit(solution)/shard_map/ppermute | solution.py:433
  103.1 5.0 %collective-permute-start.22 = (bf16[1,128,512]{2,1,0:T(8,128)(2,1)S(1)}, bf16[1,128,512]{2,1,0:T(8,128)(2,1)S(1)}, u32[]{:S(2)}, u32[]{:S(2)}) collective-permute-start(bf16[1,128,512]{2,1,0:T(8,128)(2,1)S(1)} %pad_maximum_fusion.5.refs_0_), channel_id=1, source_target_pairs={{0,16},{1,17},{2,18},{3,19},{4,20},{5,21},{6,22},{7,23},{8,24},{9,... | collective-permute-start | bytes 393224 | tf_op jit(solution)/shard_map/ppermute | solution.py:433
  108.1 15.3 %collective-permute-start.23 = (bf16[2,128,512]{2,1,0:T(8,128)(2,1)S(1)}, bf16[2,128,512]{2,1,0:T(8,128)(2,1)S(1)}, u32[]{:S(2)}, u32[]{:S(2)}) collective-permute-start(bf16[2,128,512]{2,1,0:T(8,128)(2,1)S(1)} %pad_maximum_fusion.4), channel_id=1, source_target_pairs={{0,8},{1,9},{2,10},{3,11},{4,12},{5,13},{6,14},{7,15},{8,0},{9,1},... | collective-permute-start | bytes 786440 | tf_op jit(solution)/shard_map/ppermute | solution.py:433
  108.3 4.6 %collective-permute-start.24 = (bf16[1,64,512]{2,1,0:T(8,128)(2,1)S(1)}, bf16[1,64,512]{2,1,0:T(8,128)(2,1)S(1)}, u32[]{:S(2)}, u32[]{:S(2)}) collective-permute-start(bf16[1,64,512]{2,1,0:T(8,128)(2,1)S(1)} %get-tuple-element.65), channel_id=1, source_target_pairs={{0,1},{1,0},{2,3},{3,2},{4,5},{5,4},{6,7},{7,6},{8,9},{9,8},{10,11... | collective-permute-start | bytes 196616 | tf_op jit(solution)/shard_map/ppermute | solution.py:433
  108.3 5.9 %collective-permute-start.25 = (bf16[1,64,512]{2,1,0:T(8,128)(2,1)S(1)}, bf16[1,64,512]{2,1,0:T(8,128)(2,1)S(1)}, u32[]{:S(2)}, u32[]{:S(2)}) collective-permute-start(bf16[1,64,512]{2,1,0:T(8,128)(2,1)S(1)} %get-tuple-element.64), channel_id=1, source_target_pairs={{0,2},{1,3},{2,0},{3,1},{4,6},{5,7},{6,4},{7,5},{8,10},{9,11},{10,... | collective-permute-start | bytes 196616 | tf_op jit(solution)/shard_map/ppermute | solution.py:433
  108.4 7.2 %collective-permute-start.26 = (bf16[1,64,512]{2,1,0:T(8,128)(2,1)S(1)}, bf16[1,64,512]{2,1,0:T(8,128)(2,1)S(1)}, u32[]{:S(2)}, u32[]{:S(2)}) collective-permute-start(bf16[1,64,512]{2,1,0:T(8,128)(2,1)S(1)} %get-tuple-element.63), channel_id=1, source_target_pairs={{0,3},{1,2},{2,1},{3,0},{4,7},{5,6},{6,5},{7,4},{8,11},{9,10},{10,... | collective-permute-start | bytes 196616 | tf_op jit(solution)/shard_map/ppermute | solution.py:433
  111.8 10.0 %collective-permute-start.27 = (bf16[1,64,512]{2,1,0:T(8,128)(2,1)S(1)}, bf16[1,64,512]{2,1,0:T(8,128)(2,1)S(1)}, u32[]{:S(2)}, u32[]{:S(2)}) collective-permute-start(bf16[1,64,512]{2,1,0:T(8,128)(2,1)S(1)} %get-tuple-element.62), channel_id=1, source_target_pairs={{0,4},{1,5},{2,6},{3,7},{4,0},{5,1},{6,2},{7,3},{8,12},{9,13},{10,... | collective-permute-start | bytes 196616 | tf_op jit(solution)/shard_map/ppermute | solution.py:433
  112.8 10.6 %collective-permute-start.28 = (bf16[1,64,512]{2,1,0:T(8,128)(2,1)S(1)}, bf16[1,64,512]{2,1,0:T(8,128)(2,1)S(1)}, u32[]{:S(2)}, u32[]{:S(2)}) collective-permute-start(bf16[1,64,512]{2,1,0:T(8,128)(2,1)S(1)} %get-tuple-element.61), channel_id=1, source_target_pairs={{0,5},{1,4},{2,7},{3,6},{4,1},{5,0},{6,3},{7,2},{8,13},{9,12},{10,... | collective-permute-start | bytes 196616 | tf_op jit(solution)/shard_map/ppermute | solution.py:433
  114.3 9.2 %collective-permute-start.29 = (bf16[1,64,512]{2,1,0:T(8,128)(2,1)S(1)}, bf16[1,64,512]{2,1,0:T(8,128)(2,1)S(1)}, u32[]{:S(2)}, u32[]{:S(2)}) collective-permute-start(bf16[1,64,512]{2,1,0:T(8,128)(2,1)S(1)} %get-tuple-element.60), channel_id=1, source_target_pairs={{0,6},{1,7},{2,4},{3,5},{4,2},{5,3},{6,0},{7,1},{8,14},{9,15},{10,... | collective-permute-start | bytes 196616 | tf_op jit(solution)/shard_map/ppermute | solution.py:433
  115.6 7.8 %collective-permute-start.30 = (bf16[1,64,512]{2,1,0:T(8,128)(2,1)S(1)}, bf16[1,64,512]{2,1,0:T(8,128)(2,1)S(1)}, u32[]{:S(2)}, u32[]{:S(2)}) collective-permute-start(bf16[1,64,512]{2,1,0:T(8,128)(2,1)S(1)} %get-tuple-element.59), channel_id=1, source_target_pairs={{0,7},{1,6},{2,5},{3,4},{4,3},{5,2},{6,1},{7,0},{8,15},{9,14},{10,... | collective-permute-start | bytes 196616 | tf_op jit(solution)/shard_map/ppermute | solution.py:433
  124.5 5.3 %collective-permute-start.31 = (bf16[2,72,512]{2,1,0:T(8,128)(2,1)S(1)}, bf16[2,72,512]{2,1,0:T(8,128)(2,1)S(1)}, u32[]{:S(2)}, u32[]{:S(2)}) collective-permute-start(bf16[2,72,512]{2,1,0:T(8,128)(2,1)S(1)} %get-tuple-element.51), channel_id=1, source_target_pairs={{0,1},{1,0},{2,3},{3,2},{4,5},{5,4},{6,7},{7,6},{8,9},{9,8},{10,11... | collective-permute-start | bytes 442376 | tf_op jit(solution)/shard_map/ppermute | solution.py:433
  125.8 8.0 %collective-permute-start.32 = (bf16[2,72,512]{2,1,0:T(8,128)(2,1)S(1)}, bf16[2,72,512]{2,1,0:T(8,128)(2,1)S(1)}, u32[]{:S(2)}, u32[]{:S(2)}) collective-permute-start(bf16[2,72,512]{2,1,0:T(8,128)(2,1)S(1)} %get-tuple-element.52), channel_id=1, source_target_pairs={{0,2},{1,3},{2,0},{3,1},{4,6},{5,7},{6,4},{7,5},{8,10},{9,11},{10,... | collective-permute-start | bytes 442376 | tf_op jit(solution)/shard_map/ppermute | solution.py:433
  129.1 6.7 %collective-permute-start.33 = (bf16[2,72,512]{2,1,0:T(8,128)(2,1)S(1)}, bf16[2,72,512]{2,1,0:T(8,128)(2,1)S(1)}, u32[]{:S(2)}, u32[]{:S(2)}) collective-permute-start(bf16[2,72,512]{2,1,0:T(8,128)(2,1)S(1)} %get-tuple-element.53), channel_id=1, source_target_pairs={{0,3},{1,2},{2,1},{3,0},{4,7},{5,6},{6,5},{7,4},{8,11},{9,10},{10,... | collective-permute-start | bytes 442376 | tf_op jit(solution)/shard_map/ppermute | solution.py:433
  135.9 5.3 %collective-permute-start.34 = (bf16[72,512]{1,0:T(8,128)(2,1)S(1)}, bf16[72,512]{1,0:T(8,128)(2,1)S(1)}, u32[]{:S(2)}, u32[]{:S(2)}) collective-permute-start(bf16[72,512]{1,0:T(8,128)(2,1)S(1)} %get-tuple-element.55), channel_id=1, source_target_pairs={{0,4},{1,5},{2,6},{3,7},{4,0},{5,1},{6,2},{7,3},{8,12},{9,13},{10,... | collective-permute-start | bytes 221192 | tf_op jit(solution)/shard_map/ppermute | solution.py:433
  (5 other events, 140.7 us)
